TPU v7x, 512 devices: a whole 4x8x8 slice. The times are simulated.
512 devices in a mesh: lat: 16 (over y, x_lo), lon: 32 (over x_hi, z, core).
Axes of the slice: x: 4 (x_hi: 2, x_lo: 2; x = x_hi * 2 + x_lo), y: 8, z: 8, core: 2. Of those that a mesh axis runs over, the one named last changes fastest.
Arguments:
- adjoint_in: bfloat16 [8, 100, 32, 4096], P(None, None, 'lat', 'lon'), may hold values from -6 to 6
- state: bfloat16 [2, 8, 100, 32, 4096], P(None, None, None, 'lat', 'lon'), may hold values from 0.29882812 to 1
- inverses: bfloat16 [3, 8, 100, 100], replicated
- courant_lon: float32 [32, 4096], P('lat', 'lon'), may hold values from 0.1 to 0.4
- courant_lat: float32 [32, 4096], P('lat', 'lon'), may hold values from 0.1 to 0.4
- emission: float32 [100, 32, 4096], P(None, 'lat', 'lon'), may hold values from 0.02 to 0.2
- region_id: int32 [32, 4096], P('lat', 'lon'), may hold values from 0 to 511, as said below
- stiffness: int32 [8, 32, 4096], P(None, 'lat', 'lon'), may hold values from 1 to 3
Outputs:
- adjoint_out: bfloat16 [8, 100, 32, 4096], P(None, None, 'lat', 'lon')
- emission_grad: float32 [512, 100], P(('lat', 'lon'))
Inputs may be any that keep to these rules, and one draw needn't show every extreme that they name: `region_id`: constant on aligned tiles of 2 x 2 columns.
All inputs are finite; a program needn't handle non-finite values.
Results may differ from a plain program's by a relative error of at most 0.0048.
Values sent between devices are 32-bit elements; how exact they have to be, the bound alone decides.
No kernel may reach another device: no remote copies, remote signals or barrier semaphores. Data moves between devices by JAX's collectives and lax.ppermute only.
A program may use at most 64 MiB of HBM per device.

v0:
```python
import jax
import jax.numpy as jnp
from jax import lax
from jax.sharding import PartitionSpec as P

STEPS = 3
NWIN = 2
ADV = 2
REG_DEV = 1


def shifted(block, axis, distance):
    devices = range(lax.axis_size(axis))
    route = [((i - distance) % len(devices), i) for i in devices]
    return lax.ppermute(block, axis, route)


def from_behind(block, axis, distance):
    devices = range(lax.axis_size(axis))
    route = [(i - distance, i) for i in devices if i - distance in devices]
    return lax.ppermute(block, axis, route)


def advect(lam, clon, clat, east, south):
    right = jnp.concatenate([lam[:, :, :, 1:], east], axis=3)
    down = jnp.concatenate([lam[:, :, 1:, :], south], axis=2)
    return (1.0 - clon - clat) * lam + clat * down + clon * right


def transport_each(lam, courant_lon, courant_lat):
    for k in range(ADV):
        east = shifted(lam[:, :, :, :1], "lon", -1)
        south = from_behind(lam[:, :, :1, :], "lat", -1)
        lam = advect(lam, courant_lon, courant_lat, east, south)
    return lam


def transposed(mats, right_side):
    return lax.dot_general(
        mats, right_side, (((1,), (1,)), ((0,), (0,))), preferred_element_type=jnp.float32
    )


def chemistry(lam, factor, inverses, stiffness):
    levels, spec, rows, cols = lam.shape
    flat = lam.reshape(levels, spec, rows * cols)
    yfac = factor.reshape(levels, spec, rows * cols)
    live = stiffness.reshape(levels, 1, rows * cols)
    for s in reversed(range(STEPS)):
        mats = inverses[s]

        def advance(values, mats=mats, s=s):
            first = transposed(mats, values.astype(jnp.bfloat16))
            second = transposed(mats, (first * yfac).astype(jnp.bfloat16))
            third = transposed(mats, (second * yfac).astype(jnp.bfloat16))
            cand = 0.4 * values + 0.3 * first + 0.2 * second + 0.1 * third
            return jnp.where(live > s, cand, values)

        flat = lax.cond(jnp.any(stiffness > s), advance, lambda values: values, flat)
    return flat.reshape(levels, spec, rows, cols)


def per_device(
    adjoint_in, state, inverses, courant_lon, courant_lat, emission, region_id, stiffness
):
    lam = adjoint_in.astype(jnp.float32)
    surface = jnp.zeros(emission.shape, jnp.float32)
    for window in reversed(range(NWIN)):
        lam = transport_each(lam, courant_lon, courant_lat)
        lam = chemistry(lam, state[window], inverses, stiffness)
        surface = surface + lam[0]
    spec = emission.shape[0]
    regions = REG_DEV * lax.axis_size("lat") * lax.axis_size("lon")
    contrib = (surface * emission).reshape(spec, -1)
    labels = lax.broadcasted_iota(jnp.int32, (regions, contrib.shape[1]), 0)
    onehot = (region_id.reshape(1, -1) == labels).astype(jnp.float32)
    partial_value = lax.dot_general(
        onehot,
        contrib,
        (((1,), (1,)), ((), ())),
        precision=lax.Precision.HIGHEST,
        preferred_element_type=jnp.float32,
    )
    total = lax.psum(partial_value, ("lat", "lon"))
    share = REG_DEV
    grad = lax.dynamic_slice_in_dim(total, lax.axis_index(("lat", "lon")) * share, share, 0)
    return (lam.astype(jnp.bfloat16), grad)


def solution(mesh):
    in_specs = (
        P(None, None, "lat", "lon"),
        P(None, None, None, "lat", "lon"),
        P(),
        P("lat", "lon"),
        P("lat", "lon"),
        P(None, "lat", "lon"),
        P("lat", "lon"),
        P(None, "lat", "lon"),
    )
    out_specs = (P(None, None, "lat", "lon"), P(("lat", "lon"), None))
    return jax.shard_map(
        per_device, mesh=mesh, in_specs=in_specs, out_specs=out_specs, check_vma=False
    )
```

profile of v0, /device:TPU:1, one launch (start us, length us, event | category | flops | bytes accessed | tf_op | source)
XLA Modules:
  0.0 368.7 jit_solution(13266423001030300704)
XLA Ops:
  7.2 1.1 copy_convert_fusion.5
  9.1 1.3 collective-permute-start
  10.8 8.8 %collective-permute-start.1 = (f32[8,100,2,1]{1,0,3,2:T(8,128)S(1)}, f32[8,100,2,1]{1,0,3,2:T(8,128)S(1)}, u32[]{:S(2)}, u32[]{:S(2)}) collective-permute-start(f32[8,100,2,1]{1,0,3,2:T(8,128)S(1)} %copy.34), channel_id=1, source_target_pairs={{1,0},{2,1},{3,2},{4,3},{5,4},{6,5},{7,6},{8,7},{9,8},{10,9},{11,1... | collective-permute-start | bytes 19208 | tf_op jit(solution)/shard_map/ppermute | solution.py:15
  20.9 1.3 fusion.65
  22.2 0.9 fusion.82
  23.2 1.4 collective-permute-start.2
  24.6 1.3 fusion.79
  26.3 8.0 %collective-permute-start.3 = (f32[8,100,2,1]{1,0,3,2:T(8,128)S(1)}, f32[8,100,2,1]{1,0,3,2:T(8,128)}, u32[]{:S(2)}, u32[]{:S(2)}) collective-permute-start(f32[8,100,2,1]{1,0,3,2:T(8,128)S(1)} %copy.36), channel_id=1, source_target_pairs={{1,0},{2,1},{3,2},{4,3},{5,4},{6,5},{7,6},{8,7},{9,8},{10,9},{11,1... | collective-permute-start | bytes 19208 | tf_op jit(solution)/shard_map/ppermute | solution.py:15
  38.1 1.1 copy.37
  39.9 1.4 fusion.68
  41.6 1.3 conditional.7
  43.0 1.3 conditional.8
  45.4 1.3 collective-permute-start.4
  46.7 1.0 copy.49
  47.6 9.1 %collective-permute-start.5 = (f32[8,100,2,1]{1,0,3,2:T(8,128)}, f32[8,100,2,1]{1,0,3,2:T(8,128)}, u32[]{:S(2)}, u32[]{:S(2)}) collective-permute-start(f32[8,100,2,1]{1,0,3,2:T(8,128)} %copy.49), channel_id=1, source_target_pairs={{1,0},{2,1},{3,2},{4,3},{5,4},{6,5},{7,6},{8,7},{9,8},{10,9},{11,1... | collective-permute-start | bytes 19208 | tf_op jit(solution)/shard_map/ppermute | solution.py:15
  57.0 0.9 collective-permute-done.5
  57.9 2.0 copy.50
  60.5 1.7 multiply_add_fusion
  62.2 1.0 fusion.80
  63.2 1.3 collective-permute-start.6
  64.8 6.5 %collective-permute-start.7 = (f32[8,100,2,1]{1,0,3,2:T(8,128)S(1)}, f32[8,100,2,1]{1,0,3,2:T(8,128)S(1)}, u32[]{:S(2)}, u32[]{:S(2)}) collective-permute-start(f32[8,100,2,1]{1,0,3,2:T(8,128)S(1)} %copy.51), channel_id=1, source_target_pairs={{1,0},{2,1},{3,2},{4,3},{5,4},{6,5},{7,6},{8,7},{9,8},{10,9},{11,1... | collective-permute-start | bytes 19208 | tf_op jit(solution)/shard_map/ppermute | solution.py:15
  71.3 1.1 copy.137
  72.4 1.2 slice.111
  73.6 1.3 copy.52
  75.5 2.6 fusion.71
  78.6 1.3 conditional.10
  80.0 1.3 conditional.11
  81.4 0.8 copy-done.5
  83.1 1.1 fusion.76
  84.4 1.1 copy.60
  85.5 275.2 %all-reduce.2.cloned.1.call-done = f32[512,100]{1,0:T(8,128)} async-done(((f32[512,100]{1,0:T(8,128)}), f32[512,100]{1,0:T(8,128)}) %all-reduce.2.cloned.1.call-update) | async-done | bytes 204816 | tf_op jit(solution)/shard_map/psum | solution.py:84
  360.7 1.2 constant_dynamic-slice_fusion
  (80 shorter events, 16.1 us)
Async XLA Ops:
  7.2 353.5 %all-reduce.2.cloned.1.call-start = ((), (), s32[]{:S(2)}) async-start(), calls=%async_computation | async-start | bytes 524288 | tf_op jit(solution)/shard_map/psum | solution.py:84
  9.1 11.7 %collective-permute-start = (f32[8,100,1,128]{3,0,2,1:T(8,128)}, f32[8,100,1,128]{3,0,2,1:T(8,128)}, u32[]{:S(2)}, u32[]{:S(2)}) collective-permute-start(f32[8,100,1,128]{3,0,2,1:T(8,128)} %get-tuple-element.166), channel_id=1, source_target_pairs={{32,0},{64,32},{96,64},{128,96},{160,128},{192,160},{224,192},{256... | collective-permute-start | bytes 1228808 | tf_op jit(solution)/shard_map/ppermute | solution.py:21
  10.4 9.2 %copy-start.7 = (f32[2,128]{1,0:T(2,128)S(1)}, f32[2,128]{1,0:T(2,128)}, u32[]{:S(2)}) copy-start(f32[2,128]{1,0:T(2,128)} %param.23) | copy-start | bytes 3076
  10.4 9.2 %copy-start.8 = (f32[2,128]{1,0:T(2,128)S(1)}, f32[2,128]{1,0:T(2,128)}, u32[]{:S(2)}) copy-start(f32[2,128]{1,0:T(2,128)} %param.24) | copy-start | bytes 3076
  10.8 9.6 %collective-permute-start.1 = (f32[8,100,2,1]{1,0,3,2:T(8,128)S(1)}, f32[8,100,2,1]{1,0,3,2:T(8,128)S(1)}, u32[]{:S(2)}, u32[]{:S(2)}) collective-permute-start(f32[8,100,2,1]{1,0,3,2:T(8,128)S(1)} %copy.34), channel_id=1, source_target_pairs={{1,0},{2,1},{3,2},{4,3},{5,4},{6,5},{7,6},{8,7},{9,8},{10,9},{11,1... | collective-permute-start | bytes 19208 | tf_op jit(solution)/shard_map/ppermute | solution.py:15
  19.6 1.2 copy-start.9
  19.9 1.0 copy-start.2
  22.2 2.4 copy-start.4
  23.2 1.5 copy-start.3
  23.2 16.1 %collective-permute-start.2 = (f32[8,100,1,128]{3,0,2,1:T(8,128)}, f32[8,100,1,128]{3,0,2,1:T(8,128)}, u32[]{:S(2)}, u32[]{:S(2)}) collective-permute-start(f32[8,100,1,128]{3,0,2,1:T(8,128)} %get-tuple-element.164), channel_id=1, source_target_pairs={{32,0},{64,32},{96,64},{128,96},{160,128},{192,160},{224,192},{256... | collective-permute-start | bytes 1228808 | tf_op jit(solution)/shard_map/ppermute | solution.py:21
  26.0 8.4 %copy-start.6 = (s32[8,2,128]{2,1,0:T(2,128)S(1)}, s32[8,2,128]{2,1,0:T(2,128)}, u32[]{:S(2)}) copy-start(s32[8,2,128]{2,1,0:T(2,128)} %param.27) | copy-start | bytes 24580
  26.3 11.7 %collective-permute-start.3 = (f32[8,100,2,1]{1,0,3,2:T(8,128)S(1)}, f32[8,100,2,1]{1,0,3,2:T(8,128)}, u32[]{:S(2)}, u32[]{:S(2)}) collective-permute-start(f32[8,100,2,1]{1,0,3,2:T(8,128)S(1)} %copy.36), channel_id=1, source_target_pairs={{1,0},{2,1},{3,2},{4,3},{5,4},{6,5},{7,6},{8,7},{9,8},{10,9},{11,1... | collective-permute-start | bytes 19208 | tf_op jit(solution)/shard_map/ppermute | solution.py:15
  39.2 0.7 copy-start.10
  45.4 14.5 %collective-permute-start.4 = (f32[8,100,1,128]{3,0,2,1:T(8,128)}, f32[8,100,1,128]{3,0,2,1:T(8,128)}, u32[]{:S(2)}, u32[]{:S(2)}) collective-permute-start(f32[8,100,1,128]{3,0,2,1:T(8,128)} %get-tuple-element.162), channel_id=1, source_target_pairs={{32,0},{64,32},{96,64},{128,96},{160,128},{192,160},{224,192},{256... | collective-permute-start | bytes 1228808 | tf_op jit(solution)/shard_map/ppermute | solution.py:21
  47.6 10.2 %collective-permute-start.5 = (f32[8,100,2,1]{1,0,3,2:T(8,128)}, f32[8,100,2,1]{1,0,3,2:T(8,128)}, u32[]{:S(2)}, u32[]{:S(2)}) collective-permute-start(f32[8,100,2,1]{1,0,3,2:T(8,128)} %copy.49), channel_id=1, source_target_pairs={{1,0},{2,1},{3,2},{4,3},{5,4},{6,5},{7,6},{8,7},{9,8},{10,9},{11,1... | collective-permute-start | bytes 19208 | tf_op jit(solution)/shard_map/ppermute | solution.py:15
  57.0 5.2 %copy-start = (f32[8,100,2,127]{3,0,2,1:T(8,128)}, f32[8,100,2,127]{3,0,2,1:T(8,128)S(1)}, u32[]{:S(2)}) copy-start(f32[8,100,2,127]{3,0,2,1:T(8,128)S(1)} %slice.107) | copy-start | bytes 2438404
  59.9 0.7 copy-start.11
  63.2 11.7 %collective-permute-start.6 = (f32[8,100,1,128]{3,0,2,1:T(8,128)}, f32[8,100,1,128]{3,0,2,1:T(8,128)}, u32[]{:S(2)}, u32[]{:S(2)}) collective-permute-start(f32[8,100,1,128]{3,0,2,1:T(8,128)} %get-tuple-element.160), channel_id=1, source_target_pairs={{32,0},{64,32},{96,64},{128,96},{160,128},{192,160},{224,192},{256... | collective-permute-start | bytes 1228808 | tf_op jit(solution)/shard_map/ppermute | solution.py:21
  64.8 8.7 %collective-permute-start.7 = (f32[8,100,2,1]{1,0,3,2:T(8,128)S(1)}, f32[8,100,2,1]{1,0,3,2:T(8,128)S(1)}, u32[]{:S(2)}, u32[]{:S(2)}) collective-permute-start(f32[8,100,2,1]{1,0,3,2:T(8,128)S(1)} %copy.51), channel_id=1, source_target_pairs={{1,0},{2,1},{3,2},{4,3},{5,4},{6,5},{7,6},{8,7},{9,8},{10,9},{11,1... | collective-permute-start | bytes 19208 | tf_op jit(solution)/shard_map/ppermute | solution.py:15
  73.6 1.3 copy-start.1
  74.9 0.7 copy-start.12
  81.4 0.9 copy-start.5
  82.4 0.7 copy-start.13
Sparse Core Ops, SparseCore 0:
  84.3 276.3 all-reduce.1
where the time goes:
time: 370 us; the launch traced here: 369 us
  waiting for transfers between devices  277 us (75%)
  starting transfers between devices  37.6 us (10%)
  local copies, waits for them, and re-layouts  22.6 us (6%)
  between operations  16.3 us (4%)
  other arithmetic  8.95 us (2%)
  matrix products  6.27 us (2%)
    psum x1, waiting for transfers between devices, per_device(): total = lax.psum(partial_value, ('lat', 'lon'))  275 us
    ppermute x4, starting transfers between devices, shifted(): return lax.ppermute(block, axis, route)  32.3 us
  transfers between devices with their start and end apart: 9, of which 3 were waited for; matrix products, arithmetic and copies ran while one was open for 4% of the time, Pallas kernels for 0%

commit v1 on v0

v1 whole, which is shorter than its diff:
```python
import functools
import jax
import jax.numpy as jnp
from jax import lax
from jax.experimental import pallas as pl
from jax.experimental.pallas import tpu as pltpu
from jax.sharding import PartitionSpec as P

STEPS = 3
EXTRA = 8
F32 = jnp.float32
BF16 = jnp.bfloat16
ANY = pl.BlockSpec(memory_space=pl.ANY)
VMEM = pl.BlockSpec(memory_space=pltpu.VMEM)


def lanes(shape):
    return lax.broadcasted_iota(jnp.int32, shape, len(shape) - 1)


def place(acc, block, slot):
    moved = pltpu.roll(block, 2 * slot, 1) if slot else block
    at = lanes(block.shape)
    return jnp.where((at >= 2 * slot) & (at < 2 * slot + 2), moved, acc)


def pack_kernel(adj, clon, clat, first, rest, west, *, rows):
    levels = adj.shape[0]
    acc = jnp.zeros((rows, adj.shape[2]), F32)
    for lev in range(levels):
        block = adj[lev].astype(F32)
        if lev == 0:
            first[0:rows] = block
        else:
            rest[(lev - 1) * rows : lev * rows] = block
        acc = place(acc, block, lev)
    west[0:rows] = acc
    for out in (first, west):
        out[rows : rows + 2] = clon[...]
        out[rows + 2 : rows + 4] = clat[...]
        out[rows + 4 : rows + 8] = jnp.zeros((4, clon.shape[1]), F32)


def pull(block, lane_from, lane_to, width):
    shift = (lane_to - lane_from) % width
    return pltpu.roll(block, shift, 1) if shift else block


def advected(own, north, west, diag, lev, slot, cour):
    rows, width = cour["rows"], own.shape[1]
    spec = rows // 2
    last = lanes((spec, width)) == width - 1
    base = lev * rows

    def pick(ref, start, parity):
        return ref[pl.ds(start + parity, spec, stride=2), :]

    r0, r1 = pick(own, base, 0), pick(own, base, 1)
    r2, r3 = pick(north, base, 0), pick(north, base, 1)
    w0, w1, d = pick(west, 0, 0), pick(west, 0, 1), pick(diag, 0, 0)
    end = width - 1
    e0, e1 = pull(w0, 2 * slot, end, width), pull(w1, 2 * slot, end, width)
    g0, g1 = pull(w0, 2 * slot + 1, end, width), pull(w1, 2 * slot + 1, end, width)
    d0 = pull(d, 2 * slot, end, width)

    def right(block, edge):
        return jnp.where(last, edge, pltpu.roll(block, width - 1, 1))

    def step(mid, down, east, at):
        return cour["keep"][at] * mid + cour["lat"][at] * down + cour["lon"][at] * east

    a0 = step(r0, r1, right(r0, e0), 0)
    a1 = step(r1, r2, right(r1, e1), 1)
    a2 = step(r2, r3, right(r2, d0), 2)
    f0 = step(e0, e1, g0, 3)
    f1 = step(e1, d0, g1, 4)
    b0 = step(a0, a1, right(a0, f0), 0)
    b1 = step(a1, a2, right(a1, f1), 1)
    return b0, b1


def courant(clon, clat, north_c, west_c, rows):
    width = clon.shape[1]

    def edge(row):
        return pltpu.roll(jnp.broadcast_to(row, (8, width)), width - 1, 1)[0:1]

    lon = [clon[0:1], clon[1:2], north_c[rows : rows + 1]]
    lat = [clat[0:1], clat[1:2], north_c[rows + 2 : rows + 3]]
    lon += [edge(west_c[rows : rows + 1]), edge(west_c[rows + 1 : rows + 2])]
    lat += [edge(west_c[rows + 2 : rows + 3]), edge(west_c[rows + 3 : rows + 4])]
    keep = [1.0 - a - b for a, b in zip(lon, lat)]
    return {"rows": rows, "lon": lon, "lat": lat, "keep": keep}


def split3(value):
    high = value.astype(BF16)
    left = value - high.astype(F32)
    mid = left.astype(BF16)
    low = (left - mid.astype(F32)).astype(BF16)
    return high, mid, low


def window_kernel(
    *refs, window, first_level, count, rows, slots, last, grad, regions
):
    refs = list(refs)
    own, north, west, diag, clon, clat, north_c, west_c, stiff, state_h, mats_h = refs[:11]
    refs = refs[11:]
    if grad:
        before, emission, region = refs[:3]
        refs = refs[3:]
    if last and not grad:
        refs = refs[1:]
    if last:
        out_h = refs.pop(0)
        if grad:
            partial = refs.pop(0)
    else:
        lam_out, west_out = refs[:2]
        refs = refs[2:]
    x_s, y_s, flat_s, state_s, mats_s, sems = refs[:6]
    refs = refs[6:]
    spec, width = rows // 2, clon.shape[1]
    get_state = pltpu.make_async_copy(
        state_h.at[window, pl.ds(first_level, count)], state_s, sems.at[0]
    )
    get_mats = pltpu.make_async_copy(
        mats_h.at[:, pl.ds(first_level, count)], mats_s, sems.at[1]
    )
    get_state.start()
    get_mats.start()
    cour = courant(clon, clat, north_c, west_c, rows)
    for lev in range(count):
        b0, b1 = advected(own, north, west, diag, lev, slots[lev], cour)
        x_s[lev, :, 0:width] = b0
        x_s[lev, :, width : 2 * width] = b1
    get_state.wait()
    for lev in range(count):
        flat_s[lev] = state_s[lev].astype(F32)
        y_s[lev, :, 0:width] = flat_s[lev, pl.ds(0, spec, stride=2), :]
        y_s[lev, :, width : 2 * width] = flat_s[lev, pl.ds(1, spec, stride=2), :]
    get_mats.wait()
    live = []
    for lev in range(count):
        both = stiff[first_level + lev]
        live.append(jnp.concatenate([both[0:1], both[1:2]], axis=1))

    def stage(i, carry):
        s = STEPS - 1 - i
        rights = [x_s[lev].astype(BF16) for lev in range(count)]
        cands = [0.4 * x_s[lev] for lev in range(count)]
        for k, share in enumerate((0.3, 0.2, 0.1)):
            prods = [
                jnp.dot(mats_s[s, lev], rights[lev], preferred_element_type=F32)
                for lev in range(count)
            ]
            cands = [cands[lev] + share * prods[lev] for lev in range(count)]
            if k < 2:
                rights = [(prods[lev] * y_s[lev]).astype(BF16) for lev in range(count)]
        for lev in range(count):
            x_s[lev] = jnp.where(live[lev] > s, cands[lev], x_s[lev])
        return carry

    lax.fori_loop(0, STEPS, stage, 0)
    acc = [jnp.zeros((spec, width), F32)] * 2
    for lev in range(count):
        for r in range(2):
            half = x_s[lev, :, r * width : (r + 1) * width]
            if last:
                flat_s[lev, pl.ds(r, spec, stride=2), :] = half
            else:
                lam_out[pl.ds(lev * rows + r, spec, stride=2), :] = half
                acc[r] = place(acc[r], half, lev)
    if not last:
        for r in range(2):
            west_out[pl.ds(r, spec, stride=2), :] = acc[r]
        return
    out_s = refs.pop(0)
    for lev in range(count):
        out_s[lev] = flat_s[lev].astype(BF16)
    put = pltpu.make_async_copy(out_s, out_h.at[pl.ds(first_level, count)], sems.at[2])
    put.start()
    if grad:
        ids = jnp.concatenate([region[0:1], region[1:2]], axis=1)
        labels = lax.broadcasted_iota(jnp.int32, (regions, 2 * width), 0)
        onehot = jnp.where(labels == ids, 1.0, 0.0).astype(BF16)
        total = []
        for r in range(2):
            now = flat_s[0, pl.ds(r, spec, stride=2), :]
            then = before[pl.ds(r, spec, stride=2), :]
            total.append((now + then) * emission[pl.ds(r, spec, stride=2), :])
        contrib = jnp.concatenate(total, axis=1)
        contrib = jnp.concatenate([contrib, jnp.zeros((width - spec, 2 * width), F32)], axis=0)
        result = jnp.zeros((regions, width), F32)
        for piece in split3(contrib):
            result = result + lax.dot_general(
                onehot, piece, (((1,), (1,)), ((), ())), preferred_element_type=F32
            )
        partial[...] = result
    put.wait()


def run_window(
    own, north, west, diag, shared, window, first_level, count, slots, last, extra=None, prior=None
):
    clon, clat, north_c, west_c, stiff, state, mats = shared
    rows, width = state.shape[2], state.shape[3]
    spec = rows // 2
    grad = extra is not None
    regions = 0
    args = [own, north, west, diag, clon, clat, north_c, west_c, stiff, state, mats]
    specs = [VMEM] * 9 + [ANY] * 2
    aliases = {}
    if grad:
        before, emission, region, regions = extra
        args += [before, emission, region]
        specs += [VMEM] * 3
    if last:
        levels = state.shape[1]
        if not grad:
            aliases = {len(args): 0}
            args.append(prior)
            specs.append(ANY)
        out_shape = [jax.ShapeDtypeStruct((levels, rows, width), BF16)]
        out_specs = [ANY]
        if grad:
            out_shape.append(jax.ShapeDtypeStruct((regions, width), F32))
            out_specs.append(VMEM)
    else:
        out_shape = [
            jax.ShapeDtypeStruct((count * rows, width), F32),
            jax.ShapeDtypeStruct((rows, width), F32),
        ]
        out_specs = [VMEM] * 2
    scratch = [
        pltpu.VMEM((count, spec, 2 * width), F32),
        pltpu.VMEM((count, spec, 2 * width), F32),
        pltpu.VMEM((count, rows, width), F32),
        pltpu.VMEM((count, rows, width), BF16),
        pltpu.VMEM((STEPS, count, spec, spec), BF16),
        pltpu.SemaphoreType.DMA((3,)),
    ]
    if last:
        scratch.append(pltpu.VMEM((count, rows, width), BF16))
    body = functools.partial(
        window_kernel,
        window=window,
        first_level=first_level,
        count=count,
        rows=rows,
        slots=slots,
        last=last,
        grad=grad,
        regions=regions,
    )
    return pl.pallas_call(
        body,
        out_shape=out_shape,
        in_specs=specs,
        out_specs=out_specs,
        scratch_shapes=scratch,
        input_output_aliases=aliases,
        name=f"window{window}_from{first_level}",
        compiler_params=pltpu.CompilerParams(vmem_limit_bytes=32 * 2**20),
    )(*args)


def to_north(block):
    bands = lax.axis_size("lat")
    return lax.ppermute(block, "lat", [(i + 1, i) for i in range(bands - 1)])


def to_west(block):
    blocks = lax.axis_size("lon")
    return lax.ppermute(block, "lon", [((j + 1) % blocks, j) for j in range(blocks)])


def to_northwest(block):
    bands, blocks = lax.axis_size("lat"), lax.axis_size("lon")
    route = [
        ((i + 1) * blocks + (j + 1) % blocks, i * blocks + j)
        for i in range(bands - 1)
        for j in range(blocks)
    ]
    return lax.ppermute(block, ("lat", "lon"), route)


def per_device(
    adjoint_in, state, inverses, courant_lon, courant_lat, emission, region_id, stiffness
):
    windows, levels, spec, lat_rows, width = state.shape
    rows = spec * lat_rows
    regions = lax.axis_size("lat") * lax.axis_size("lon")
    adj = adjoint_in.reshape(levels, rows, width)
    flat_state = state.reshape(windows, levels, rows, width)
    flat_em = emission.reshape(rows, width)
    mats = jnp.swapaxes(inverses, 2, 3)
    low1, rest1, west1 = pl.pallas_call(
        functools.partial(pack_kernel, rows=rows),
        out_shape=[
            jax.ShapeDtypeStruct((rows + EXTRA, width), F32),
            jax.ShapeDtypeStruct(((levels - 1) * rows, width), F32),
            jax.ShapeDtypeStruct((rows + EXTRA, width), F32),
        ],
        in_specs=[VMEM] * 3,
        out_specs=[VMEM] * 3,
        name="pack",
    )(adj, courant_lon, courant_lat)
    low1_n = to_north(low1)
    west1_w = to_west(west1)
    west1_d = to_northwest(west1)
    rest1_n = to_north(rest1)
    shared = (courant_lon, courant_lat, low1_n, west1_w, stiffness, flat_state, mats)
    low0, low0_p = run_window(
        low1, low1_n, west1_w, west1_d, shared, 1, 0, 1, [0], False
    )
    low_extra = (low0, flat_em, region_id, regions)
    out, partial = run_window(
        low0, to_north(low0), to_west(low0_p), to_northwest(low0_p),
        shared, 0, 0, 1, [0], True, extra=low_extra,
    )
    rest1_n, partial = lax.optimization_barrier((rest1_n, partial))
    spread = lax.all_to_all(partial, ("lat", "lon"), 0, 0, tiled=True)
    rest0, rest0_p = run_window(
        rest1, rest1_n, west1_w, west1_d, shared, 1, 1, levels - 1, list(range(1, levels)), False
    )
    out = run_window(
        rest0, to_north(rest0), to_west(rest0_p), to_northwest(rest0_p),
        shared, 0, 1, levels - 1, list(range(levels - 1)), True, prior=out,
    )[0]
    grad = jnp.sum(spread, axis=0, keepdims=True)[:, :spec]
    return out.reshape(levels, spec, lat_rows, width), grad


def solution(mesh):
    in_specs = (
        P(None, None, "lat", "lon"),
        P(None, None, None, "lat", "lon"),
        P(),
        P("lat", "lon"),
        P("lat", "lon"),
        P(None, "lat", "lon"),
        P("lat", "lon"),
        P(None, "lat", "lon"),
    )
    out_specs = (P(None, None, "lat", "lon"), P(("lat", "lon"), None))
    return jax.shard_map(
        per_device, mesh=mesh, in_specs=in_specs, out_specs=out_specs, check_vma=False
    )
```

time: 370 us -> 104 us (0.28)
  waiting for transfers between devices: 277 us -> 16.8 us
  starting transfers between devices: 37.6 us -> 66.2 us
  local copies, waits for them, and re-layouts: 22.6 us -> 2.22 us
  Pallas kernels: 0 us -> 15.5 us
  between operations: 16.3 us -> 0.85 us
  other arithmetic: 8.95 us -> 2.01 us
  matrix products: 6.27 us -> 0 us
    psum x1 -> x0, waiting for transfers between devices: 275 us -> none  [per_device(): total = lax.psum(partial_value, ('lat', 'lon'))]
    all_to_all x0 -> x1, starting transfers between devices: none -> 31.7 us  [per_device(): spread = lax.all_to_all(partial, ('lat', 'lon'), 0, 0, tiled=True)]
    pallas_call x0 -> x5, Pallas kernels: none -> 15.5 us  [the longest x4 13.4 us: run_window(): pl.pallas_call(body, out_shape=out_shape, in_specs=specs, out_specs=out_s...]
    slice x14 -> x0, local copies, waits for them, and re-layouts: 9 us -> none  [the longest x4 3.51 us: advect(): down = jnp.concatenate([lam[:, :, 1:, :], south], axis=2)]
    all_to_all x0 -> x1, waiting for transfers between devices: none -> 8.41 us  [per_device(): spread = lax.all_to_all(partial, ('lat', 'lon'), 0, 0, tiled=True)]
    ppermute x8 -> x10, waiting for transfers between devices: 1.36 us -> 8.41 us  [the longest x4 5.85 us: to_north(): return lax.ppermute(block, 'lat', [(i + 1, i) for i in range(bands - 1)])]
    dot_general x13 -> x0, matrix products: 6.27 us -> none  [the longest x12 5.19 us: transposed(): lax.dot_general(mats, right_side, (((1,), (1,)), ((0,), (0,))), preferred...]
    add x4 -> x0, other arithmetic: 5.65 us -> none  [the longest x3 5.64 us: advect(): return (1.0 - clon - clat) * lam + clat * down + clon * right]
  transfers between devices with their start and end apart: 9 -> 11, of which waited for: 3 -> 4; matrix products, arithmetic and copies ran while one was open for 4% -> 3% of each run, Pallas kernels for 0% -> 5%
where the time goes in v1:
time: 104 us
  starting transfers between devices  66.2 us (64%)
  waiting for transfers between devices  16.8 us (16%)
  Pallas kernels  15.5 us (15%)
  local copies, waits for them, and re-layouts  2.22 us (2%)
  other arithmetic  2.01 us (2%)
    all_to_all x1, starting transfers between devices, per_device(): spread = lax.all_to_all(partial, ('lat', 'lon'), 0, 0, tiled=True)  31.7 us
    ppermute x3, starting transfers between devices, to_west(): lax.ppermute(block, 'lon', [((j + 1) % blocks, j) for j in range(blocks)])  25.3 us
    pallas_call x4, Pallas kernels, run_window(): pl.pallas_call(body, out_shape=out_shape, in_specs=specs, out_specs=out_s...  13.4 us
    all_to_all x1, waiting for transfers between devices, per_device(): spread = lax.all_to_all(partial, ('lat', 'lon'), 0, 0, tiled=True)  8.41 us
    ppermute x4, waiting for transfers between devices, to_north(): return lax.ppermute(block, 'lat', [(i + 1, i) for i in range(bands - 1)])  5.85 us
    ppermute x4, starting transfers between devices, to_north(): return lax.ppermute(block, 'lat', [(i + 1, i) for i in range(bands - 1)])  5.16 us
    ppermute x3, starting transfers between devices, to_northwest(): return lax.ppermute(block, ('lat', 'lon'), route)  4.01 us
    ppermute x3, waiting for transfers between devices, to_northwest(): return lax.ppermute(block, ('lat', 'lon'), route)  2.55 us
  transfers between devices with their start and end apart: 11, of which 4 were waited for; matrix products, arithmetic and copies ran while one was open for 3% of the time, Pallas kernels for 5%

profile of v1, /device:TPU:1, one launch (start us, length us, event | category | flops | bytes accessed | tf_op | source)
XLA Modules:
  0.0 103.6 jit_solution(1078342747483334457)
XLA Ops:
  0.6 2.1 %pack.1 = (f32[208,128]{1,0:T(8,128)}, f32[1400,128]{1,0:T(8,128)}, f32[208,128]{1,0:T(8,128)}) custom-call(bf16[8,200,128]{2,1,0:T(8,128)(2,1)} %bitcast.20, f32[2,128]{1,0:T(2,128)} %refs_4_.7, f32[2,128]{1,0:T(2,128)} %refs_5_.7), custom_call_target="tpu_custom_call" | custom-call | tf_op jit(solution)/shard_map/pack/pallas_call | solution.py:299
  2.7 1.3 %collective-permute-start = (f32[1400,128]{1,0:T(8,128)}, f32[1400,128]{1,0:T(8,128)S(1)}, u32[]{:S(2)}, u32[]{:S(2)}) collective-permute-start(f32[1400,128]{1,0:T(8,128)} %get-tuple-element.13.refs_0_), channel_id=1, source_target_pairs={{32,0},{64,32},{96,64},{128,96},{160,128},{192,160},{224,192},{256... | collective-permute-start | bytes 2150408 | tf_op jit(solution)/shard_map/ppermute | solution.py:271
  4.0 1.3 %collective-permute-start.1 = (f32[208,128]{1,0:T(8,128)}, f32[208,128]{1,0:T(8,128)S(1)}, u32[]{:S(2)}, u32[]{:S(2)}) collective-permute-start(f32[208,128]{1,0:T(8,128)} %get-tuple-element.14.refs_0_), channel_id=1, source_target_pairs={{32,0},{64,32},{96,64},{128,96},{160,128},{192,160},{224,192},{256... | collective-permute-start | bytes 319496 | tf_op jit(solution)/shard_map/ppermute | solution.py:271
  5.3 0.0 copy-start.3
  5.3 1.4 %collective-permute-start.3 = (f32[208,128]{1,0:T(8,128)}, f32[208,128]{1,0:T(8,128)S(1)}, u32[]{:S(2)}, u32[]{:S(2)}) collective-permute-start(f32[208,128]{1,0:T(8,128)} %get-tuple-element.15), channel_id=1, source_target_pairs={{33,0},{34,1},{35,2},{36,3},{37,4},{38,5},{39,6},{40,7},{41,8},{42... | collective-permute-start | bytes 319496 | tf_op jit(solution)/shard_map/ppermute | solution.py:286
  6.7 8.8 %collective-permute-start.2 = (f32[208,128]{1,0:T(8,128)}, f32[208,128]{1,0:T(8,128)S(1)}, u32[]{:S(2)}, u32[]{:S(2)}) collective-permute-start(f32[208,128]{1,0:T(8,128)} %get-tuple-element.15), channel_id=1, source_target_pairs={{1,0},{2,1},{3,2},{4,3},{5,4},{6,5},{7,6},{8,7},{9,8},{10,9},{11,1... | collective-permute-start | bytes 319496 | tf_op jit(solution)/shard_map/ppermute | solution.py:276
  15.5 0.0 copy-start.2
  15.6 0.0 copy-start.6
  15.6 1.5 %copy.12 = bf16[3,8,100,100]{2,3,1,0:T(8,128)(2,1)S(1)} copy(bf16[3,8,100,100]{3,1,2,0:T(8,128)(2,1)} %param.10) | data formatting | bytes 960000 | tf_op args[2]
  17.1 3.0 %collective-permute-done.1.refs_1_.refs_6_ = f32[208,128]{1,0:T(8,128)S(1)} collective-permute-done((f32[208,128]{1,0:T(8,128)}, f32[208,128]{1,0:T(8,128)S(1)}, u32[]{:S(2)}, u32[]{:S(2)}) %collective-permute-start.1) | collective-permute-done | bytes 106528 | tf_op jit(solution)/shard_map/ppermute | solution.py:271
  20.1 0.0 collective-permute-done.3.refs_3_
  20.1 0.0 collective-permute-done.2.refs_2_.refs_7_
  20.1 0.6 copy-done.5
  20.8 1.7 %window1_from0.1 = (f32[200,128]{1,0:T(8,128)S(1)}, f32[200,128]{1,0:T(8,128)S(1)}) custom-call(f32[208,128]{1,0:T(8,128)S(1)} %copy-done.3, f32[208,128]{1,0:T(8,128)S(1)} %collective-permute-done.1.refs_1_.refs_6_, f32[208,128]{1,0:T(8,128)S(1)} %collective-permute-done.2.refs_2_.refs_7_, f32[208,128]{1,0:T(8,128)S(1)} %collective-permute-done.3.refs_3_, ...), custom_call_target="tpu_custom_call" | custom-call | tf_op jit(solution)/shard_map/window1_from0/pallas_call | solution.py:257
  22.5 1.3 %collective-permute-start.4 = (f32[200,128]{1,0:T(8,128)S(1)}, f32[200,128]{1,0:T(8,128)S(1)}, u32[]{:S(2)}, u32[]{:S(2)}) collective-permute-start(f32[200,128]{1,0:T(8,128)S(1)} %get-tuple-element.16.refs_0_.refs_11_), channel_id=1, source_target_pairs={{32,0},{64,32},{96,64},{128,96},{160,128},{192,160},{224,192},{256... | collective-permute-start | bytes 307208 | tf_op jit(solution)/shard_map/ppermute | solution.py:271
  23.8 0.0 copy-start.7
  23.8 1.3 %collective-permute-start.6 = (f32[200,128]{1,0:T(8,128)S(1)}, f32[200,128]{1,0:T(8,128)S(1)}, u32[]{:S(2)}, u32[]{:S(2)}) collective-permute-start(f32[200,128]{1,0:T(8,128)S(1)} %get-tuple-element.17), channel_id=1, source_target_pairs={{33,0},{34,1},{35,2},{36,3},{37,4},{38,5},{39,6},{40,7},{41,8},{42... | collective-permute-start | bytes 307208 | tf_op jit(solution)/shard_map/ppermute | solution.py:286
  25.1 10.3 %collective-permute-start.5 = (f32[200,128]{1,0:T(8,128)S(1)}, f32[200,128]{1,0:T(8,128)S(1)}, u32[]{:S(2)}, u32[]{:S(2)}) collective-permute-start(f32[200,128]{1,0:T(8,128)S(1)} %get-tuple-element.17), channel_id=1, source_target_pairs={{1,0},{2,1},{3,2},{4,3},{5,4},{6,5},{7,6},{8,7},{9,8},{10,9},{11,1... | collective-permute-start | bytes 307208 | tf_op jit(solution)/shard_map/ppermute | solution.py:276
  35.4 2.9 %collective-permute-done.4.refs_1_ = f32[200,128]{1,0:T(8,128)S(1)} collective-permute-done((f32[200,128]{1,0:T(8,128)S(1)}, f32[200,128]{1,0:T(8,128)S(1)}, u32[]{:S(2)}, u32[]{:S(2)}) %collective-permute-start.4) | collective-permute-done | bytes 102432 | tf_op jit(solution)/shard_map/ppermute | solution.py:271
  38.2 2.5 %collective-permute-done.6.refs_3_ = f32[200,128]{1,0:T(8,128)S(1)} collective-permute-done((f32[200,128]{1,0:T(8,128)S(1)}, f32[200,128]{1,0:T(8,128)S(1)}, u32[]{:S(2)}, u32[]{:S(2)}) %collective-permute-start.6) | collective-permute-done | bytes 102432 | tf_op jit(solution)/shard_map/ppermute | solution.py:286
  40.8 3.4 %window0_from0.1 = (bf16[8,200,128]{2,1,0:T(8,128)(2,1)}, f32[512,128]{1,0:T(8,128)}) custom-call(f32[200,128]{1,0:T(8,128)S(1)} %get-tuple-element.16.refs_0_.refs_11_, f32[200,128]{1,0:T(8,128)S(1)} %collective-permute-done.4.refs_1_, f32[200,128]{1,0:T(8,128)S(1)} %collective-permute-done.5.refs_2_, f32[200,128]{1,0:T(8,128)S(1)} %collective-permute-done.6.refs_3_, ...), custom_call_target="tpu_custom_call" | custom-call | tf_op jit(solution)/shard_map/window0_from0/pallas_call | solution.py:257
  44.2 0.0 collective-permute-done.refs_1_
  44.2 3.9 %window1_from1.1 = (f32[1400,128]{1,0:T(8,128)S(1)}, f32[200,128]{1,0:T(8,128)S(1)}) custom-call(f32[1400,128]{1,0:T(8,128)S(1)} %copy-done.1, f32[1400,128]{1,0:T(8,128)S(1)} %collective-permute-done.refs_1_, f32[208,128]{1,0:T(8,128)S(1)} %collective-permute-done.2.refs_2_.refs_7_, f32[208,128]{1,0:T(8,128)S(1)} %collective-permute-done.3.refs_3_, ...), custom_call_target="tpu_custom_call" | custom-call | tf_op jit(solution)/shard_map/window1_from1/pallas_call | solution.py:257
  48.1 1.3 %collective-permute-start.7 = (f32[1400,128]{1,0:T(8,128)S(1)}, f32[1400,128]{1,0:T(8,128)S(1)}, u32[]{:S(2)}, u32[]{:S(2)}) collective-permute-start(f32[1400,128]{1,0:T(8,128)S(1)} %get-tuple-element.20.refs_0_), channel_id=1, source_target_pairs={{32,0},{64,32},{96,64},{128,96},{160,128},{192,160},{224,192},{256... | collective-permute-start | bytes 2150408 | tf_op jit(solution)/shard_map/ppermute | solution.py:271
  49.4 31.7 %all-to-all-start = ((f32[512,1,128]{2,1,0:T(1,128)}), f32[512,1,128]{2,1,0:T(1,128)}, u32[]{:S(2)}, u32[]{:S(2)}) async-start(f32[512,1,128]{2,1,0:T(1,128)} %bitcast.6), calls=%async_computation | async-start | bytes 524288 | tf_op jit(solution)/shard_map/all_to_all | solution.py:324
  81.1 1.3 %collective-permute-start.9 = (f32[200,128]{1,0:T(8,128)S(1)}, f32[200,128]{1,0:T(8,128)S(1)}, u32[]{:S(2)}, u32[]{:S(2)}) collective-permute-start(f32[200,128]{1,0:T(8,128)S(1)} %get-tuple-element.21), channel_id=1, source_target_pairs={{33,0},{34,1},{35,2},{36,3},{37,4},{38,5},{39,6},{40,7},{41,8},{42... | collective-permute-start | bytes 307208 | tf_op jit(solution)/shard_map/ppermute | solution.py:286
  82.4 6.3 %collective-permute-start.8 = (f32[200,128]{1,0:T(8,128)S(1)}, f32[200,128]{1,0:T(8,128)S(1)}, u32[]{:S(2)}, u32[]{:S(2)}) collective-permute-start(f32[200,128]{1,0:T(8,128)S(1)} %get-tuple-element.21), channel_id=1, source_target_pairs={{1,0},{2,1},{3,2},{4,3},{5,4},{6,5},{7,6},{8,7},{9,8},{10,9},{11,1... | collective-permute-start | bytes 307208 | tf_op jit(solution)/shard_map/ppermute | solution.py:276
  88.7 8.4 %all-to-all-done = f32[512,1,128]{2,1,0:T(1,128)} async-done(((f32[512,1,128]{2,1,0:T(1,128)}), f32[512,1,128]{2,1,0:T(1,128)}, u32[]{:S(2)}, u32[]{:S(2)}) %all-to-all-start) | async-done | bytes 262176 | tf_op jit(solution)/shard_map/all_to_all | solution.py:324
  97.1 2.0 %reduce_sum.9 = f32[128]{0:T(128)} reduce(f32[512,1,128]{2,1,0:T(1,128)} %all-to-all-done, f32[]{:T(128)} %constant.0.clone.1), dimensions={0,1}, to_apply=%region_0.0 | reduce | flops 65408 | bytes 262660 | tf_op jit(solution)/shard_map/reduce_sum | solution.py:332
  99.1 0.0 collective-permute-done.9.refs_3_
  99.1 0.0 collective-permute-done.8.refs_2_
  99.1 4.5 %window0_from1.1 = bf16[8,200,128]{2,1,0:T(8,128)(2,1)} custom-call(f32[1400,128]{1,0:T(8,128)S(1)} %get-tuple-element.20.refs_0_, f32[1400,128]{1,0:T(8,128)S(1)} %collective-permute-done.7.refs_1_, f32[200,128]{1,0:T(8,128)S(1)} %collective-permute-done.8.refs_2_, f32[200,128]{1,0:T(8,128)S(1)} %collective-permute-done.9.refs_3_, ...), custom_call_target="tpu_custom_call", output_to_operand_aliasing={{}: (11, {})} | custom-call | tf_op jit(solution)/shard_map/window0_from1/pallas_call | solution.py:257
  (13 shorter events, 0.0 us)
Async XLA Ops:
  0.6 19.4 %copy-start = (bf16[2,8,100,2,128]{4,3,2,1,0:T(2,128)(2,1)S(1)}, bf16[2,8,100,2,128]{4,3,2,1,0:T(2,128)(2,1)}, u32[]{:S(2)}) copy-start(bf16[2,8,100,2,128]{4,3,2,1,0:T(2,128)(2,1)} %param.9) | copy-start | bytes 2457604
  2.7 41.5 %collective-permute-start = (f32[1400,128]{1,0:T(8,128)}, f32[1400,128]{1,0:T(8,128)S(1)}, u32[]{:S(2)}, u32[]{:S(2)}) collective-permute-start(f32[1400,128]{1,0:T(8,128)} %get-tuple-element.13.refs_0_), channel_id=1, source_target_pairs={{32,0},{64,32},{96,64},{128,96},{160,128},{192,160},{224,192},{256... | collective-permute-start | bytes 2150408 | tf_op jit(solution)/shard_map/ppermute | solution.py:271
  4.0 16.1 %collective-permute-start.1 = (f32[208,128]{1,0:T(8,128)}, f32[208,128]{1,0:T(8,128)S(1)}, u32[]{:S(2)}, u32[]{:S(2)}) collective-permute-start(f32[208,128]{1,0:T(8,128)} %get-tuple-element.14.refs_0_), channel_id=1, source_target_pairs={{32,0},{64,32},{96,64},{128,96},{160,128},{192,160},{224,192},{256... | collective-permute-start | bytes 319496 | tf_op jit(solution)/shard_map/ppermute | solution.py:271
  5.3 14.8 %copy-start.3 = (f32[208,128]{1,0:T(8,128)S(1)}, f32[208,128]{1,0:T(8,128)}, u32[]{:S(2)}) copy-start(f32[208,128]{1,0:T(8,128)} %get-tuple-element.14.refs_0_) | copy-start | bytes 319492
  5.3 14.8 %collective-permute-start.3 = (f32[208,128]{1,0:T(8,128)}, f32[208,128]{1,0:T(8,128)S(1)}, u32[]{:S(2)}, u32[]{:S(2)}) collective-permute-start(f32[208,128]{1,0:T(8,128)} %get-tuple-element.15), channel_id=1, source_target_pairs={{33,0},{34,1},{35,2},{36,3},{37,4},{38,5},{39,6},{40,7},{41,8},{42... | collective-permute-start | bytes 319496 | tf_op jit(solution)/shard_map/ppermute | solution.py:286
  6.7 13.3 %collective-permute-start.2 = (f32[208,128]{1,0:T(8,128)}, f32[208,128]{1,0:T(8,128)S(1)}, u32[]{:S(2)}, u32[]{:S(2)}) collective-permute-start(f32[208,128]{1,0:T(8,128)} %get-tuple-element.15), channel_id=1, source_target_pairs={{1,0},{2,1},{3,2},{4,3},{5,4},{6,5},{7,6},{8,7},{9,8},{10,9},{11,1... | collective-permute-start | bytes 319496 | tf_op jit(solution)/shard_map/ppermute | solution.py:276
  15.5 4.6 %copy-start.2 = (s32[8,2,128]{2,1,0:T(2,128)S(1)}, s32[8,2,128]{2,1,0:T(2,128)}, u32[]{:S(2)}) copy-start(s32[8,2,128]{2,1,0:T(2,128)} %refs_8_.7) | copy-start | bytes 24580
  15.6 4.6 %copy-start.6 = (f32[2,128]{1,0:T(2,128)S(1)}, f32[2,128]{1,0:T(2,128)}, u32[]{:S(2)}) copy-start(f32[2,128]{1,0:T(2,128)} %refs_5_.7) | copy-start | bytes 3076
  20.1 0.7 copy-start.5
  20.8 20.0 %copy-start.4 = (f32[100,2,128]{2,1,0:T(2,128)S(1)}, f32[100,2,128]{2,1,0:T(2,128)}, u32[]{:S(2)}) copy-start(f32[100,2,128]{2,1,0:T(2,128)} %param.13) | copy-start | bytes 307204
  22.5 15.8 %collective-permute-start.4 = (f32[200,128]{1,0:T(8,128)S(1)}, f32[200,128]{1,0:T(8,128)S(1)}, u32[]{:S(2)}, u32[]{:S(2)}) collective-permute-start(f32[200,128]{1,0:T(8,128)S(1)} %get-tuple-element.16.refs_0_.refs_11_), channel_id=1, source_target_pairs={{32,0},{64,32},{96,64},{128,96},{160,128},{192,160},{224,192},{256... | collective-permute-start | bytes 307208 | tf_op jit(solution)/shard_map/ppermute | solution.py:271
  23.8 17.0 %copy-start.7 = (s32[2,128]{1,0:T(2,128)S(1)}, s32[2,128]{1,0:T(2,128)}, u32[]{:S(2)}) copy-start(s32[2,128]{1,0:T(2,128)} %refs_13_.1) | copy-start | bytes 3076
  23.8 17.0 %collective-permute-start.6 = (f32[200,128]{1,0:T(8,128)S(1)}, f32[200,128]{1,0:T(8,128)S(1)}, u32[]{:S(2)}, u32[]{:S(2)}) collective-permute-start(f32[200,128]{1,0:T(8,128)S(1)} %get-tuple-element.17), channel_id=1, source_target_pairs={{33,0},{34,1},{35,2},{36,3},{37,4},{38,5},{39,6},{40,7},{41,8},{42... | collective-permute-start | bytes 307208 | tf_op jit(solution)/shard_map/ppermute | solution.py:286
  25.1 15.7 %collective-permute-start.5 = (f32[200,128]{1,0:T(8,128)S(1)}, f32[200,128]{1,0:T(8,128)S(1)}, u32[]{:S(2)}, u32[]{:S(2)}) collective-permute-start(f32[200,128]{1,0:T(8,128)S(1)} %get-tuple-element.17), channel_id=1, source_target_pairs={{1,0},{2,1},{3,2},{4,3},{5,4},{6,5},{7,6},{8,7},{9,8},{10,9},{11,1... | collective-permute-start | bytes 307208 | tf_op jit(solution)/shard_map/ppermute | solution.py:276
  40.8 3.4 %copy-start.1 = (f32[1400,128]{1,0:T(8,128)S(1)}, f32[1400,128]{1,0:T(8,128)}, u32[]{:S(2)}) copy-start(f32[1400,128]{1,0:T(8,128)} %get-tuple-element.13.refs_0_) | copy-start | bytes 2150404
  48.1 51.0 %collective-permute-start.7 = (f32[1400,128]{1,0:T(8,128)S(1)}, f32[1400,128]{1,0:T(8,128)S(1)}, u32[]{:S(2)}, u32[]{:S(2)}) collective-permute-start(f32[1400,128]{1,0:T(8,128)S(1)} %get-tuple-element.20.refs_0_), channel_id=1, source_target_pairs={{32,0},{64,32},{96,64},{128,96},{160,128},{192,160},{224,192},{256... | collective-permute-start | bytes 2150408 | tf_op jit(solution)/shard_map/ppermute | solution.py:271
  49.4 47.7 %all-to-all-start = ((f32[512,1,128]{2,1,0:T(1,128)}), f32[512,1,128]{2,1,0:T(1,128)}, u32[]{:S(2)}, u32[]{:S(2)}) async-start(f32[512,1,128]{2,1,0:T(1,128)} %bitcast.6), calls=%async_computation | async-start | bytes 524288 | tf_op jit(solution)/shard_map/all_to_all | solution.py:324
  81.1 18.0 %collective-permute-start.9 = (f32[200,128]{1,0:T(8,128)S(1)}, f32[200,128]{1,0:T(8,128)S(1)}, u32[]{:S(2)}, u32[]{:S(2)}) collective-permute-start(f32[200,128]{1,0:T(8,128)S(1)} %get-tuple-element.21), channel_id=1, source_target_pairs={{33,0},{34,1},{35,2},{36,3},{37,4},{38,5},{39,6},{40,7},{41,8},{42... | collective-permute-start | bytes 307208 | tf_op jit(solution)/shard_map/ppermute | solution.py:286
  82.4 16.7 %collective-permute-start.8 = (f32[200,128]{1,0:T(8,128)S(1)}, f32[200,128]{1,0:T(8,128)S(1)}, u32[]{:S(2)}, u32[]{:S(2)}) collective-permute-start(f32[200,128]{1,0:T(8,128)S(1)} %get-tuple-element.21), channel_id=1, source_target_pairs={{1,0},{2,1},{3,2},{4,3},{5,4},{6,5},{7,6},{8,7},{9,8},{10,9},{11,1... | collective-permute-start | bytes 307208 | tf_op jit(solution)/shard_map/ppermute | solution.py:276

commit v2 on v1

--- a/solution.py
+++ b/solution.py
@@ -8,37 +8,58 @@
 
 STEPS = 3
 EXTRA = 8
+TAIL = 104
+WIDE = 4
 F32 = jnp.float32
 BF16 = jnp.bfloat16
 ANY = pl.BlockSpec(memory_space=pl.ANY)
+HBM = pl.BlockSpec(memory_space=pltpu.HBM)
 VMEM = pl.BlockSpec(memory_space=pltpu.VMEM)
+
+
+def vmem(mib):
+    return pltpu.CompilerParams(vmem_limit_bytes=mib * 2**20)
 
 
 def lanes(shape):
     return lax.broadcasted_iota(jnp.int32, shape, len(shape) - 1)
 
 
-def place(acc, block, slot):
-    moved = pltpu.roll(block, 2 * slot, 1) if slot else block
+def place(acc, block, start):
+    moved = pltpu.roll(block, start, 1) if start else block
     at = lanes(block.shape)
-    return jnp.where((at >= 2 * slot) & (at < 2 * slot + 2), moved, acc)
-
-
-def pack_kernel(adj, clon, clat, first, rest, west, *, rows):
-    levels = adj.shape[0]
-    acc = jnp.zeros((rows, adj.shape[2]), F32)
+    return jnp.where((at >= start) & (at < start + WIDE), moved, acc)
+
+
+def tall(row):
+    return jnp.broadcast_to(row, (8, row.shape[1]))
+
+
+def pack_kernel(adj, clon, clat, stiff, state_h, first, rest, west, state_s, sem, *, rows):
+    levels, _, width = adj.shape
+    half = width // 2
+    get = pltpu.make_async_copy(state_h.at[state_h.shape[0] - 1], state_s, sem)
+    get.start()
+    acc = jnp.zeros((rows, width), F32)
+    grades = jnp.zeros((8, width), F32)
     for lev in range(levels):
         block = adj[lev].astype(F32)
         if lev == 0:
             first[0:rows] = block
         else:
             rest[(lev - 1) * rows : lev * rows] = block
-        acc = place(acc, block, lev)
+        acc = place(acc, block, WIDE * lev)
+        both = stiff[lev].astype(F32)
+        grades = place(grades, tall(both[0:1]), WIDE * lev)
+        grades = place(grades, tall(both[1:2]), half + WIDE * lev)
+    get.wait()
+    for lev in range(levels):
+        acc = place(acc, state_s[lev].astype(F32), half + WIDE * lev)
     west[0:rows] = acc
     for out in (first, west):
         out[rows : rows + 2] = clon[...]
         out[rows + 2 : rows + 4] = clat[...]
-        out[rows + 4 : rows + 8] = jnp.zeros((4, clon.shape[1]), F32)
+        out[rows + 4 : rows + 8] = grades[0:4]
 
 
 def pull(block, lane_from, lane_to, width):
@@ -46,36 +67,41 @@
     return pltpu.roll(block, shift, 1) if shift else block
 
 
-def advected(own, north, west, diag, lev, slot, cour):
-    rows, width = cour["rows"], own.shape[1]
-    spec = rows // 2
-    last = lanes((spec, width)) == width - 1
-    base = lev * rows
-
-    def pick(ref, start, parity):
-        return ref[pl.ds(start + parity, spec, stride=2), :]
+def mixed(cour, at, mid, down, east):
+    return cour["keep"][at] * mid + cour["lat"][at] * down + cour["lon"][at] * east
+
+
+def with_keep(lon, lat):
+    return {"lon": lon, "lat": lat, "keep": [1.0 - a - b for a, b in zip(lon, lat)]}
+
+
+def advected(own, north, west, corner, lev, start, cour):
+    width = own.shape[1]
+    spec = west.shape[0] // 2
+    end = width - 1
+    last = lanes((spec, width)) == end
+    base = lev * 2 * spec
+
+    def pick(ref, first, parity):
+        return ref[pl.ds(first + parity, spec, stride=2), :]
 
     r0, r1 = pick(own, base, 0), pick(own, base, 1)
     r2, r3 = pick(north, base, 0), pick(north, base, 1)
-    w0, w1, d = pick(west, 0, 0), pick(west, 0, 1), pick(diag, 0, 0)
-    end = width - 1
-    e0, e1 = pull(w0, 2 * slot, end, width), pull(w1, 2 * slot, end, width)
-    g0, g1 = pull(w0, 2 * slot + 1, end, width), pull(w1, 2 * slot + 1, end, width)
-    d0 = pull(d, 2 * slot, end, width)
+    w0, w1 = pick(west, 0, 0), pick(west, 0, 1)
+    e0, e1 = pull(w0, start, end, width), pull(w1, start, end, width)
+    g0, g1 = pull(w0, start + 1, end, width), pull(w1, start + 1, end, width)
+    d0 = pull(corner, start, end, width)
 
     def right(block, edge):
         return jnp.where(last, edge, pltpu.roll(block, width - 1, 1))
 
-    def step(mid, down, east, at):
-        return cour["keep"][at] * mid + cour["lat"][at] * down + cour["lon"][at] * east
-
-    a0 = step(r0, r1, right(r0, e0), 0)
-    a1 = step(r1, r2, right(r1, e1), 1)
-    a2 = step(r2, r3, right(r2, d0), 2)
-    f0 = step(e0, e1, g0, 3)
-    f1 = step(e1, d0, g1, 4)
-    b0 = step(a0, a1, right(a0, f0), 0)
-    b1 = step(a1, a2, right(a1, f1), 1)
+    a0 = mixed(cour, 0, r0, r1, right(r0, e0))
+    a1 = mixed(cour, 1, r1, r2, right(r1, e1))
+    a2 = mixed(cour, 2, r2, r3, right(r2, d0))
+    f0 = mixed(cour, 3, e0, e1, g0)
+    f1 = mixed(cour, 4, e1, d0, g1)
+    b0 = mixed(cour, 0, a0, a1, right(a0, f0))
+    b1 = mixed(cour, 1, a1, a2, right(a1, f1))
     return b0, b1
 
 
@@ -83,14 +109,73 @@
     width = clon.shape[1]
 
     def edge(row):
-        return pltpu.roll(jnp.broadcast_to(row, (8, width)), width - 1, 1)[0:1]
+        return pltpu.roll(tall(row), width - 1, 1)[0:1]
 
     lon = [clon[0:1], clon[1:2], north_c[rows : rows + 1]]
     lat = [clat[0:1], clat[1:2], north_c[rows + 2 : rows + 3]]
     lon += [edge(west_c[rows : rows + 1]), edge(west_c[rows + 1 : rows + 2])]
     lat += [edge(west_c[rows + 2 : rows + 3]), edge(west_c[rows + 3 : rows + 4])]
-    keep = [1.0 - a - b for a, b in zip(lon, lat)]
-    return {"rows": rows, "lon": lon, "lat": lat, "keep": keep}
+    return with_keep(lon, lat)
+
+
+def strip_kernel(west, diag, mats, out, *, rows):
+    spec, width = rows // 2, west.shape[1]
+    half = width // 2
+    levels = mats.shape[1]
+    at = lanes((spec, width))
+
+    def pick(ref, parity):
+        return ref[pl.ds(parity, spec, stride=2), :]
+
+    def spread(row):
+        wide = tall(row)
+        acc = jnp.zeros((8, width), F32)
+        for lev in range(levels):
+            acc = place(acc, wide, WIDE * lev)
+        return acc[0:1]
+
+    def right(block):
+        return pltpu.roll(block, width - 1, 1)
+
+    w0, w1, d0, d1 = pick(west, 0), pick(west, 1), pick(diag, 0), pick(diag, 1)
+    lon = [spread(west[rows + i : rows + i + 1]) for i in range(2)]
+    lat = [spread(west[rows + i : rows + i + 1]) for i in range(2, 4)]
+    lon.append(spread(diag[rows : rows + 1]))
+    lat.append(spread(diag[rows + 2 : rows + 3]))
+    cour = with_keep(lon, lat)
+    a0 = mixed(cour, 0, w0, w1, right(w0))
+    a1 = mixed(cour, 1, w1, d0, right(w1))
+    a2 = mixed(cour, 2, d0, d1, right(d0))
+    b0 = mixed(cour, 0, a0, a1, right(a0))
+    b1 = mixed(cour, 1, a1, a2, right(a1))
+    value = jnp.where(at < half, b0, pltpu.roll(b1, half, 1))
+    factor = jnp.where(at < half, pltpu.roll(w0, half, 1), w1)
+    live = west[rows + 4 : rows + 5]
+    group = (at & (half - 1)) // WIDE
+
+    def times(s, right_side):
+        low = right_side.astype(BF16)
+        acc = jnp.dot(mats[s, 0], low, preferred_element_type=F32)
+        for lev in range(1, levels):
+            prod = jnp.dot(mats[s, lev], low, preferred_element_type=F32)
+            acc = jnp.where(group == lev, prod, acc)
+        return acc
+
+    def stage(i, value):
+        s = STEPS - 1 - i
+        one = times(s, value)
+        two = times(s, one * factor)
+        three = times(s, two * factor)
+        cand = 0.4 * value + 0.3 * one + 0.2 * two + 0.1 * three
+        return jnp.where(live > s.astype(F32), cand, value)
+
+    value = lax.fori_loop(0, STEPS, stage, value)
+    out[pl.ds(0, spec, stride=2), :] = value
+    out[pl.ds(1, spec, stride=2), :] = pltpu.roll(value, half, 1)
+
+
+def sum_kernel(parts, out):
+    out[...] = jnp.sum(parts[...], axis=0, keepdims=True)
 
 
 def split3(value):
@@ -102,23 +187,24 @@
 
 
 def window_kernel(
-    *refs, window, first_level, count, rows, slots, last, grad, regions
+    *refs, window, first_level, count, rows, last, grad, regions
 ):
     refs = list(refs)
-    own, north, west, diag, clon, clat, north_c, west_c, stiff, state_h, mats_h = refs[:11]
+    own, north, west, corner_r, clon, clat, north_c, west_c, stiff, state_h, mats_h = refs[:11]
     refs = refs[11:]
     if grad:
         before, emission, region = refs[:3]
         refs = refs[3:]
     if last and not grad:
         refs = refs[1:]
+    if not last:
+        edge_r = refs.pop(0)
     if last:
         out_h = refs.pop(0)
         if grad:
             partial = refs.pop(0)
     else:
-        lam_out, west_out = refs[:2]
-        refs = refs[2:]
+        lam_out = refs.pop(0)
     x_s, y_s, flat_s, state_s, mats_s, sems = refs[:6]
     refs = refs[6:]
     spec, width = rows // 2, clon.shape[1]
@@ -131,8 +217,14 @@
     get_state.start()
     get_mats.start()
     cour = courant(clon, clat, north_c, west_c, rows)
+    if last:
+        corner = north[count * rows : count * rows + spec]
+    else:
+        corner = corner_r[pl.ds(0, spec, stride=2), :]
+    west_v = west.at[0:rows]
     for lev in range(count):
-        b0, b1 = advected(own, north, west, diag, lev, slots[lev], cour)
+        start = WIDE * (first_level + lev)
+        b0, b1 = advected(own, north, west_v, corner, lev, start, cour)
         x_s[lev, :, 0:width] = b0
         x_s[lev, :, width : 2 * width] = b1
     get_state.wait()
@@ -163,7 +255,6 @@
         return carry
 
     lax.fori_loop(0, STEPS, stage, 0)
-    acc = [jnp.zeros((spec, width), F32)] * 2
     for lev in range(count):
         for r in range(2):
             half = x_s[lev, :, r * width : (r + 1) * width]
@@ -171,10 +262,10 @@
                 flat_s[lev, pl.ds(r, spec, stride=2), :] = half
             else:
                 lam_out[pl.ds(lev * rows + r, spec, stride=2), :] = half
-                acc[r] = place(acc[r], half, lev)
     if not last:
-        for r in range(2):
-            west_out[pl.ds(r, spec, stride=2), :] = acc[r]
+        lam_out[count * rows : count * rows + spec] = edge_r[pl.ds(0, spec, stride=2), :]
+        pad = TAIL - spec
+        lam_out[count * rows + spec :] = jnp.zeros((pad, width), F32)
         return
     out_s = refs.pop(0)
     for lev in range(count):
@@ -202,20 +293,23 @@
 
 
 def run_window(
-    own, north, west, diag, shared, window, first_level, count, slots, last, extra=None, prior=None
+    own, north, west, corner, shared, window, first_level, count, last, extra=None, prior=None, edge=None
 ):
     clon, clat, north_c, west_c, stiff, state, mats = shared
     rows, width = state.shape[2], state.shape[3]
     spec = rows // 2
     grad = extra is not None
     regions = 0
-    args = [own, north, west, diag, clon, clat, north_c, west_c, stiff, state, mats]
+    args = [own, north, west, corner, clon, clat, north_c, west_c, stiff, state, mats]
     specs = [VMEM] * 9 + [ANY] * 2
     aliases = {}
     if grad:
         before, emission, region, regions = extra
         args += [before, emission, region]
         specs += [VMEM] * 3
+    if not last:
+        args.append(edge)
+        specs.append(VMEM)
     if last:
         levels = state.shape[1]
         if not grad:
@@ -229,10 +323,9 @@
             out_specs.append(VMEM)
     else:
         out_shape = [
-            jax.ShapeDtypeStruct((count * rows, width), F32),
-            jax.ShapeDtypeStruct((rows, width), F32),
+            jax.ShapeDtypeStruct((count * rows + TAIL, width), F32),
         ]
-        out_specs = [VMEM] * 2
+        out_specs = [VMEM]
     scratch = [
         pltpu.VMEM((count, spec, 2 * width), F32),
         pltpu.VMEM((count, spec, 2 * width), F32),
@@ -249,7 +342,6 @@
         first_level=first_level,
         count=count,
         rows=rows,
-        slots=slots,
         last=last,
         grad=grad,
         regions=regions,
@@ -262,7 +354,7 @@
         scratch_shapes=scratch,
         input_output_aliases=aliases,
         name=f"window{window}_from{first_level}",
-        compiler_params=pltpu.CompilerParams(vmem_limit_bytes=32 * 2**20),
+        compiler_params=vmem(40 if count > 1 else 8),
     )(*args)
 
 
@@ -303,33 +395,55 @@
             jax.ShapeDtypeStruct(((levels - 1) * rows, width), F32),
             jax.ShapeDtypeStruct((rows + EXTRA, width), F32),
         ],
-        in_specs=[VMEM] * 3,
+        in_specs=[VMEM] * 4 + [HBM],
         out_specs=[VMEM] * 3,
+        scratch_shapes=[pltpu.VMEM((levels, rows, width), BF16), pltpu.SemaphoreType.DMA],
         name="pack",
-    )(adj, courant_lon, courant_lat)
+        compiler_params=vmem(56),
+    )(adj, courant_lon, courant_lat, stiffness, flat_state)
     low1_n = to_north(low1)
     west1_w = to_west(west1)
     west1_d = to_northwest(west1)
+    rest1, low1_n, west1_w, west1_d = lax.optimization_barrier(
+        (rest1, low1_n, west1_w, west1_d)
+    )
     rest1_n = to_north(rest1)
     shared = (courant_lon, courant_lat, low1_n, west1_w, stiffness, flat_state, mats)
-    low0, low0_p = run_window(
-        low1, low1_n, west1_w, west1_d, shared, 1, 0, 1, [0], False
-    )
+    strip = pl.pallas_call(
+        functools.partial(strip_kernel, rows=rows),
+        out_shape=jax.ShapeDtypeStruct((rows, width), F32),
+        in_specs=[VMEM] * 3,
+        out_specs=VMEM,
+        name="strip",
+        compiler_params=vmem(8),
+    )(west1_w, west1_d, mats)
+    low0 = run_window(
+        low1, low1_n, west1_w, west1_d, shared, 1, 0, 1, False, edge=strip
+    )[0]
+    low0_n = to_north(low0)
+    rest1_n, low0_n = lax.optimization_barrier((rest1_n, low0_n))
+    rest0 = run_window(
+        rest1, rest1_n, west1_w, west1_d, shared, 1, 1, levels - 1, False, edge=strip
+    )[0]
+    rest0_n = to_north(rest0)
+    low0_n, rest0 = lax.optimization_barrier((low0_n, rest0))
     low_extra = (low0, flat_em, region_id, regions)
     out, partial = run_window(
-        low0, to_north(low0), to_west(low0_p), to_northwest(low0_p),
-        shared, 0, 0, 1, [0], True, extra=low_extra,
-    )
-    rest1_n, partial = lax.optimization_barrier((rest1_n, partial))
+        low0, low0_n, strip, strip, shared, 0, 0, 1, True, extra=low_extra
+    )
     spread = lax.all_to_all(partial, ("lat", "lon"), 0, 0, tiled=True)
-    rest0, rest0_p = run_window(
-        rest1, rest1_n, west1_w, west1_d, shared, 1, 1, levels - 1, list(range(1, levels)), False
-    )
     out = run_window(
-        rest0, to_north(rest0), to_west(rest0_p), to_northwest(rest0_p),
-        shared, 0, 1, levels - 1, list(range(levels - 1)), True, prior=out,
+        rest0, rest0_n, strip, strip, shared, 0, 1, levels - 1, True, prior=out
     )[0]
-    grad = jnp.sum(spread, axis=0, keepdims=True)[:, :spec]
+    out, spread = lax.optimization_barrier((out, spread))
+    grad = pl.pallas_call(
+        sum_kernel,
+        out_shape=jax.ShapeDtypeStruct((1, width), F32),
+        in_specs=[VMEM],
+        out_specs=VMEM,
+        name="gather_sum",
+        compiler_params=vmem(4),
+    )(spread)[:, :spec]
     return out.reshape(levels, spec, lat_rows, width), grad
 
 

time: 104 us -> 92.4 us (0.89)
  starting transfers between devices: 66.2 us -> 41.1 us
  waiting for transfers between devices: 16.8 us -> 28.8 us
  Pallas kernels: 15.5 us -> 20.7 us
  other arithmetic: 2.01 us -> 0 us
  local copies, waits for them, and re-layouts: 2.22 us -> 0.57 us
    ppermute x3 -> x1, starting transfers between devices: 25.3 us -> 8.79 us  [to_west(): lax.ppermute(block, 'lon', [((j + 1) % blocks, j) for j in range(blocks)])]
    ppermute x4, waiting for transfers between devices: 5.85 us -> 15.9 us  [to_north(): return lax.ppermute(block, 'lat', [(i + 1, i) for i in range(bands - 1)])]
    all_to_all x1, starting transfers between devices: 31.7 us -> 25.6 us  [per_device(): spread = lax.all_to_all(partial, ('lat', 'lon'), 0, 0, tiled=True)]
    all_to_all x1, waiting for transfers between devices: 8.41 us -> 11.7 us  [per_device(): spread = lax.all_to_all(partial, ('lat', 'lon'), 0, 0, tiled=True)]
    pallas_call x0 -> x2, Pallas kernels: none -> 3.24 us  [the longest x1 2.66 us: per_device(): pl.pallas_call(functools.partial(strip_kernel, rows=rows), out_shape=jax....]
    ppermute x3 -> x1, starting transfers between devices: 4.01 us -> 1.29 us  [to_northwest(): return lax.ppermute(block, ('lat', 'lon'), route)]
    ppermute x3 -> x1, waiting for transfers between devices: 2.55 us -> 0.01 us  [to_northwest(): return lax.ppermute(block, ('lat', 'lon'), route)]
    reduce_sum x1 -> x0, other arithmetic: 2.01 us -> none  [per_device(): grad = jnp.sum(spread, axis=0, keepdims=True)[:, :spec]]
  transfers between devices with their start and end apart: 11 -> 7, of which waited for: 4 -> 3; matrix products, arithmetic and copies ran while one was open for 3% -> 1% of each run, Pallas kernels for 5% -> 14%
where the time goes in v2:
time: 92.4 us; the launch traced here: 92 us
  starting transfers between devices  41.1 us (44%)
  waiting for transfers between devices  28.8 us (31%)
  Pallas kernels  20.7 us (22%)
    all_to_all x1, starting transfers between devices, per_device(): spread = lax.all_to_all(partial, ('lat', 'lon'), 0, 0, tiled=True)  25.6 us
    ppermute x4, waiting for transfers between devices, to_north(): return lax.ppermute(block, 'lat', [(i + 1, i) for i in range(bands - 1)])  15.9 us
    pallas_call x4, Pallas kernels, run_window(): pl.pallas_call(body, out_shape=out_shape, in_specs=specs, out_specs=out_s...  14.4 us
    all_to_all x1, waiting for transfers between devices, per_device(): spread = lax.all_to_all(partial, ('lat', 'lon'), 0, 0, tiled=True)  11.7 us
    ppermute x1, starting transfers between devices, to_west(): lax.ppermute(block, 'lon', [((j + 1) % blocks, j) for j in range(blocks)])  8.79 us
    ppermute x4, starting transfers between devices, to_north(): return lax.ppermute(block, 'lat', [(i + 1, i) for i in range(bands - 1)])  5.42 us
    pallas_call x1, Pallas kernels, per_device(): pl.pallas_call(functools.partial(pack_kernel, rows=rows), out_shape=[jax....  3.05 us
    pallas_call x1, Pallas kernels, per_device(): pl.pallas_call(functools.partial(strip_kernel, rows=rows), out_shape=jax....  2.66 us
  transfers between devices with their start and end apart: 7, of which 3 were waited for; matrix products, arithmetic and copies ran while one was open for 1% of the time, Pallas kernels for 14%

profile of v2, /device:TPU:1, one launch (start us, length us, event | category | flops | bytes accessed | tf_op | source)
XLA Modules:
  0.0 92.0 jit_solution(9139636803045412941)
XLA Ops:
  0.6 0.0 copy-start.8
  0.6 3.0 %pack.1 = (f32[208,128]{1,0:T(8,128)}, f32[1400,128]{1,0:T(8,128)}, f32[208,128]{1,0:T(8,128)}) custom-call(bf16[8,200,128]{2,1,0:T(8,128)(2,1)} %bitcast.22, f32[2,128]{1,0:T(2,128)} %refs_4_.7, f32[2,128]{1,0:T(2,128)} %refs_5_.7, s32[8,2,128]{2,1,0:T(2,128)} %refs_8_.7, bf16[2,8,200,128]{3,2,1,0:T(8,128)(2,1)} %bitcast.15), custom_call_target="tpu_custom_call" | custom-call | tf_op jit(solution)/shard_map/pack/pallas_call | solution.py:391
  3.7 1.3 %collective-permute-start = (f32[208,128]{1,0:T(8,128)}, f32[208,128]{1,0:T(8,128)S(1)}, u32[]{:S(2)}, u32[]{:S(2)}) collective-permute-start(f32[208,128]{1,0:T(8,128)} %get-tuple-element.18.refs_0_), channel_id=1, source_target_pairs={{32,0},{64,32},{96,64},{128,96},{160,128},{192,160},{224,192},{256... | collective-permute-start | bytes 319496 | tf_op jit(solution)/shard_map/ppermute | solution.py:363
  5.0 1.3 %collective-permute-start.2 = (f32[208,128]{1,0:T(8,128)}, f32[208,128]{1,0:T(8,128)S(1)}, u32[]{:S(2)}, u32[]{:S(2)}) collective-permute-start(f32[208,128]{1,0:T(8,128)} %get-tuple-element.19), channel_id=1, source_target_pairs={{33,0},{34,1},{35,2},{36,3},{37,4},{38,5},{39,6},{40,7},{41,8},{42... | collective-permute-start | bytes 319496 | tf_op jit(solution)/shard_map/ppermute | solution.py:378
  6.3 8.8 %collective-permute-start.1 = (f32[208,128]{1,0:T(8,128)}, f32[208,128]{1,0:T(8,128)S(1)}, u32[]{:S(2)}, u32[]{:S(2)}) collective-permute-start(f32[208,128]{1,0:T(8,128)} %get-tuple-element.19), channel_id=1, source_target_pairs={{1,0},{2,1},{3,2},{4,3},{5,4},{6,5},{7,6},{8,7},{9,8},{10,9},{11,1... | collective-permute-start | bytes 319496 | tf_op jit(solution)/shard_map/ppermute | solution.py:368
  15.1 0.0 collective-permute-done.refs_1_.refs_6_
  15.1 0.0 collective-permute-done.2.diag.refs_3_
  15.1 1.1 %collective-permute-done.1.west.refs_2_.refs_7_ = f32[208,128]{1,0:T(8,128)S(1)} collective-permute-done((f32[208,128]{1,0:T(8,128)}, f32[208,128]{1,0:T(8,128)S(1)}, u32[]{:S(2)}, u32[]{:S(2)}) %collective-permute-start.1) | collective-permute-done | bytes 106528 | tf_op jit(solution)/shard_map/ppermute | solution.py:368
  16.2 1.4 %collective-permute-start.3 = (f32[1400,128]{1,0:T(8,128)}, f32[1400,128]{1,0:T(8,128)S(1)}, u32[]{:S(2)}, u32[]{:S(2)}) collective-permute-start(f32[1400,128]{1,0:T(8,128)} %get-tuple-element.20.refs_0_), channel_id=1, source_target_pairs={{32,0},{64,32},{96,64},{128,96},{160,128},{192,160},{224,192},{256... | collective-permute-start | bytes 2150408 | tf_op jit(solution)/shard_map/ppermute | solution.py:363
  17.7 0.0 copy-done.8
  17.7 0.5 copy.12
  18.2 0.0 copy-start.3
  18.2 0.0 copy-start.5
  18.2 0.0 copy-start.6
  18.2 2.7 %strip.1.refs_11_.refs_2_.refs_3_ = f32[200,128]{1,0:T(8,128)S(1)} custom-call(f32[208,128]{1,0:T(8,128)S(1)} %collective-permute-done.1.west.refs_2_.refs_7_, f32[208,128]{1,0:T(8,128)S(1)} %collective-permute-done.2.diag.refs_3_, bf16[3,8,100,100]{3,2,1,0:T(8,128)(2,1)S(1)} %bitcast.10), custom_call_target="tpu_custom_call" | custom-call | tf_op jit(solution)/shard_map/strip/pallas_call | solution.py:412
  20.9 0.0 copy-done
  20.9 0.0 copy-done.2
  20.9 0.0 copy-done.3
  20.9 1.7 %window1_from0.1.refs_0_.refs_11_ = f32[304,128]{1,0:T(8,128)S(1)} custom-call(f32[208,128]{1,0:T(8,128)S(1)} %copy-done.3, f32[208,128]{1,0:T(8,128)S(1)} %collective-permute-done.refs_1_.refs_6_, f32[208,128]{1,0:T(8,128)S(1)} %collective-permute-done.1.west.refs_2_.refs_7_, f32[208,128]{1,0:T(8,128)S(1)} %collective-permute-done.2.diag.refs_3_, ...), custom_call_target="tpu_custom_call" | custom-call | tf_op jit(solution)/shard_map/window1_from0/pallas_call | solution.py:349
  22.7 0.0 copy-start.4
  22.7 1.4 %collective-permute-start.4 = (f32[304,128]{1,0:T(8,128)S(1)}, f32[304,128]{1,0:T(8,128)S(1)}, u32[]{:S(2)}, u32[]{:S(2)}) collective-permute-start(f32[304,128]{1,0:T(8,128)S(1)} %window1_from0.1.refs_0_.refs_11_), channel_id=1, source_target_pairs={{32,0},{64,32},{96,64},{128,96},{160,128},{192,160},{224,192},{256... | collective-permute-start | bytes 466952 | tf_op jit(solution)/shard_map/ppermute | solution.py:363
  24.1 15.9 %collective-permute-done.4.refs_1_ = f32[304,128]{1,0:T(8,128)S(1)} collective-permute-done((f32[304,128]{1,0:T(8,128)S(1)}, f32[304,128]{1,0:T(8,128)S(1)}, u32[]{:S(2)}, u32[]{:S(2)}) %collective-permute-start.4) | collective-permute-done | bytes 155680 | tf_op jit(solution)/shard_map/ppermute | solution.py:363
  40.0 0.0 collective-permute-done.3.refs_1_
  40.0 3.7 %window1_from1.1.refs_0_ = f32[1504,128]{1,0:T(8,128)S(1)} custom-call(f32[1400,128]{1,0:T(8,128)S(1)} %copy-done.1, f32[1400,128]{1,0:T(8,128)S(1)} %collective-permute-done.3.refs_1_, f32[208,128]{1,0:T(8,128)S(1)} %collective-permute-done.1.west.refs_2_.refs_7_, f32[208,128]{1,0:T(8,128)S(1)} %collective-permute-done.2.diag.refs_3_, ...), custom_call_target="tpu_custom_call" | custom-call | tf_op jit(solution)/shard_map/window1_from1/pallas_call | solution.py:349
  43.7 0.0 copy-start.7
  43.8 1.3 %collective-permute-start.5 = (f32[1504,128]{1,0:T(8,128)S(1)}, f32[1504,128]{1,0:T(8,128)}, u32[]{:S(2)}, u32[]{:S(2)}) collective-permute-start(f32[1504,128]{1,0:T(8,128)S(1)} %window1_from1.1.refs_0_), channel_id=1, source_target_pairs={{32,0},{64,32},{96,64},{128,96},{160,128},{192,160},{224,192},{256... | collective-permute-start | bytes 2310152 | tf_op jit(solution)/shard_map/ppermute | solution.py:363
  45.1 3.4 %window0_from0.1 = (bf16[8,200,128]{2,1,0:T(8,128)(2,1)}, f32[512,128]{1,0:T(8,128)}) custom-call(f32[304,128]{1,0:T(8,128)S(1)} %window1_from0.1.refs_0_.refs_11_, f32[304,128]{1,0:T(8,128)S(1)} %collective-permute-done.4.refs_1_, f32[200,128]{1,0:T(8,128)S(1)} %strip.1.refs_11_.refs_2_.refs_3_, f32[200,128]{1,0:T(8,128)S(1)} %strip.1.refs_11_.refs_2_.refs_3_, ...), custom_call_target="tpu_custom_call" | custom-call | tf_op jit(solution)/shard_map/window0_from0/pallas_call | solution.py:349
  48.5 25.6 %all-to-all-start = ((f32[512,1,128]{2,1,0:T(1,128)}), f32[512,1,128]{2,1,0:T(1,128)S(1)}, u32[]{:S(2)}, u32[]{:S(2)}) async-start(f32[512,1,128]{2,1,0:T(1,128)} %bitcast.5), calls=%async_computation | async-start | bytes 524288 | tf_op jit(solution)/shard_map/all_to_all | solution.py:434
  74.1 0.0 collective-permute-done.5.refs_1_
  74.1 5.6 %window0_from1.1 = bf16[8,200,128]{2,1,0:T(8,128)(2,1)} custom-call(f32[1504,128]{1,0:T(8,128)S(1)} %window1_from1.1.refs_0_, f32[1504,128]{1,0:T(8,128)} %collective-permute-done.5.refs_1_, f32[200,128]{1,0:T(8,128)S(1)} %strip.1.refs_11_.refs_2_.refs_3_, f32[200,128]{1,0:T(8,128)S(1)} %strip.1.refs_11_.refs_2_.refs_3_, ...), custom_call_target="tpu_custom_call", output_to_operand_aliasing={{}: (11, {})} | custom-call | tf_op jit(solution)/shard_map/window0_from1/pallas_call | solution.py:349
  79.7 11.7 %all-to-all-done = f32[512,1,128]{2,1,0:T(1,128)S(1)} async-done(((f32[512,1,128]{2,1,0:T(1,128)}), f32[512,1,128]{2,1,0:T(1,128)S(1)}, u32[]{:S(2)}, u32[]{:S(2)}) %all-to-all-start) | async-done | bytes 262176 | tf_op jit(solution)/shard_map/all_to_all | solution.py:434
  91.4 0.6 gather_sum.1
  (8 shorter events, 0.0 us)
Async XLA Ops:
  0.6 17.0 %copy-start.8 = (bf16[3,8,100,100]{3,1,2,0:T(8,128)(2,1)S(1)}, bf16[3,8,100,100]{3,1,2,0:T(8,128)(2,1)}, u32[]{:S(2)}) copy-start(bf16[3,8,100,100]{3,1,2,0:T(8,128)(2,1)} %param.10) | copy-start | bytes 1440004
  3.7 11.4 %collective-permute-start = (f32[208,128]{1,0:T(8,128)}, f32[208,128]{1,0:T(8,128)S(1)}, u32[]{:S(2)}, u32[]{:S(2)}) collective-permute-start(f32[208,128]{1,0:T(8,128)} %get-tuple-element.18.refs_0_), channel_id=1, source_target_pairs={{32,0},{64,32},{96,64},{128,96},{160,128},{192,160},{224,192},{256... | collective-permute-start | bytes 319496 | tf_op jit(solution)/shard_map/ppermute | solution.py:363
  5.0 10.1 %collective-permute-start.2 = (f32[208,128]{1,0:T(8,128)}, f32[208,128]{1,0:T(8,128)S(1)}, u32[]{:S(2)}, u32[]{:S(2)}) collective-permute-start(f32[208,128]{1,0:T(8,128)} %get-tuple-element.19), channel_id=1, source_target_pairs={{33,0},{34,1},{35,2},{36,3},{37,4},{38,5},{39,6},{40,7},{41,8},{42... | collective-permute-start | bytes 319496 | tf_op jit(solution)/shard_map/ppermute | solution.py:378
  6.3 9.9 %collective-permute-start.1 = (f32[208,128]{1,0:T(8,128)}, f32[208,128]{1,0:T(8,128)S(1)}, u32[]{:S(2)}, u32[]{:S(2)}) collective-permute-start(f32[208,128]{1,0:T(8,128)} %get-tuple-element.19), channel_id=1, source_target_pairs={{1,0},{2,1},{3,2},{4,3},{5,4},{6,5},{7,6},{8,7},{9,8},{10,9},{11,1... | collective-permute-start | bytes 319496 | tf_op jit(solution)/shard_map/ppermute | solution.py:368
  16.2 4.7 %copy-start = (bf16[2,8,100,2,128]{4,3,2,1,0:T(2,128)(2,1)S(1)}, bf16[2,8,100,2,128]{4,3,2,1,0:T(2,128)(2,1)}, u32[]{:S(2)}) copy-start(bf16[2,8,100,2,128]{4,3,2,1,0:T(2,128)(2,1)} %param.9) | copy-start | bytes 2457604
  16.2 23.8 %collective-permute-start.3 = (f32[1400,128]{1,0:T(8,128)}, f32[1400,128]{1,0:T(8,128)S(1)}, u32[]{:S(2)}, u32[]{:S(2)}) collective-permute-start(f32[1400,128]{1,0:T(8,128)} %get-tuple-element.20.refs_0_), channel_id=1, source_target_pairs={{32,0},{64,32},{96,64},{128,96},{160,128},{192,160},{224,192},{256... | collective-permute-start | bytes 2150408 | tf_op jit(solution)/shard_map/ppermute | solution.py:363
  18.2 2.7 %copy-start.2 = (s32[8,2,128]{2,1,0:T(2,128)S(1)}, s32[8,2,128]{2,1,0:T(2,128)}, u32[]{:S(2)}) copy-start(s32[8,2,128]{2,1,0:T(2,128)} %refs_8_.7) | copy-start | bytes 24580
  18.2 2.7 %copy-start.3 = (f32[208,128]{1,0:T(8,128)S(1)}, f32[208,128]{1,0:T(8,128)}, u32[]{:S(2)}) copy-start(f32[208,128]{1,0:T(8,128)} %get-tuple-element.18.refs_0_) | copy-start | bytes 319492
  18.2 2.7 %copy-start.5 = (f32[2,128]{1,0:T(2,128)S(1)}, f32[2,128]{1,0:T(2,128)}, u32[]{:S(2)}) copy-start(f32[2,128]{1,0:T(2,128)} %refs_4_.7) | copy-start | bytes 3076
  18.2 2.7 %copy-start.6 = (f32[2,128]{1,0:T(2,128)S(1)}, f32[2,128]{1,0:T(2,128)}, u32[]{:S(2)}) copy-start(f32[2,128]{1,0:T(2,128)} %refs_5_.7) | copy-start | bytes 3076
  20.9 19.1 %copy-start.1 = (f32[1400,128]{1,0:T(8,128)S(1)}, f32[1400,128]{1,0:T(8,128)}, u32[]{:S(2)}) copy-start(f32[1400,128]{1,0:T(8,128)} %get-tuple-element.20.refs_0_) | copy-start | bytes 2150404
  22.7 22.4 %copy-start.4 = (f32[100,2,128]{2,1,0:T(2,128)S(1)}, f32[100,2,128]{2,1,0:T(2,128)}, u32[]{:S(2)}) copy-start(f32[100,2,128]{2,1,0:T(2,128)} %param.13) | copy-start | bytes 307204
  22.7 17.3 %collective-permute-start.4 = (f32[304,128]{1,0:T(8,128)S(1)}, f32[304,128]{1,0:T(8,128)S(1)}, u32[]{:S(2)}, u32[]{:S(2)}) collective-permute-start(f32[304,128]{1,0:T(8,128)S(1)} %window1_from0.1.refs_0_.refs_11_), channel_id=1, source_target_pairs={{32,0},{64,32},{96,64},{128,96},{160,128},{192,160},{224,192},{256... | collective-permute-start | bytes 466952 | tf_op jit(solution)/shard_map/ppermute | solution.py:363
  43.7 1.3 %copy-start.7 = (s32[2,128]{1,0:T(2,128)S(1)}, s32[2,128]{1,0:T(2,128)}, u32[]{:S(2)}) copy-start(s32[2,128]{1,0:T(2,128)} %refs_13_.1) | copy-start | bytes 3076
  43.8 30.3 %collective-permute-start.5 = (f32[1504,128]{1,0:T(8,128)S(1)}, f32[1504,128]{1,0:T(8,128)}, u32[]{:S(2)}, u32[]{:S(2)}) collective-permute-start(f32[1504,128]{1,0:T(8,128)S(1)} %window1_from1.1.refs_0_), channel_id=1, source_target_pairs={{32,0},{64,32},{96,64},{128,96},{160,128},{192,160},{224,192},{256... | collective-permute-start | bytes 2310152 | tf_op jit(solution)/shard_map/ppermute | solution.py:363
  48.5 43.0 %all-to-all-start = ((f32[512,1,128]{2,1,0:T(1,128)}), f32[512,1,128]{2,1,0:T(1,128)S(1)}, u32[]{:S(2)}, u32[]{:S(2)}) async-start(f32[512,1,128]{2,1,0:T(1,128)} %bitcast.5), calls=%async_computation | async-start | bytes 524288 | tf_op jit(solution)/shard_map/all_to_all | solution.py:434

commit v3 on v2

--- a/solution.py
+++ b/solution.py
@@ -10,6 +10,7 @@
 EXTRA = 8
 TAIL = 104
 WIDE = 4
+COST = ((10_000_000, 10_000_000), (40_000_000, 10_000_000))
 F32 = jnp.float32
 BF16 = jnp.bfloat16
 ANY = pl.BlockSpec(memory_space=pl.ANY)
@@ -35,7 +36,7 @@
     return jnp.broadcast_to(row, (8, row.shape[1]))
 
 
-def pack_kernel(adj, clon, clat, stiff, state_h, first, rest, west, state_s, sem, *, rows):
+def pack_kernel(adj, clon, clat, stiff, state_h, first, state_s, sem, *, rows):
     levels, _, width = adj.shape
     half = width // 2
     get = pltpu.make_async_copy(state_h.at[state_h.shape[0] - 1], state_s, sem)
@@ -46,8 +47,6 @@
         block = adj[lev].astype(F32)
         if lev == 0:
             first[0:rows] = block
-        else:
-            rest[(lev - 1) * rows : lev * rows] = block
         acc = place(acc, block, WIDE * lev)
         both = stiff[lev].astype(F32)
         grades = place(grades, tall(both[0:1]), WIDE * lev)
@@ -55,11 +54,15 @@
     get.wait()
     for lev in range(levels):
         acc = place(acc, state_s[lev].astype(F32), half + WIDE * lev)
-    west[0:rows] = acc
-    for out in (first, west):
-        out[rows : rows + 2] = clon[...]
-        out[rows + 2 : rows + 4] = clat[...]
-        out[rows + 4 : rows + 8] = grades[0:4]
+    first[rows : 2 * rows] = acc
+    first[2 * rows : 2 * rows + 2] = clon[...]
+    first[2 * rows + 2 : 2 * rows + 4] = clat[...]
+    first[2 * rows + 4 : 2 * rows + 8] = grades[0:4]
+
+
+def rest_kernel(adj, first, rest, *, rows):
+    for lev in range(1, adj.shape[0]):
+        rest[(lev - 1) * rows : lev * rows] = adj[lev].astype(F32)
 
 
 def pull(block, lane_from, lane_to, width):
@@ -111,15 +114,16 @@
     def edge(row):
         return pltpu.roll(tall(row), width - 1, 1)[0:1]
 
-    lon = [clon[0:1], clon[1:2], north_c[rows : rows + 1]]
-    lat = [clat[0:1], clat[1:2], north_c[rows + 2 : rows + 3]]
+    lon = [clon[0:1], clon[1:2], north_c[2 * rows : 2 * rows + 1]]
+    lat = [clat[0:1], clat[1:2], north_c[2 * rows + 2 : 2 * rows + 3]]
     lon += [edge(west_c[rows : rows + 1]), edge(west_c[rows + 1 : rows + 2])]
     lat += [edge(west_c[rows + 2 : rows + 3]), edge(west_c[rows + 3 : rows + 4])]
     return with_keep(lon, lat)
 
 
-def strip_kernel(west, diag, mats, out, *, rows):
-    spec, width = rows // 2, west.shape[1]
+def strip_kernel(both, mats, out, *, rows):
+    west, diag = both.at[0 : rows + EXTRA], both.at[rows + EXTRA : 2 * (rows + EXTRA)]
+    spec, width = rows // 2, both.shape[1]
     half = width // 2
     levels = mats.shape[1]
     at = lanes((spec, width))
@@ -197,7 +201,7 @@
         refs = refs[3:]
     if last and not grad:
         refs = refs[1:]
-    if not last:
+    if not last and first_level == 0:
         edge_r = refs.pop(0)
     if last:
         out_h = refs.pop(0)
@@ -218,9 +222,9 @@
     get_mats.start()
     cour = courant(clon, clat, north_c, west_c, rows)
     if last:
-        corner = north[count * rows : count * rows + spec]
+        corner = corner_r[rows : rows + spec]
     else:
-        corner = corner_r[pl.ds(0, spec, stride=2), :]
+        corner = corner_r[pl.ds(rows + EXTRA, spec, stride=2), :]
     west_v = west.at[0:rows]
     for lev in range(count):
         start = WIDE * (first_level + lev)
@@ -263,9 +267,9 @@
             else:
                 lam_out[pl.ds(lev * rows + r, spec, stride=2), :] = half
     if not last:
-        lam_out[count * rows : count * rows + spec] = edge_r[pl.ds(0, spec, stride=2), :]
-        pad = TAIL - spec
-        lam_out[count * rows + spec :] = jnp.zeros((pad, width), F32)
+        if first_level == 0:
+            lam_out[rows : rows + spec] = edge_r[pl.ds(0, spec, stride=2), :]
+            lam_out[rows + spec :] = jnp.zeros((TAIL - spec, width), F32)
         return
     out_s = refs.pop(0)
     for lev in range(count):
@@ -307,7 +311,7 @@
         before, emission, region, regions = extra
         args += [before, emission, region]
         specs += [VMEM] * 3
-    if not last:
+    if edge is not None:
         args.append(edge)
         specs.append(VMEM)
     if last:
@@ -323,7 +327,7 @@
             out_specs.append(VMEM)
     else:
         out_shape = [
-            jax.ShapeDtypeStruct((count * rows + TAIL, width), F32),
+            jax.ShapeDtypeStruct((count * rows + (0 if edge is None else TAIL), width), F32),
         ]
         out_specs = [VMEM]
     scratch = [
@@ -354,6 +358,7 @@
         scratch_shapes=scratch,
         input_output_aliases=aliases,
         name=f"window{window}_from{first_level}",
+        cost_estimate=pl.CostEstimate(flops=0, transcendentals=0, bytes_accessed=COST[window][first_level]),
         compiler_params=vmem(40 if count > 1 else 8),
     )(*args)
 
@@ -366,16 +371,6 @@
 def to_west(block):
     blocks = lax.axis_size("lon")
     return lax.ppermute(block, "lon", [((j + 1) % blocks, j) for j in range(blocks)])
-
-
-def to_northwest(block):
-    bands, blocks = lax.axis_size("lat"), lax.axis_size("lon")
-    route = [
-        ((i + 1) * blocks + (j + 1) % blocks, i * blocks + j)
-        for i in range(bands - 1)
-        for j in range(blocks)
-    ]
-    return lax.ppermute(block, ("lat", "lon"), route)
 
 
 def per_device(
@@ -388,52 +383,54 @@
     flat_state = state.reshape(windows, levels, rows, width)
     flat_em = emission.reshape(rows, width)
     mats = jnp.swapaxes(inverses, 2, 3)
-    low1, rest1, west1 = pl.pallas_call(
+    low1 = pl.pallas_call(
         functools.partial(pack_kernel, rows=rows),
-        out_shape=[
-            jax.ShapeDtypeStruct((rows + EXTRA, width), F32),
-            jax.ShapeDtypeStruct(((levels - 1) * rows, width), F32),
-            jax.ShapeDtypeStruct((rows + EXTRA, width), F32),
-        ],
+        out_shape=jax.ShapeDtypeStruct((2 * rows + EXTRA, width), F32),
         in_specs=[VMEM] * 4 + [HBM],
-        out_specs=[VMEM] * 3,
+        out_specs=VMEM,
         scratch_shapes=[pltpu.VMEM((levels, rows, width), BF16), pltpu.SemaphoreType.DMA],
         name="pack",
         compiler_params=vmem(56),
     )(adj, courant_lon, courant_lat, stiffness, flat_state)
     low1_n = to_north(low1)
-    west1_w = to_west(west1)
-    west1_d = to_northwest(west1)
-    rest1, low1_n, west1_w, west1_d = lax.optimization_barrier(
-        (rest1, low1_n, west1_w, west1_d)
-    )
+    rest1 = pl.pallas_call(
+        functools.partial(rest_kernel, rows=rows),
+        out_shape=jax.ShapeDtypeStruct(((levels - 1) * rows, width), F32),
+        in_specs=[VMEM, ANY],
+        out_specs=VMEM,
+        name="rest",
+        compiler_params=vmem(56),
+    )(adj, low1)
+    rest1, low1_n = lax.optimization_barrier((rest1, low1_n))
     rest1_n = to_north(rest1)
+    west1_w = to_west(jnp.concatenate([low1[rows:], low1_n[rows:]], axis=0))
     shared = (courant_lon, courant_lat, low1_n, west1_w, stiffness, flat_state, mats)
     strip = pl.pallas_call(
         functools.partial(strip_kernel, rows=rows),
         out_shape=jax.ShapeDtypeStruct((rows, width), F32),
-        in_specs=[VMEM] * 3,
+        in_specs=[VMEM] * 2,
         out_specs=VMEM,
         name="strip",
+        cost_estimate=pl.CostEstimate(flops=0, transcendentals=0, bytes_accessed=40_000_000),
         compiler_params=vmem(8),
-    )(west1_w, west1_d, mats)
+    )(west1_w, mats)
     low0 = run_window(
-        low1, low1_n, west1_w, west1_d, shared, 1, 0, 1, False, edge=strip
+        low1, low1_n, west1_w, west1_w, shared, 1, 0, 1, False, edge=strip
     )[0]
     low0_n = to_north(low0)
     rest1_n, low0_n = lax.optimization_barrier((rest1_n, low0_n))
     rest0 = run_window(
-        rest1, rest1_n, west1_w, west1_d, shared, 1, 1, levels - 1, False, edge=strip
+        rest1, rest1_n, west1_w, west1_w, shared, 1, 1, levels - 1, False
     )[0]
     rest0_n = to_north(rest0)
     low0_n, rest0 = lax.optimization_barrier((low0_n, rest0))
     low_extra = (low0, flat_em, region_id, regions)
     out, partial = run_window(
-        low0, low0_n, strip, strip, shared, 0, 0, 1, True, extra=low_extra
+        low0, low0_n, strip, low0_n, shared, 0, 0, 1, True, extra=low_extra
     )
     spread = lax.all_to_all(partial, ("lat", "lon"), 0, 0, tiled=True)
     out = run_window(
-        rest0, rest0_n, strip, strip, shared, 0, 1, levels - 1, True, prior=out
+        rest0, rest0_n, strip, low0_n, shared, 0, 1, levels - 1, True, prior=out
     )[0]
     out, spread = lax.optimization_barrier((out, spread))
     grad = pl.pallas_call(

time: 92.4 us -> 92.5 us (level)
  waiting for transfers between devices: 28.8 us -> 22.9 us
  starting transfers between devices: 41.1 us -> 44.1 us
  Pallas kernels: 20.7 us -> 23.5 us
    ppermute x4, waiting for transfers between devices: 15.9 us -> 10.5 us  [to_north(): return lax.ppermute(block, 'lat', [(i + 1, i) for i in range(bands - 1)])]
    all_to_all x1, starting transfers between devices: 25.6 us -> 29.2 us  [per_device(): spread = lax.all_to_all(partial, ('lat', 'lon'), 0, 0, tiled=True)]
    pallas_call x1 -> x2, Pallas kernels: 3.05 us -> 4.82 us  [the longest x1 2.9 us: per_device(): pl.pallas_call(functools.partial(pack_kernel, rows=rows), out_shape=jax.S...]
    ppermute x1 -> x0, starting transfers between devices: 1.29 us -> none  [to_northwest(): return lax.ppermute(block, ('lat', 'lon'), route)]
    pallas_call x4, Pallas kernels: 14.4 us -> 15.4 us  [run_window(): pl.pallas_call(body, out_shape=out_shape, in_specs=specs, out_specs=out_s...]
  transfers between devices with their start and end apart: 7 -> 6, of which waited for: 3 -> 4; matrix products, arithmetic and copies ran while one was open for 1% -> 1% of each run, Pallas kernels for 14% -> 17%
where the time goes in v3:
time: 92.5 us; the launch traced here: 92 us
  starting transfers between devices  44.1 us (48%)
  Pallas kernels  23.5 us (25%)
  waiting for transfers between devices  22.9 us (25%)
    all_to_all x1, starting transfers between devices, per_device(): spread = lax.all_to_all(partial, ('lat', 'lon'), 0, 0, tiled=True)  29.2 us
    pallas_call x4, Pallas kernels, run_window(): pl.pallas_call(body, out_shape=out_shape, in_specs=specs, out_specs=out_s...  15.4 us
    all_to_all x1, waiting for transfers between devices, per_device(): spread = lax.all_to_all(partial, ('lat', 'lon'), 0, 0, tiled=True)  11.8 us
    ppermute x4, waiting for transfers between devices, to_north(): return lax.ppermute(block, 'lat', [(i + 1, i) for i in range(bands - 1)])  10.5 us
    ppermute x1, starting transfers between devices, to_west(): lax.ppermute(block, 'lon', [((j + 1) % blocks, j) for j in range(blocks)])  9.48 us
    ppermute x4, starting transfers between devices, to_north(): return lax.ppermute(block, 'lat', [(i + 1, i) for i in range(bands - 1)])  5.42 us
    pallas_call x1, Pallas kernels, per_device(): pl.pallas_call(functools.partial(pack_kernel, rows=rows), out_shape=jax.S...  2.9 us
    pallas_call x1, Pallas kernels, per_device(): pl.pallas_call(functools.partial(strip_kernel, rows=rows), out_shape=jax....  2.66 us
  transfers between devices with their start and end apart: 6, of which 4 were waited for; matrix products, arithmetic and copies ran while one was open for 1% of the time, Pallas kernels for 17%

profile of v3, /device:TPU:1, one launch (start us, length us, event | category | flops | bytes accessed | tf_op | source)
XLA Modules:
  0.0 92.0 jit_solution(11369846438497075099)
XLA Ops:
  0.6 2.9 %pack.1.first.refs_0_ = f32[408,128]{1,0:T(8,128)} custom-call(bf16[8,200,128]{2,1,0:T(8,128)(2,1)} %bitcast.22, f32[2,128]{1,0:T(2,128)} %refs_4_.7, f32[2,128]{1,0:T(2,128)} %refs_5_.7, s32[8,2,128]{2,1,0:T(2,128)} %refs_8_.7, bf16[2,8,200,128]{3,2,1,0:T(8,128)(2,1)} %bitcast.15), custom_call_target="tpu_custom_call" | custom-call | tf_op jit(solution)/shard_map/pack/pallas_call | solution.py:386
  3.5 0.0 copy-start.2
  3.5 1.4 %collective-permute-start = (f32[408,128]{1,0:T(8,128)}, f32[408,128]{1,0:T(8,128)S(1)}, u32[]{:S(2)}, u32[]{:S(2)}) collective-permute-start(f32[408,128]{1,0:T(8,128)} %pack.1.first.refs_0_), channel_id=1, source_target_pairs={{32,0},{64,32},{96,64},{128,96},{160,128},{192,160},{224,192},{256... | collective-permute-start | bytes 626696 | tf_op jit(solution)/shard_map/ppermute | solution.py:368
  5.0 1.9 %rest.1.refs_0_ = f32[1400,128]{1,0:T(8,128)} custom-call(bf16[8,200,128]{2,1,0:T(8,128)(2,1)} %bitcast.23, f32[408,128]{1,0:T(8,128)} %pack.1.first.refs_0_), custom_call_target="tpu_custom_call" | custom-call | tf_op jit(solution)/shard_map/rest/pallas_call | solution.py:396
  6.9 4.1 %collective-permute-done.refs_1_.refs_6_ = f32[408,128]{1,0:T(8,128)S(1)} collective-permute-done((f32[408,128]{1,0:T(8,128)}, f32[408,128]{1,0:T(8,128)S(1)}, u32[]{:S(2)}, u32[]{:S(2)}) %collective-permute-start) | collective-permute-done | bytes 208928 | tf_op jit(solution)/shard_map/ppermute | solution.py:368
  11.0 1.3 %collective-permute-start.1 = (f32[1400,128]{1,0:T(8,128)}, f32[1400,128]{1,0:T(8,128)}, u32[]{:S(2)}, u32[]{:S(2)}) collective-permute-start(f32[1400,128]{1,0:T(8,128)} %rest.1.refs_0_), channel_id=1, source_target_pairs={{32,0},{64,32},{96,64},{128,96},{160,128},{192,160},{224,192},{256... | collective-permute-start | bytes 2150408 | tf_op jit(solution)/shard_map/ppermute | solution.py:368
  12.3 0.0 copy-done.2
  12.4 0.0 copy-start
  12.4 9.5 %collective-permute-start.2 = (f32[416,128]{1,0:T(8,128)S(1)}, f32[416,128]{1,0:T(8,128)S(1)}, u32[]{:S(2)}, u32[]{:S(2)}) collective-permute-start(f32[416,128]{1,0:T(8,128)S(1)} %pad_maximum_fusion), channel_id=1, source_target_pairs={{1,0},{2,1},{3,2},{4,3},{5,4},{6,5},{7,6},{8,7},{9,8},{10,9},{11,1... | collective-permute-start | bytes 638984 | tf_op jit(solution)/shard_map/ppermute | solution.py:373
  21.9 0.0 copy-done.8
  21.9 0.5 copy.12
  22.4 0.7 collective-permute-done.2.both.refs_2_.refs_3_.refs_7_
  23.1 2.7 %strip.1.refs_11_.refs_2_ = f32[200,128]{1,0:T(8,128)S(1)} custom-call(f32[416,128]{1,0:T(8,128)S(1)} %collective-permute-done.2.both.refs_2_.refs_3_.refs_7_, bf16[3,8,100,100]{3,2,1,0:T(8,128)(2,1)S(1)} %bitcast.10), custom_call_target="tpu_custom_call" | custom-call | bytes 40000000 | tf_op jit(solution)/shard_map/strip/pallas_call | solution.py:408
  25.8 0.0 copy-done
  25.8 0.0 copy-done.3
  25.8 0.0 copy-done.5
  25.8 1.7 %window1_from0.1.refs_0_.refs_11_ = f32[304,128]{1,0:T(8,128)S(1)} custom-call(f32[408,128]{1,0:T(8,128)S(1)} %copy-done.2, f32[408,128]{1,0:T(8,128)S(1)} %collective-permute-done.refs_1_.refs_6_, f32[416,128]{1,0:T(8,128)S(1)} %collective-permute-done.2.both.refs_2_.refs_3_.refs_7_, f32[416,128]{1,0:T(8,128)S(1)} %collective-permute-done.2.both.refs_2_.refs_3_.refs_7_, ...), custom_call_target="tpu_custom_call" | custom-call | bytes 40000000 | tf_op jit(solution)/shard_map/window1_from0/pallas_call | solution.py:353
  27.6 0.0 copy-start.4
  27.6 1.4 %collective-permute-start.3 = (f32[304,128]{1,0:T(8,128)S(1)}, f32[304,128]{1,0:T(8,128)S(1)}, u32[]{:S(2)}, u32[]{:S(2)}) collective-permute-start(f32[304,128]{1,0:T(8,128)S(1)} %window1_from0.1.refs_0_.refs_11_), channel_id=1, source_target_pairs={{32,0},{64,32},{96,64},{128,96},{160,128},{192,160},{224,192},{256... | collective-permute-start | bytes 466952 | tf_op jit(solution)/shard_map/ppermute | solution.py:368
  29.0 6.4 %collective-permute-done.3.refs_1_.refs_3_ = f32[304,128]{1,0:T(8,128)S(1)} collective-permute-done((f32[304,128]{1,0:T(8,128)S(1)}, f32[304,128]{1,0:T(8,128)S(1)}, u32[]{:S(2)}, u32[]{:S(2)}) %collective-permute-start.3) | collective-permute-done | bytes 155680 | tf_op jit(solution)/shard_map/ppermute | solution.py:368
  35.4 0.0 collective-permute-done.1.refs_1_
  35.4 4.8 %window1_from1.1.refs_0_ = f32[1400,128]{1,0:T(8,128)S(1)} custom-call(f32[1400,128]{1,0:T(8,128)S(1)} %copy-done.1, f32[1400,128]{1,0:T(8,128)} %collective-permute-done.1.refs_1_, f32[416,128]{1,0:T(8,128)S(1)} %collective-permute-done.2.both.refs_2_.refs_3_.refs_7_, f32[416,128]{1,0:T(8,128)S(1)} %collective-permute-done.2.both.refs_2_.refs_3_.refs_7_, ...), custom_call_target="tpu_custom_call" | custom-call | bytes 10000000 | tf_op jit(solution)/shard_map/window1_from1/pallas_call | solution.py:353
  40.2 0.0 copy-start.7
  40.2 1.3 %collective-permute-start.4 = (f32[1400,128]{1,0:T(8,128)S(1)}, f32[1400,128]{1,0:T(8,128)}, u32[]{:S(2)}, u32[]{:S(2)}) collective-permute-start(f32[1400,128]{1,0:T(8,128)S(1)} %window1_from1.1.refs_0_), channel_id=1, source_target_pairs={{32,0},{64,32},{96,64},{128,96},{160,128},{192,160},{224,192},{256... | collective-permute-start | bytes 2150408 | tf_op jit(solution)/shard_map/ppermute | solution.py:368
  41.5 0.0 copy-done.4
  41.5 0.0 copy-done.7
  41.5 3.4 %window0_from0.1 = (bf16[8,200,128]{2,1,0:T(8,128)(2,1)}, f32[512,128]{1,0:T(8,128)}) custom-call(f32[304,128]{1,0:T(8,128)S(1)} %window1_from0.1.refs_0_.refs_11_, f32[304,128]{1,0:T(8,128)S(1)} %collective-permute-done.3.refs_1_.refs_3_, f32[200,128]{1,0:T(8,128)S(1)} %strip.1.refs_11_.refs_2_, f32[304,128]{1,0:T(8,128)S(1)} %collective-permute-done.3.refs_1_.refs_3_, ...), custom_call_target="tpu_custom_call" | custom-call | bytes 10000000 | tf_op jit(solution)/shard_map/window0_from0/pallas_call | solution.py:353
  44.9 29.2 %all-to-all-start = ((f32[512,1,128]{2,1,0:T(1,128)}), f32[512,1,128]{2,1,0:T(1,128)S(1)}, u32[]{:S(2)}, u32[]{:S(2)}) async-start(f32[512,1,128]{2,1,0:T(1,128)} %bitcast.5), calls=%async_computation | async-start | bytes 524288 | tf_op jit(solution)/shard_map/all_to_all | solution.py:431
  74.1 0.0 collective-permute-done.4.refs_1_
  74.1 5.6 %window0_from1.1 = bf16[8,200,128]{2,1,0:T(8,128)(2,1)} custom-call(f32[1400,128]{1,0:T(8,128)S(1)} %window1_from1.1.refs_0_, f32[1400,128]{1,0:T(8,128)} %collective-permute-done.4.refs_1_, f32[200,128]{1,0:T(8,128)S(1)} %strip.1.refs_11_.refs_2_, f32[304,128]{1,0:T(8,128)S(1)} %collective-permute-done.3.refs_1_.refs_3_, ...), custom_call_target="tpu_custom_call", output_to_operand_aliasing={{}: (11, {})} | custom-call | bytes 10000000 | tf_op jit(solution)/shard_map/window0_from1/pallas_call | solution.py:353
  79.6 11.8 %all-to-all-done = f32[512,1,128]{2,1,0:T(1,128)S(1)} async-done(((f32[512,1,128]{2,1,0:T(1,128)}), f32[512,1,128]{2,1,0:T(1,128)S(1)}, u32[]{:S(2)}, u32[]{:S(2)}) %all-to-all-start) | async-done | bytes 262176 | tf_op jit(solution)/shard_map/all_to_all | solution.py:431
  91.4 0.6 gather_sum.1
  (10 shorter events, 0.0 us)
Async XLA Ops:
  3.5 8.8 %copy-start.2 = (f32[408,128]{1,0:T(8,128)S(1)}, f32[408,128]{1,0:T(8,128)}, u32[]{:S(2)}) copy-start(f32[408,128]{1,0:T(8,128)} %pack.1.first.refs_0_) | copy-start | bytes 626692
  3.5 7.5 %collective-permute-start = (f32[408,128]{1,0:T(8,128)}, f32[408,128]{1,0:T(8,128)S(1)}, u32[]{:S(2)}, u32[]{:S(2)}) collective-permute-start(f32[408,128]{1,0:T(8,128)} %pack.1.first.refs_0_), channel_id=1, source_target_pairs={{32,0},{64,32},{96,64},{128,96},{160,128},{192,160},{224,192},{256... | collective-permute-start | bytes 626696 | tf_op jit(solution)/shard_map/ppermute | solution.py:368
  6.9 15.0 %copy-start.8 = (bf16[3,8,100,100]{3,1,2,0:T(8,128)(2,1)S(1)}, bf16[3,8,100,100]{3,1,2,0:T(8,128)(2,1)}, u32[]{:S(2)}) copy-start(bf16[3,8,100,100]{3,1,2,0:T(8,128)(2,1)} %param.10) | copy-start | bytes 1440004
  11.0 24.3 %collective-permute-start.1 = (f32[1400,128]{1,0:T(8,128)}, f32[1400,128]{1,0:T(8,128)}, u32[]{:S(2)}, u32[]{:S(2)}) collective-permute-start(f32[1400,128]{1,0:T(8,128)} %rest.1.refs_0_), channel_id=1, source_target_pairs={{32,0},{64,32},{96,64},{128,96},{160,128},{192,160},{224,192},{256... | collective-permute-start | bytes 2150408 | tf_op jit(solution)/shard_map/ppermute | solution.py:368
  12.4 13.4 %copy-start = (bf16[2,8,100,2,128]{4,3,2,1,0:T(2,128)(2,1)S(1)}, bf16[2,8,100,2,128]{4,3,2,1,0:T(2,128)(2,1)}, u32[]{:S(2)}) copy-start(bf16[2,8,100,2,128]{4,3,2,1,0:T(2,128)(2,1)} %param.9) | copy-start | bytes 2457604
  12.4 10.7 %collective-permute-start.2 = (f32[416,128]{1,0:T(8,128)S(1)}, f32[416,128]{1,0:T(8,128)S(1)}, u32[]{:S(2)}, u32[]{:S(2)}) collective-permute-start(f32[416,128]{1,0:T(8,128)S(1)} %pad_maximum_fusion), channel_id=1, source_target_pairs={{1,0},{2,1},{3,2},{4,3},{5,4},{6,5},{7,6},{8,7},{9,8},{10,9},{11,1... | collective-permute-start | bytes 638984 | tf_op jit(solution)/shard_map/ppermute | solution.py:373
  23.1 2.7 %copy-start.3 = (s32[8,2,128]{2,1,0:T(2,128)S(1)}, s32[8,2,128]{2,1,0:T(2,128)}, u32[]{:S(2)}) copy-start(s32[8,2,128]{2,1,0:T(2,128)} %refs_8_.7) | copy-start | bytes 24580
  23.1 2.7 %copy-start.5 = (f32[2,128]{1,0:T(2,128)S(1)}, f32[2,128]{1,0:T(2,128)}, u32[]{:S(2)}) copy-start(f32[2,128]{1,0:T(2,128)} %refs_4_.7) | copy-start | bytes 3076
  23.1 2.7 %copy-start.6 = (f32[2,128]{1,0:T(2,128)S(1)}, f32[2,128]{1,0:T(2,128)}, u32[]{:S(2)}) copy-start(f32[2,128]{1,0:T(2,128)} %refs_5_.7) | copy-start | bytes 3076
  25.8 9.6 %copy-start.1 = (f32[1400,128]{1,0:T(8,128)S(1)}, f32[1400,128]{1,0:T(8,128)}, u32[]{:S(2)}) copy-start(f32[1400,128]{1,0:T(8,128)} %rest.1.refs_0_) | copy-start | bytes 2150404
  27.6 13.9 %copy-start.4 = (f32[100,2,128]{2,1,0:T(2,128)S(1)}, f32[100,2,128]{2,1,0:T(2,128)}, u32[]{:S(2)}) copy-start(f32[100,2,128]{2,1,0:T(2,128)} %param.13) | copy-start | bytes 307204
  27.6 7.8 %collective-permute-start.3 = (f32[304,128]{1,0:T(8,128)S(1)}, f32[304,128]{1,0:T(8,128)S(1)}, u32[]{:S(2)}, u32[]{:S(2)}) collective-permute-start(f32[304,128]{1,0:T(8,128)S(1)} %window1_from0.1.refs_0_.refs_11_), channel_id=1, source_target_pairs={{32,0},{64,32},{96,64},{128,96},{160,128},{192,160},{224,192},{256... | collective-permute-start | bytes 466952 | tf_op jit(solution)/shard_map/ppermute | solution.py:368
  40.2 1.3 %copy-start.7 = (s32[2,128]{1,0:T(2,128)S(1)}, s32[2,128]{1,0:T(2,128)}, u32[]{:S(2)}) copy-start(s32[2,128]{1,0:T(2,128)} %refs_13_.1) | copy-start | bytes 3076
  40.2 33.9 %collective-permute-start.4 = (f32[1400,128]{1,0:T(8,128)S(1)}, f32[1400,128]{1,0:T(8,128)}, u32[]{:S(2)}, u32[]{:S(2)}) collective-permute-start(f32[1400,128]{1,0:T(8,128)S(1)} %window1_from1.1.refs_0_), channel_id=1, source_target_pairs={{32,0},{64,32},{96,64},{128,96},{160,128},{192,160},{224,192},{256... | collective-permute-start | bytes 2150408 | tf_op jit(solution)/shard_map/ppermute | solution.py:368
  44.9 46.5 %all-to-all-start = ((f32[512,1,128]{2,1,0:T(1,128)}), f32[512,1,128]{2,1,0:T(1,128)S(1)}, u32[]{:S(2)}, u32[]{:S(2)}) async-start(f32[512,1,128]{2,1,0:T(1,128)} %bitcast.5), calls=%async_computation | async-start | bytes 524288 | tf_op jit(solution)/shard_map/all_to_all | solution.py:431

commit v4 on v3

--- a/solution.py
+++ b/solution.py
@@ -34,6 +34,10 @@
 
 def tall(row):
     return jnp.broadcast_to(row, (8, row.shape[1]))
+
+
+def folded_rows(rows):
+    return -(-rows // 16) * 8
 
 
 def pack_kernel(adj, clon, clat, stiff, state_h, first, state_s, sem, *, rows):
@@ -53,11 +57,14 @@
         grades = place(grades, tall(both[1:2]), half + WIDE * lev)
     get.wait()
     for lev in range(levels):
-        acc = place(acc, state_s[lev].astype(F32), half + WIDE * lev)
-    first[rows : 2 * rows] = acc
-    first[2 * rows : 2 * rows + 2] = clon[...]
-    first[2 * rows + 2 : 2 * rows + 4] = clat[...]
-    first[2 * rows + 4 : 2 * rows + 8] = grades[0:4]
+        acc = place(acc, state_s[lev].astype(F32), half // 2 + WIDE * lev)
+    folded = folded_rows(rows)
+    upper = jnp.concatenate([acc[folded:], jnp.zeros((2 * folded - rows, width), F32)], axis=0)
+    first[rows : rows + folded] = acc[0:folded] + pltpu.roll(upper, half, 1)
+    at = rows + folded
+    first[at : at + 2] = clon[...]
+    first[at + 2 : at + 4] = clat[...]
+    first[at + 4 : at + 8] = grades[0:4]
 
 
 def rest_kernel(adj, first, rest, *, rows):
@@ -114,14 +121,22 @@
     def edge(row):
         return pltpu.roll(tall(row), width - 1, 1)[0:1]
 
-    lon = [clon[0:1], clon[1:2], north_c[2 * rows : 2 * rows + 1]]
-    lat = [clat[0:1], clat[1:2], north_c[2 * rows + 2 : 2 * rows + 3]]
+    at = rows + folded_rows(rows)
+    lon = [clon[0:1], clon[1:2], north_c[at : at + 1]]
+    lat = [clat[0:1], clat[1:2], north_c[at + 2 : at + 3]]
     lon += [edge(west_c[rows : rows + 1]), edge(west_c[rows + 1 : rows + 2])]
     lat += [edge(west_c[rows + 2 : rows + 3]), edge(west_c[rows + 3 : rows + 4])]
     return with_keep(lon, lat)
 
 
-def strip_kernel(both, mats, out, *, rows):
+def strip_kernel(packed, mats, out, both, *, rows):
+    folded = folded_rows(rows)
+    for i in range(2):
+        src, dst = i * (folded + EXTRA), i * (rows + EXTRA)
+        block = packed[src : src + folded]
+        both[dst : dst + folded] = block
+        both[dst + folded : dst + rows] = pltpu.roll(block, block.shape[1] // 2, 1)[0 : rows - folded]
+        both[dst + rows : dst + rows + EXTRA] = packed[src + folded : src + folded + EXTRA]
     west, diag = both.at[0 : rows + EXTRA], both.at[rows + EXTRA : 2 * (rows + EXTRA)]
     spec, width = rows // 2, both.shape[1]
     half = width // 2
@@ -153,7 +168,8 @@
     b0 = mixed(cour, 0, a0, a1, right(a0))
     b1 = mixed(cour, 1, a1, a2, right(a1))
     value = jnp.where(at < half, b0, pltpu.roll(b1, half, 1))
-    factor = jnp.where(at < half, pltpu.roll(w0, half, 1), w1)
+    quarter = half // 2
+    factor = jnp.where(at < half, pltpu.roll(w0, width - quarter, 1), pltpu.roll(w1, quarter, 1))
     live = west[rows + 4 : rows + 5]
     group = (at & (half - 1)) // WIDE
 
@@ -206,7 +222,7 @@
     if last:
         out_h = refs.pop(0)
         if grad:
-            partial = refs.pop(0)
+            mine, theirs = refs.pop(0), refs.pop(0)
     else:
         lam_out = refs.pop(0)
     x_s, y_s, flat_s, state_s, mats_s, sems = refs[:6]
@@ -292,7 +308,8 @@
             result = result + lax.dot_general(
                 onehot, piece, (((1,), (1,)), ((), ())), preferred_element_type=F32
             )
-        partial[...] = result
+        mine[...] = result[0 : regions // 2]
+        theirs[...] = result[regions // 2 :]
     put.wait()
 
 
@@ -323,8 +340,8 @@
         out_shape = [jax.ShapeDtypeStruct((levels, rows, width), BF16)]
         out_specs = [ANY]
         if grad:
-            out_shape.append(jax.ShapeDtypeStruct((regions, width), F32))
-            out_specs.append(VMEM)
+            out_shape += [jax.ShapeDtypeStruct((regions // 2, width), F32)] * 2
+            out_specs += [VMEM] * 2
     else:
         out_shape = [
             jax.ShapeDtypeStruct((count * rows + (0 if edge is None else TAIL), width), F32),
@@ -385,7 +402,7 @@
     mats = jnp.swapaxes(inverses, 2, 3)
     low1 = pl.pallas_call(
         functools.partial(pack_kernel, rows=rows),
-        out_shape=jax.ShapeDtypeStruct((2 * rows + EXTRA, width), F32),
+        out_shape=jax.ShapeDtypeStruct((rows + folded_rows(rows) + EXTRA, width), F32),
         in_specs=[VMEM] * 4 + [HBM],
         out_specs=VMEM,
         scratch_shapes=[pltpu.VMEM((levels, rows, width), BF16), pltpu.SemaphoreType.DMA],
@@ -404,31 +421,41 @@
     rest1, low1_n = lax.optimization_barrier((rest1, low1_n))
     rest1_n = to_north(rest1)
     west1_w = to_west(jnp.concatenate([low1[rows:], low1_n[rows:]], axis=0))
-    shared = (courant_lon, courant_lat, low1_n, west1_w, stiffness, flat_state, mats)
-    strip = pl.pallas_call(
+    strip, both = pl.pallas_call(
         functools.partial(strip_kernel, rows=rows),
-        out_shape=jax.ShapeDtypeStruct((rows, width), F32),
+        out_shape=[
+            jax.ShapeDtypeStruct((rows, width), F32),
+            jax.ShapeDtypeStruct((2 * (rows + EXTRA), width), F32),
+        ],
         in_specs=[VMEM] * 2,
-        out_specs=VMEM,
+        out_specs=[VMEM] * 2,
         name="strip",
         cost_estimate=pl.CostEstimate(flops=0, transcendentals=0, bytes_accessed=40_000_000),
         compiler_params=vmem(8),
     )(west1_w, mats)
+    shared = (courant_lon, courant_lat, low1_n, both, stiffness, flat_state, mats)
     low0 = run_window(
-        low1, low1_n, west1_w, west1_w, shared, 1, 0, 1, False, edge=strip
+        low1, low1_n, both, both, shared, 1, 0, 1, False, edge=strip
     )[0]
     low0_n = to_north(low0)
-    rest1_n, low0_n = lax.optimization_barrier((rest1_n, low0_n))
+    rest1_n, low0 = lax.optimization_barrier((rest1_n, low0))
     rest0 = run_window(
-        rest1, rest1_n, west1_w, west1_w, shared, 1, 1, levels - 1, False
+        rest1, rest1_n, both, both, shared, 1, 1, levels - 1, False
     )[0]
+    low0_n, rest0 = lax.optimization_barrier((low0_n, rest0))
     rest0_n = to_north(rest0)
-    low0_n, rest0 = lax.optimization_barrier((low0_n, rest0))
-    low_extra = (low0, flat_em, region_id, regions)
-    out, partial = run_window(
+    parity = lax.axis_index("lon") % 2
+    slot = region_id // 2 + jnp.where(region_id % 2 == parity, 0, regions // 2)
+    low_extra = (low0, flat_em, slot, regions)
+    out, mine, theirs = run_window(
         low0, low0_n, strip, low0_n, shared, 0, 0, 1, True, extra=low_extra
     )
-    spread = lax.all_to_all(partial, ("lat", "lon"), 0, 0, tiled=True)
+    pairs = [(k ^ 1, k) for k in range(regions)]
+    mine = mine + lax.ppermute(theirs, ("lat", "lon"), pairs)
+    groups = [list(range(k, regions, 2)) for k in range(2)]
+    spread = lax.all_to_all(
+        mine, ("lat", "lon"), 0, 0, axis_index_groups=groups, tiled=True
+    )
     out = run_window(
         rest0, rest0_n, strip, low0_n, shared, 0, 1, levels - 1, True, prior=out
     )[0]

time: 92.5 us -> 89.2 us (0.964)
  waiting for transfers between devices: 22.9 us -> 13.3 us
  starting transfers between devices: 44.1 us -> 49 us
  local copies, waits for them, and re-layouts: 0.58 us -> 1.89 us
    ppermute x0 -> x1, starting transfers between devices: none -> 9.13 us  [per_device(): mine = mine + lax.ppermute(theirs, ('lat', 'lon'), pairs)]
    ppermute x4, waiting for transfers between devices: 10.5 us -> 4.35 us  [to_north(): return lax.ppermute(block, 'lat', [(i + 1, i) for i in range(bands - 1)])]
    all_to_all x1, starting transfers between devices: 29.2 us -> 24.5 us  [per_device(): lax.all_to_all(mine, ('lat', 'lon'), 0, 0, axis_index_groups=groups, tile...]
    all_to_all x1, waiting for transfers between devices: 11.8 us -> 7.62 us  [per_device(): lax.all_to_all(mine, ('lat', 'lon'), 0, 0, axis_index_groups=groups, tile...]
    unnamed x19, local copies, waits for them, and re-layouts: 0.56 us -> 1.88 us
    ppermute x0 -> x1, waiting for transfers between devices: none -> 0.96 us  [per_device(): mine = mine + lax.ppermute(theirs, ('lat', 'lon'), pairs)]
  transfers between devices with their start and end apart: 6 -> 7, of which waited for: 4 -> 5; matrix products, arithmetic and copies ran while one was open for 1% -> 1% of each run, Pallas kernels for 17% -> 22%
where the time goes in v4:
time: 89.2 us; the launch traced here: 88.7 us
  starting transfers between devices  49 us (55%)
  Pallas kernels  22.9 us (26%)
  waiting for transfers between devices  13.3 us (15%)
  local copies, waits for them, and re-layouts  1.89 us (2%)
    all_to_all x1, starting transfers between devices, per_device(): lax.all_to_all(mine, ('lat', 'lon'), 0, 0, axis_index_groups=groups, tile...  24.5 us
    pallas_call x4, Pallas kernels, run_window(): pl.pallas_call(body, out_shape=out_shape, in_specs=specs, out_specs=out_s...  14.7 us
    ppermute x1, starting transfers between devices, to_west(): lax.ppermute(block, 'lon', [((j + 1) % blocks, j) for j in range(blocks)])  9.94 us
    ppermute x1, starting transfers between devices, per_device(): mine = mine + lax.ppermute(theirs, ('lat', 'lon'), pairs)  9.13 us
    all_to_all x1, waiting for transfers between devices, per_device(): lax.all_to_all(mine, ('lat', 'lon'), 0, 0, axis_index_groups=groups, tile...  7.62 us
    ppermute x4, starting transfers between devices, to_north(): return lax.ppermute(block, 'lat', [(i + 1, i) for i in range(bands - 1)])  5.41 us
    ppermute x4, waiting for transfers between devices, to_north(): return lax.ppermute(block, 'lat', [(i + 1, i) for i in range(bands - 1)])  4.35 us
    pallas_call x1, Pallas kernels, per_device(): pl.pallas_call(functools.partial(pack_kernel, rows=rows), out_shape=jax.S...  2.94 us
  transfers between devices with their start and end apart: 7, of which 5 were waited for; matrix products, arithmetic and copies ran while one was open for 1% of the time, Pallas kernels for 22%

profile of v4, /device:TPU:1, one launch (start us, length us, event | category | flops | bytes accessed | tf_op | source)
XLA Modules:
  0.0 88.7 jit_solution(2662076788965336488)
XLA Ops:
  0.6 2.9 %pack.1.first.refs_0_ = f32[312,128]{1,0:T(8,128)} custom-call(bf16[8,200,128]{2,1,0:T(8,128)(2,1)} %bitcast.22, f32[2,128]{1,0:T(2,128)} %refs_4_.7, f32[2,128]{1,0:T(2,128)} %refs_5_.7, s32[8,2,128]{2,1,0:T(2,128)} %refs_8_.7, bf16[2,8,200,128]{3,2,1,0:T(8,128)(2,1)} %bitcast.15), custom_call_target="tpu_custom_call" | custom-call | tf_op jit(solution)/shard_map/pack/pallas_call | solution.py:403
  3.6 0.0 copy-start.2
  3.6 0.0 copy-start.7
  3.6 1.4 %collective-permute-start = (f32[312,128]{1,0:T(8,128)}, f32[312,128]{1,0:T(8,128)S(1)}, u32[]{:S(2)}, u32[]{:S(2)}) collective-permute-start(f32[312,128]{1,0:T(8,128)} %pack.1.first.refs_0_), channel_id=1, source_target_pairs={{32,0},{64,32},{96,64},{128,96},{160,128},{192,160},{224,192},{256... | collective-permute-start | bytes 479240 | tf_op jit(solution)/shard_map/ppermute | solution.py:385
  5.0 1.9 %rest.1.refs_0_ = f32[1400,128]{1,0:T(8,128)} custom-call(bf16[8,200,128]{2,1,0:T(8,128)(2,1)} %bitcast.23, f32[312,128]{1,0:T(8,128)} %pack.1.first.refs_0_), custom_call_target="tpu_custom_call" | custom-call | tf_op jit(solution)/shard_map/rest/pallas_call | solution.py:413
  7.0 3.6 %collective-permute-done.refs_1_.refs_6_ = f32[312,128]{1,0:T(8,128)S(1)} collective-permute-done((f32[312,128]{1,0:T(8,128)}, f32[312,128]{1,0:T(8,128)S(1)}, u32[]{:S(2)}, u32[]{:S(2)}) %collective-permute-start) | collective-permute-done | bytes 159776 | tf_op jit(solution)/shard_map/ppermute | solution.py:385
  10.6 1.3 %collective-permute-start.3 = (f32[1400,128]{1,0:T(8,128)}, f32[1400,128]{1,0:T(8,128)}, u32[]{:S(2)}, u32[]{:S(2)}) collective-permute-start(f32[1400,128]{1,0:T(8,128)} %rest.1.refs_0_), channel_id=1, source_target_pairs={{32,0},{64,32},{96,64},{128,96},{160,128},{192,160},{224,192},{256... | collective-permute-start | bytes 2150408 | tf_op jit(solution)/shard_map/ppermute | solution.py:385
  11.9 0.0 copy-start
  11.9 9.9 %collective-permute-start.1 = (f32[224,128]{1,0:T(8,128)S(1)}, f32[224,128]{1,0:T(8,128)S(1)}, u32[]{:S(2)}, u32[]{:S(2)}) collective-permute-start(f32[224,128]{1,0:T(8,128)S(1)} %pad_maximum_fusion), channel_id=1, source_target_pairs={{1,0},{2,1},{3,2},{4,3},{5,4},{6,5},{7,6},{8,7},{9,8},{10,9},{11,1... | collective-permute-start | bytes 344072 | tf_op jit(solution)/shard_map/ppermute | solution.py:390
  21.9 0.5 copy.12
  22.4 0.4 collective-permute-done.1.packed
  22.8 2.7 %strip.1 = (f32[200,128]{1,0:T(8,128)S(1)}, f32[416,128]{1,0:T(8,128)S(1)}) custom-call(f32[224,128]{1,0:T(8,128)S(1)} %collective-permute-done.1.packed, bf16[3,8,100,100]{3,2,1,0:T(8,128)(2,1)S(1)} %bitcast.10), custom_call_target="tpu_custom_call" | custom-call | bytes 40000000 | tf_op jit(solution)/shard_map/strip/pallas_call | solution.py:424
  25.5 0.0 copy-start.5
  25.6 0.6 copy-done.5
  26.2 1.7 %window1_from0.1.refs_0_.refs_11_ = f32[304,128]{1,0:T(8,128)S(1)} custom-call(f32[312,128]{1,0:T(8,128)S(1)} %copy-done.2, f32[312,128]{1,0:T(8,128)S(1)} %collective-permute-done.refs_1_.refs_6_, f32[416,128]{1,0:T(8,128)S(1)} %get-tuple-element.16.refs_2_.refs_3_.refs_7_, f32[416,128]{1,0:T(8,128)S(1)} %get-tuple-element.16.refs_2_.refs_3_.refs_7_, ...), custom_call_target="tpu_custom_call" | custom-call | bytes 40000000 | tf_op jit(solution)/shard_map/window1_from0/pallas_call | solution.py:370
  27.9 0.0 copy-start.4
  27.9 1.4 %collective-permute-start.2 = (f32[304,128]{1,0:T(8,128)S(1)}, f32[304,128]{1,0:T(8,128)S(1)}, u32[]{:S(2)}, u32[]{:S(2)}) collective-permute-start(f32[304,128]{1,0:T(8,128)S(1)} %window1_from0.1.refs_0_.refs_11_), channel_id=1, source_target_pairs={{32,0},{64,32},{96,64},{128,96},{160,128},{192,160},{224,192},{256... | collective-permute-start | bytes 466952 | tf_op jit(solution)/shard_map/ppermute | solution.py:385
  29.4 0.0 collective-permute-done.3.refs_1_
  29.4 4.8 %window1_from1.1.refs_0_ = f32[1400,128]{1,0:T(8,128)S(1)} custom-call(f32[1400,128]{1,0:T(8,128)S(1)} %copy-done.1, f32[1400,128]{1,0:T(8,128)} %collective-permute-done.3.refs_1_, f32[416,128]{1,0:T(8,128)S(1)} %get-tuple-element.16.refs_2_.refs_3_.refs_7_, f32[416,128]{1,0:T(8,128)S(1)} %get-tuple-element.16.refs_2_.refs_3_.refs_7_, ...), custom_call_target="tpu_custom_call" | custom-call | bytes 10000000 | tf_op jit(solution)/shard_map/window1_from1/pallas_call | solution.py:370
  34.2 0.8 collective-permute-done.2.refs_1_.refs_3_
  35.0 1.3 %collective-permute-start.4 = (f32[1400,128]{1,0:T(8,128)S(1)}, f32[1400,128]{1,0:T(8,128)}, u32[]{:S(2)}, u32[]{:S(2)}) collective-permute-start(f32[1400,128]{1,0:T(8,128)S(1)} %window1_from1.1.refs_0_), channel_id=1, source_target_pairs={{32,0},{64,32},{96,64},{128,96},{160,128},{192,160},{224,192},{256... | collective-permute-start | bytes 2150408 | tf_op jit(solution)/shard_map/ppermute | solution.py:385
  36.3 0.0 copy-start.8
  36.3 0.7 copy-done.8
  37.0 2.7 %window0_from0.1 = (bf16[8,200,128]{2,1,0:T(8,128)(2,1)}, f32[256,128]{1,0:T(8,128)S(1)}, f32[256,128]{1,0:T(8,128)S(1)}) custom-call(f32[304,128]{1,0:T(8,128)S(1)} %window1_from0.1.refs_0_.refs_11_, f32[304,128]{1,0:T(8,128)S(1)} %collective-permute-done.2.refs_1_.refs_3_, f32[200,128]{1,0:T(8,128)S(1)} %get-tuple-element.17.refs_11_.refs_2_, ...), custom_call_target="tpu_custom_call" | custom-call | bytes 10000000 | tf_op jit(solution)/shard_map/window0_from0/pallas_call | solution.py:370
  39.6 9.1 %collective-permute-start.5 = (f32[256,128]{1,0:T(8,128)S(1)}, f32[256,128]{1,0:T(8,128)S(1)}, u32[]{:S(2)}, u32[]{:S(2)}) collective-permute-start(f32[256,128]{1,0:T(8,128)S(1)} %get-tuple-element.25), channel_id=1, source_target_pairs={{1,0},{0,1},{3,2},{2,3},{5,4},{4,5},{7,6},{6,7},{9,8},{8,9},{11,10... | collective-permute-start | bytes 393224 | tf_op jit(solution)/shard_map/ppermute | solution.py:454
  48.8 1.0 %collective-permute-done.5 = f32[256,128]{1,0:T(8,128)S(1)} collective-permute-done((f32[256,128]{1,0:T(8,128)S(1)}, f32[256,128]{1,0:T(8,128)S(1)}, u32[]{:S(2)}, u32[]{:S(2)}) %collective-permute-start.5) | collective-permute-done | bytes 131104 | tf_op jit(solution)/shard_map/ppermute | solution.py:454
  49.7 0.7 add.20
  50.4 24.5 %all-to-all-start = ((f32[256,1,128]{2,1,0:T(1,128)}), f32[256,1,128]{2,1,0:T(1,128)S(1)}, u32[]{:S(2)}, u32[]{:S(2)}) async-start(f32[256,1,128]{2,1,0:T(1,128)} %bitcast.5), calls=%async_computation | async-start | bytes 262144 | tf_op jit(solution)/shard_map/all_to_all | solution.py:456
  74.9 0.0 collective-permute-done.4.refs_1_
  74.9 5.6 %window0_from1.1 = bf16[8,200,128]{2,1,0:T(8,128)(2,1)} custom-call(f32[1400,128]{1,0:T(8,128)S(1)} %window1_from1.1.refs_0_, f32[1400,128]{1,0:T(8,128)} %collective-permute-done.4.refs_1_, f32[200,128]{1,0:T(8,128)S(1)} %get-tuple-element.17.refs_11_.refs_2_, ...), custom_call_target="tpu_custom_call", output_to_operand_aliasing={{}: (11, {})} | custom-call | bytes 10000000 | tf_op jit(solution)/shard_map/window0_from1/pallas_call | solution.py:370
  80.5 7.6 %all-to-all-done = f32[256,1,128]{2,1,0:T(1,128)S(1)} async-done(((f32[256,1,128]{2,1,0:T(1,128)}), f32[256,1,128]{2,1,0:T(1,128)S(1)}, u32[]{:S(2)}, u32[]{:S(2)}) %all-to-all-start) | async-done | bytes 131104 | tf_op jit(solution)/shard_map/all_to_all | solution.py:456
  88.1 0.6 gather_sum.1
  (14 shorter events, 0.1 us)
Async XLA Ops:
  3.6 8.3 %copy-start.2 = (f32[312,128]{1,0:T(8,128)S(1)}, f32[312,128]{1,0:T(8,128)}, u32[]{:S(2)}) copy-start(f32[312,128]{1,0:T(8,128)} %pack.1.first.refs_0_) | copy-start | bytes 479236
  3.6 18.3 %copy-start.7 = (bf16[3,8,100,100]{3,1,2,0:T(8,128)(2,1)S(1)}, bf16[3,8,100,100]{3,1,2,0:T(8,128)(2,1)}, u32[]{:S(2)}) copy-start(bf16[3,8,100,100]{3,1,2,0:T(8,128)(2,1)} %param.10) | copy-start | bytes 1440004
  3.6 6.9 %collective-permute-start = (f32[312,128]{1,0:T(8,128)}, f32[312,128]{1,0:T(8,128)S(1)}, u32[]{:S(2)}, u32[]{:S(2)}) collective-permute-start(f32[312,128]{1,0:T(8,128)} %pack.1.first.refs_0_), channel_id=1, source_target_pairs={{32,0},{64,32},{96,64},{128,96},{160,128},{192,160},{224,192},{256... | collective-permute-start | bytes 479240 | tf_op jit(solution)/shard_map/ppermute | solution.py:385
  10.6 18.8 %collective-permute-start.3 = (f32[1400,128]{1,0:T(8,128)}, f32[1400,128]{1,0:T(8,128)}, u32[]{:S(2)}, u32[]{:S(2)}) collective-permute-start(f32[1400,128]{1,0:T(8,128)} %rest.1.refs_0_), channel_id=1, source_target_pairs={{32,0},{64,32},{96,64},{128,96},{160,128},{192,160},{224,192},{256... | collective-permute-start | bytes 2150408 | tf_op jit(solution)/shard_map/ppermute | solution.py:385
  11.9 13.7 %copy-start = (bf16[2,8,100,2,128]{4,3,2,1,0:T(2,128)(2,1)S(1)}, bf16[2,8,100,2,128]{4,3,2,1,0:T(2,128)(2,1)}, u32[]{:S(2)}) copy-start(bf16[2,8,100,2,128]{4,3,2,1,0:T(2,128)(2,1)} %param.9) | copy-start | bytes 2457604
  11.9 10.9 %collective-permute-start.1 = (f32[224,128]{1,0:T(8,128)S(1)}, f32[224,128]{1,0:T(8,128)S(1)}, u32[]{:S(2)}, u32[]{:S(2)}) collective-permute-start(f32[224,128]{1,0:T(8,128)S(1)} %pad_maximum_fusion), channel_id=1, source_target_pairs={{1,0},{2,1},{3,2},{4,3},{5,4},{6,5},{7,6},{8,7},{9,8},{10,9},{11,1... | collective-permute-start | bytes 344072 | tf_op jit(solution)/shard_map/ppermute | solution.py:390
  22.8 2.8 %copy-start.3 = (s32[8,2,128]{2,1,0:T(2,128)S(1)}, s32[8,2,128]{2,1,0:T(2,128)}, u32[]{:S(2)}) copy-start(s32[8,2,128]{2,1,0:T(2,128)} %refs_8_.7) | copy-start | bytes 24580
  22.8 2.8 %copy-start.6 = (f32[2,128]{1,0:T(2,128)S(1)}, f32[2,128]{1,0:T(2,128)}, u32[]{:S(2)}) copy-start(f32[2,128]{1,0:T(2,128)} %refs_5_.7) | copy-start | bytes 3076
  25.5 0.7 copy-start.5
  26.2 3.2 %copy-start.1 = (f32[1400,128]{1,0:T(8,128)S(1)}, f32[1400,128]{1,0:T(8,128)}, u32[]{:S(2)}) copy-start(f32[1400,128]{1,0:T(8,128)} %rest.1.refs_0_) | copy-start | bytes 2150404
  27.9 9.0 %copy-start.4 = (f32[100,2,128]{2,1,0:T(2,128)S(1)}, f32[100,2,128]{2,1,0:T(2,128)}, u32[]{:S(2)}) copy-start(f32[100,2,128]{2,1,0:T(2,128)} %param.13) | copy-start | bytes 307204
  27.9 7.0 %collective-permute-start.2 = (f32[304,128]{1,0:T(8,128)S(1)}, f32[304,128]{1,0:T(8,128)S(1)}, u32[]{:S(2)}, u32[]{:S(2)}) collective-permute-start(f32[304,128]{1,0:T(8,128)S(1)} %window1_from0.1.refs_0_.refs_11_), channel_id=1, source_target_pairs={{32,0},{64,32},{96,64},{128,96},{160,128},{192,160},{224,192},{256... | collective-permute-start | bytes 466952 | tf_op jit(solution)/shard_map/ppermute | solution.py:385
  35.0 39.9 %collective-permute-start.4 = (f32[1400,128]{1,0:T(8,128)S(1)}, f32[1400,128]{1,0:T(8,128)}, u32[]{:S(2)}, u32[]{:S(2)}) collective-permute-start(f32[1400,128]{1,0:T(8,128)S(1)} %window1_from1.1.refs_0_), channel_id=1, source_target_pairs={{32,0},{64,32},{96,64},{128,96},{160,128},{192,160},{224,192},{256... | collective-permute-start | bytes 2150408 | tf_op jit(solution)/shard_map/ppermute | solution.py:385
  36.3 0.7 copy-start.8
  39.6 10.1 %collective-permute-start.5 = (f32[256,128]{1,0:T(8,128)S(1)}, f32[256,128]{1,0:T(8,128)S(1)}, u32[]{:S(2)}, u32[]{:S(2)}) collective-permute-start(f32[256,128]{1,0:T(8,128)S(1)} %get-tuple-element.25), channel_id=1, source_target_pairs={{1,0},{0,1},{3,2},{2,3},{5,4},{4,5},{7,6},{6,7},{9,8},{8,9},{11,10... | collective-permute-start | bytes 393224 | tf_op jit(solution)/shard_map/ppermute | solution.py:454
  50.4 37.7 %all-to-all-start = ((f32[256,1,128]{2,1,0:T(1,128)}), f32[256,1,128]{2,1,0:T(1,128)S(1)}, u32[]{:S(2)}, u32[]{:S(2)}) async-start(f32[256,1,128]{2,1,0:T(1,128)} %bitcast.5), calls=%async_computation | async-start | bytes 262144 | tf_op jit(solution)/shard_map/all_to_all | solution.py:456

commit v5 on v4

--- a/solution.py
+++ b/solution.py
@@ -194,8 +194,27 @@
     out[pl.ds(1, spec, stride=2), :] = pltpu.roll(value, half, 1)
 
 
-def sum_kernel(parts, out):
-    out[...] = jnp.sum(parts[...], axis=0, keepdims=True)
+def sum_kernel(parts, out, *, count):
+    size = out.shape[0]
+    if size == 1:
+        out[...] = jnp.sum(parts[...], axis=0, keepdims=True)
+        return
+    acc = parts[0:size]
+    for k in range(1, count):
+        acc = acc + parts[k * size : (k + 1) * size]
+    out[...] = acc
+
+
+def add_parts(parts, count):
+    size, width = parts.shape[0] // count, parts.shape[1]
+    return pl.pallas_call(
+        functools.partial(sum_kernel, count=count),
+        out_shape=jax.ShapeDtypeStruct((size, width), F32),
+        in_specs=[VMEM],
+        out_specs=VMEM,
+        name=f"add_{count}_parts",
+        compiler_params=vmem(4),
+    )(parts)
 
 
 def split3(value):
@@ -207,7 +226,7 @@
 
 
 def window_kernel(
-    *refs, window, first_level, count, rows, last, grad, regions
+    *refs, window, first_level, count, rows, last, grad, regions, near
 ):
     refs = list(refs)
     own, north, west, corner_r, clon, clat, north_c, west_c, stiff, state_h, mats_h = refs[:11]
@@ -222,7 +241,7 @@
     if last:
         out_h = refs.pop(0)
         if grad:
-            mine, theirs = refs.pop(0), refs.pop(0)
+            partial = refs.pop(0)
     else:
         lam_out = refs.pop(0)
     x_s, y_s, flat_s, state_s, mats_s, sems = refs[:6]
@@ -294,6 +313,7 @@
     put.start()
     if grad:
         ids = jnp.concatenate([region[0:1], region[1:2]], axis=1)
+        ids = (ids & (near - 1)) * (regions // near) + lax.shift_right_logical(ids, near.bit_length() - 1)
         labels = lax.broadcasted_iota(jnp.int32, (regions, 2 * width), 0)
         onehot = jnp.where(labels == ids, 1.0, 0.0).astype(BF16)
         total = []
@@ -308,8 +328,7 @@
             result = result + lax.dot_general(
                 onehot, piece, (((1,), (1,)), ((), ())), preferred_element_type=F32
             )
-        mine[...] = result[0 : regions // 2]
-        theirs[...] = result[regions // 2 :]
+        partial[...] = result
     put.wait()
 
 
@@ -320,12 +339,12 @@
     rows, width = state.shape[2], state.shape[3]
     spec = rows // 2
     grad = extra is not None
-    regions = 0
+    regions, near = 0, 0
     args = [own, north, west, corner, clon, clat, north_c, west_c, stiff, state, mats]
     specs = [VMEM] * 9 + [ANY] * 2
     aliases = {}
     if grad:
-        before, emission, region, regions = extra
+        before, emission, region, regions, near = extra
         args += [before, emission, region]
         specs += [VMEM] * 3
     if edge is not None:
@@ -340,8 +359,8 @@
         out_shape = [jax.ShapeDtypeStruct((levels, rows, width), BF16)]
         out_specs = [ANY]
         if grad:
-            out_shape += [jax.ShapeDtypeStruct((regions // 2, width), F32)] * 2
-            out_specs += [VMEM] * 2
+            out_shape.append(jax.ShapeDtypeStruct((regions, width), F32))
+            out_specs.append(VMEM)
     else:
         out_shape = [
             jax.ShapeDtypeStruct((count * rows + (0 if edge is None else TAIL), width), F32),
@@ -366,6 +385,7 @@
         last=last,
         grad=grad,
         regions=regions,
+        near=near,
     )
     return pl.pallas_call(
         body,
@@ -444,30 +464,25 @@
     )[0]
     low0_n, rest0 = lax.optimization_barrier((low0_n, rest0))
     rest0_n = to_north(rest0)
-    parity = lax.axis_index("lon") % 2
-    slot = region_id // 2 + jnp.where(region_id % 2 == parity, 0, regions // 2)
-    low_extra = (low0, flat_em, slot, regions)
-    out, mine, theirs = run_window(
+    bands, blocks = lax.axis_size("lat"), lax.axis_size("lon")
+    near = blocks // 2
+    far = regions // near
+    low_extra = (low0, flat_em, region_id, regions, near)
+    out, partial = run_window(
         low0, low0_n, strip, low0_n, shared, 0, 0, 1, True, extra=low_extra
     )
-    pairs = [(k ^ 1, k) for k in range(regions)]
-    mine = mine + lax.ppermute(theirs, ("lat", "lon"), pairs)
-    groups = [list(range(k, regions, 2)) for k in range(2)]
+    line = [list(range(k * near, (k + 1) * near)) for k in range(2)]
+    lines = lax.all_to_all(partial, "lon", 0, 0, axis_index_groups=line, tiled=True)
+    mine = add_parts(lines, near)
+    plane = [list(range(k, regions, near)) for k in range(near)]
     spread = lax.all_to_all(
-        mine, ("lat", "lon"), 0, 0, axis_index_groups=groups, tiled=True
+        mine, ("lat", "lon"), 0, 0, axis_index_groups=plane, tiled=True
     )
     out = run_window(
         rest0, rest0_n, strip, low0_n, shared, 0, 1, levels - 1, True, prior=out
     )[0]
     out, spread = lax.optimization_barrier((out, spread))
-    grad = pl.pallas_call(
-        sum_kernel,
-        out_shape=jax.ShapeDtypeStruct((1, width), F32),
-        in_specs=[VMEM],
-        out_specs=VMEM,
-        name="gather_sum",
-        compiler_params=vmem(4),
-    )(spread)[:, :spec]
+    grad = add_parts(spread, far)[:, :spec]
     return out.reshape(levels, spec, lat_rows, width), grad
 
 

time: 89.2 us -> 88.8 us (level)
  blocking collectives: 0 us -> 24.7 us
  starting transfers between devices: 49 us -> 30.3 us
  waiting for transfers between devices: 13.3 us -> 9.98 us
  Pallas kernels: 22.9 us -> 21.3 us
    all_to_all x0 -> x1, blocking collectives: none -> 24.7 us  [per_device(): lax.all_to_all(partial, 'lon', 0, 0, axis_index_groups=line, tiled=True)]
    all_to_all x1, starting transfers between devices: 24.5 us -> 14.9 us  [per_device(): lax.all_to_all(mine, ('lat', 'lon'), 0, 0, axis_index_groups=plane, tiled...]
    ppermute x1 -> x0, starting transfers between devices: 9.13 us -> none  [per_device(): mine = mine + lax.ppermute(theirs, ('lat', 'lon'), pairs)]
    all_to_all x1, waiting for transfers between devices: 7.62 us -> 4.14 us  [per_device(): lax.all_to_all(mine, ('lat', 'lon'), 0, 0, axis_index_groups=plane, tiled...]
    pallas_call x4, Pallas kernels: 14.7 us -> 12.5 us  [run_window(): pl.pallas_call(body, out_shape=out_shape, in_specs=specs, out_specs=out_s...]
    ppermute x4, waiting for transfers between devices: 4.35 us -> 5.43 us  [to_north(): return lax.ppermute(block, 'lat', [(i + 1, i) for i in range(bands - 1)])]
    ppermute x1 -> x0, waiting for transfers between devices: 0.96 us -> none  [per_device(): mine = mine + lax.ppermute(theirs, ('lat', 'lon'), pairs)]
  transfers between devices with their start and end apart: 7 -> 6, of which waited for: 5 -> 4; matrix products, arithmetic and copies ran while one was open for 1% -> 1% of each run, Pallas kernels for 22% -> 20%
where the time goes in v5:
time: 88.8 us; the launch traced here: 88.4 us
  starting transfers between devices  30.3 us (34%)
  blocking collectives  24.7 us (28%)
  Pallas kernels  21.3 us (24%)
  waiting for transfers between devices  9.98 us (11%)
  local copies, waits for them, and re-layouts  1.22 us (1%)
    all_to_all x1, blocking collectives, per_device(): lax.all_to_all(partial, 'lon', 0, 0, axis_index_groups=line, tiled=True)  24.7 us
    all_to_all x1, starting transfers between devices, per_device(): lax.all_to_all(mine, ('lat', 'lon'), 0, 0, axis_index_groups=plane, tiled...  14.9 us
    pallas_call x4, Pallas kernels, run_window(): pl.pallas_call(body, out_shape=out_shape, in_specs=specs, out_specs=out_s...  12.5 us
    ppermute x1, starting transfers between devices, to_west(): lax.ppermute(block, 'lon', [((j + 1) % blocks, j) for j in range(blocks)])  9.94 us
    ppermute x4, waiting for transfers between devices, to_north(): return lax.ppermute(block, 'lat', [(i + 1, i) for i in range(bands - 1)])  5.43 us
    ppermute x4, starting transfers between devices, to_north(): return lax.ppermute(block, 'lat', [(i + 1, i) for i in range(bands - 1)])  5.41 us
    all_to_all x1, waiting for transfers between devices, per_device(): lax.all_to_all(mine, ('lat', 'lon'), 0, 0, axis_index_groups=plane, tiled...  4.14 us
    pallas_call x1, Pallas kernels, per_device(): pl.pallas_call(functools.partial(pack_kernel, rows=rows), out_shape=jax.S...  2.94 us
  transfers between devices with their start and end apart: 6, of which 4 were waited for; matrix products, arithmetic and copies ran while one was open for 1% of the time, Pallas kernels for 20%

profile of v5, /device:TPU:1, one launch (start us, length us, event | category | flops | bytes accessed | tf_op | source)
XLA Modules:
  0.0 88.4 jit_solution(6586659471250995268)
XLA Ops:
  0.6 2.9 %pack.1.first.refs_0_ = f32[312,128]{1,0:T(8,128)} custom-call(bf16[8,200,128]{2,1,0:T(8,128)(2,1)} %bitcast.26, f32[2,128]{1,0:T(2,128)} %refs_4_.7, f32[2,128]{1,0:T(2,128)} %refs_5_.7, s32[8,2,128]{2,1,0:T(2,128)} %refs_8_.7, bf16[2,8,200,128]{3,2,1,0:T(8,128)(2,1)} %bitcast.17), custom_call_target="tpu_custom_call" | custom-call | tf_op jit(solution)/shard_map/pack/pallas_call | solution.py:423
  3.6 0.0 copy-start.2
  3.6 0.0 copy-start.8
  3.6 1.4 %collective-permute-start = (f32[312,128]{1,0:T(8,128)}, f32[312,128]{1,0:T(8,128)S(1)}, u32[]{:S(2)}, u32[]{:S(2)}) collective-permute-start(f32[312,128]{1,0:T(8,128)} %pack.1.first.refs_0_), channel_id=1, source_target_pairs={{32,0},{64,32},{96,64},{128,96},{160,128},{192,160},{224,192},{256... | collective-permute-start | bytes 479240 | tf_op jit(solution)/shard_map/ppermute | solution.py:405
  5.0 1.9 %rest.1.refs_0_ = f32[1400,128]{1,0:T(8,128)} custom-call(bf16[8,200,128]{2,1,0:T(8,128)(2,1)} %bitcast.27, f32[312,128]{1,0:T(8,128)} %pack.1.first.refs_0_), custom_call_target="tpu_custom_call" | custom-call | tf_op jit(solution)/shard_map/rest/pallas_call | solution.py:433
  7.0 3.6 %collective-permute-done.refs_1_.refs_6_ = f32[312,128]{1,0:T(8,128)S(1)} collective-permute-done((f32[312,128]{1,0:T(8,128)}, f32[312,128]{1,0:T(8,128)S(1)}, u32[]{:S(2)}, u32[]{:S(2)}) %collective-permute-start) | collective-permute-done | bytes 159776 | tf_op jit(solution)/shard_map/ppermute | solution.py:405
  10.6 1.3 %collective-permute-start.3 = (f32[1400,128]{1,0:T(8,128)}, f32[1400,128]{1,0:T(8,128)S(1)}, u32[]{:S(2)}, u32[]{:S(2)}) collective-permute-start(f32[1400,128]{1,0:T(8,128)} %rest.1.refs_0_), channel_id=1, source_target_pairs={{32,0},{64,32},{96,64},{128,96},{160,128},{192,160},{224,192},{256... | collective-permute-start | bytes 2150408 | tf_op jit(solution)/shard_map/ppermute | solution.py:405
  11.8 0.0 copy-done.2
  11.9 0.0 copy-start
  11.9 9.9 %collective-permute-start.1 = (f32[224,128]{1,0:T(8,128)S(1)}, f32[224,128]{1,0:T(8,128)S(1)}, u32[]{:S(2)}, u32[]{:S(2)}) collective-permute-start(f32[224,128]{1,0:T(8,128)S(1)} %pad_maximum_fusion), channel_id=1, source_target_pairs={{1,0},{2,1},{3,2},{4,3},{5,4},{6,5},{7,6},{8,7},{9,8},{10,9},{11,1... | collective-permute-start | bytes 344072 | tf_op jit(solution)/shard_map/ppermute | solution.py:410
  21.9 0.5 copy.12
  22.4 0.4 collective-permute-done.1.packed
  22.8 2.7 %strip.1 = (f32[200,128]{1,0:T(8,128)S(1)}, f32[416,128]{1,0:T(8,128)S(1)}) custom-call(f32[224,128]{1,0:T(8,128)S(1)} %collective-permute-done.1.packed, bf16[3,8,100,100]{3,2,1,0:T(8,128)(2,1)S(1)} %bitcast.12), custom_call_target="tpu_custom_call" | custom-call | bytes 40000000 | tf_op jit(solution)/shard_map/strip/pallas_call | solution.py:444
  25.5 0.0 copy-start.5
  25.6 0.6 copy-done.5
  26.2 1.7 %window1_from0.1.refs_0_.refs_11_ = f32[304,128]{1,0:T(8,128)S(1)} custom-call(f32[312,128]{1,0:T(8,128)S(1)} %copy-done.2, f32[312,128]{1,0:T(8,128)S(1)} %collective-permute-done.refs_1_.refs_6_, f32[416,128]{1,0:T(8,128)S(1)} %get-tuple-element.15.refs_2_.refs_3_.refs_7_, f32[416,128]{1,0:T(8,128)S(1)} %get-tuple-element.15.refs_2_.refs_3_.refs_7_, ...), custom_call_target="tpu_custom_call" | custom-call | bytes 40000000 | tf_op jit(solution)/shard_map/window1_from0/pallas_call | solution.py:390
  27.9 0.0 copy-start.4
  27.9 1.4 %collective-permute-start.2 = (f32[304,128]{1,0:T(8,128)S(1)}, f32[304,128]{1,0:T(8,128)S(1)}, u32[]{:S(2)}, u32[]{:S(2)}) collective-permute-start(f32[304,128]{1,0:T(8,128)S(1)} %window1_from0.1.refs_0_.refs_11_), channel_id=1, source_target_pairs={{32,0},{64,32},{96,64},{128,96},{160,128},{192,160},{224,192},{256... | collective-permute-start | bytes 466952 | tf_op jit(solution)/shard_map/ppermute | solution.py:405
  29.4 0.0 collective-permute-done.3.refs_1_
  29.4 0.0 copy-done.1
  29.4 3.7 %window1_from1.1.refs_0_ = f32[1400,128]{1,0:T(8,128)S(1)} custom-call(f32[1400,128]{1,0:T(8,128)S(1)} %copy-done.1, f32[1400,128]{1,0:T(8,128)S(1)} %collective-permute-done.3.refs_1_, f32[416,128]{1,0:T(8,128)S(1)} %get-tuple-element.15.refs_2_.refs_3_.refs_7_, f32[416,128]{1,0:T(8,128)S(1)} %get-tuple-element.15.refs_2_.refs_3_.refs_7_, ...), custom_call_target="tpu_custom_call" | custom-call | bytes 10000000 | tf_op jit(solution)/shard_map/window1_from1/pallas_call | solution.py:390
  33.1 0.0 copy-start.7
  33.1 1.8 %collective-permute-done.2.refs_1_.refs_3_ = f32[304,128]{1,0:T(8,128)S(1)} collective-permute-done((f32[304,128]{1,0:T(8,128)S(1)}, f32[304,128]{1,0:T(8,128)S(1)}, u32[]{:S(2)}, u32[]{:S(2)}) %collective-permute-start.2) | collective-permute-done | bytes 155680 | tf_op jit(solution)/shard_map/ppermute | solution.py:405
  35.0 1.3 %collective-permute-start.4 = (f32[1400,128]{1,0:T(8,128)S(1)}, f32[1400,128]{1,0:T(8,128)S(1)}, u32[]{:S(2)}, u32[]{:S(2)}) collective-permute-start(f32[1400,128]{1,0:T(8,128)S(1)} %window1_from1.1.refs_0_), channel_id=1, source_target_pairs={{32,0},{64,32},{96,64},{128,96},{160,128},{192,160},{224,192},{256... | collective-permute-start | bytes 2150408 | tf_op jit(solution)/shard_map/ppermute | solution.py:405
  36.3 2.7 %window0_from0.1 = (bf16[8,200,128]{2,1,0:T(8,128)(2,1)}, f32[512,128]{1,0:T(8,128)S(1)}) custom-call(f32[304,128]{1,0:T(8,128)S(1)} %window1_from0.1.refs_0_.refs_11_, f32[304,128]{1,0:T(8,128)S(1)} %collective-permute-done.2.refs_1_.refs_3_, f32[200,128]{1,0:T(8,128)S(1)} %get-tuple-element.16.refs_11_.refs_2_, ...), custom_call_target="tpu_custom_call" | custom-call | bytes 10000000 | tf_op jit(solution)/shard_map/window0_from0/pallas_call | solution.py:390
  38.9 24.7 %all_to_all.23 = f32[16,32,128]{2,1,0:T(8,128)S(1)} all-to-all(f32[16,32,128]{2,1,0:T(8,128)S(1)} %bitcast.23), channel_id=1, replica_groups={{0,1,2,3,4,5,6,7,8,9,10,11,12,13,14,15},{16,17,18,19,20,21,22,23,24,25,..., dimensions={0} | all-to-all | bytes 524288 | tf_op jit(solution)/shard_map/all_to_all | solution.py:475
  63.6 0.6 add_16_parts.1
  64.3 14.9 %all-to-all-start.1 = ((f32[32,1,128]{2,1,0:T(1,128)}), f32[32,1,128]{2,1,0:T(1,128)S(1)}, u32[]{:S(2)}, u32[]{:S(2)}) async-start(f32[32,1,128]{2,1,0:T(1,128)} %bitcast.7), calls=%async_computation.1 | async-start | bytes 32768 | tf_op jit(solution)/shard_map/all_to_all | solution.py:478
  79.2 0.0 collective-permute-done.4.refs_1_
  79.2 4.5 %window0_from1.1 = bf16[8,200,128]{2,1,0:T(8,128)(2,1)} custom-call(f32[1400,128]{1,0:T(8,128)S(1)} %window1_from1.1.refs_0_, f32[1400,128]{1,0:T(8,128)S(1)} %collective-permute-done.4.refs_1_, f32[200,128]{1,0:T(8,128)S(1)} %get-tuple-element.16.refs_11_.refs_2_, ...), custom_call_target="tpu_custom_call", output_to_operand_aliasing={{}: (11, {})} | custom-call | bytes 10000000 | tf_op jit(solution)/shard_map/window0_from1/pallas_call | solution.py:390
  83.7 4.1 %all-to-all-done.1 = f32[32,1,128]{2,1,0:T(1,128)S(1)} async-done(((f32[32,1,128]{2,1,0:T(1,128)}), f32[32,1,128]{2,1,0:T(1,128)S(1)}, u32[]{:S(2)}, u32[]{:S(2)}) %all-to-all-start.1) | async-done | bytes 16416 | tf_op jit(solution)/shard_map/all_to_all | solution.py:478
  87.8 0.5 add_32_parts.1
  (12 shorter events, 0.0 us)
Async XLA Ops:
  3.6 8.3 %copy-start.2 = (f32[312,128]{1,0:T(8,128)S(1)}, f32[312,128]{1,0:T(8,128)}, u32[]{:S(2)}) copy-start(f32[312,128]{1,0:T(8,128)} %pack.1.first.refs_0_) | copy-start | bytes 479236
  3.6 18.3 %copy-start.8 = (bf16[3,8,100,100]{3,1,2,0:T(8,128)(2,1)S(1)}, bf16[3,8,100,100]{3,1,2,0:T(8,128)(2,1)}, u32[]{:S(2)}) copy-start(bf16[3,8,100,100]{3,1,2,0:T(8,128)(2,1)} %param.10) | copy-start | bytes 1440004
  3.6 6.9 %collective-permute-start = (f32[312,128]{1,0:T(8,128)}, f32[312,128]{1,0:T(8,128)S(1)}, u32[]{:S(2)}, u32[]{:S(2)}) collective-permute-start(f32[312,128]{1,0:T(8,128)} %pack.1.first.refs_0_), channel_id=1, source_target_pairs={{32,0},{64,32},{96,64},{128,96},{160,128},{192,160},{224,192},{256... | collective-permute-start | bytes 479240 | tf_op jit(solution)/shard_map/ppermute | solution.py:405
  10.6 18.8 %collective-permute-start.3 = (f32[1400,128]{1,0:T(8,128)}, f32[1400,128]{1,0:T(8,128)S(1)}, u32[]{:S(2)}, u32[]{:S(2)}) collective-permute-start(f32[1400,128]{1,0:T(8,128)} %rest.1.refs_0_), channel_id=1, source_target_pairs={{32,0},{64,32},{96,64},{128,96},{160,128},{192,160},{224,192},{256... | collective-permute-start | bytes 2150408 | tf_op jit(solution)/shard_map/ppermute | solution.py:405
  11.9 13.6 %copy-start = (bf16[2,8,100,2,128]{4,3,2,1,0:T(2,128)(2,1)S(1)}, bf16[2,8,100,2,128]{4,3,2,1,0:T(2,128)(2,1)}, u32[]{:S(2)}) copy-start(bf16[2,8,100,2,128]{4,3,2,1,0:T(2,128)(2,1)} %param.9) | copy-start | bytes 2457604
  11.9 10.9 %collective-permute-start.1 = (f32[224,128]{1,0:T(8,128)S(1)}, f32[224,128]{1,0:T(8,128)S(1)}, u32[]{:S(2)}, u32[]{:S(2)}) collective-permute-start(f32[224,128]{1,0:T(8,128)S(1)} %pad_maximum_fusion), channel_id=1, source_target_pairs={{1,0},{2,1},{3,2},{4,3},{5,4},{6,5},{7,6},{8,7},{9,8},{10,9},{11,1... | collective-permute-start | bytes 344072 | tf_op jit(solution)/shard_map/ppermute | solution.py:410
  22.8 2.8 %copy-start.3 = (s32[8,2,128]{2,1,0:T(2,128)S(1)}, s32[8,2,128]{2,1,0:T(2,128)}, u32[]{:S(2)}) copy-start(s32[8,2,128]{2,1,0:T(2,128)} %refs_8_.7) | copy-start | bytes 24580
  22.8 2.8 %copy-start.6 = (f32[2,128]{1,0:T(2,128)S(1)}, f32[2,128]{1,0:T(2,128)}, u32[]{:S(2)}) copy-start(f32[2,128]{1,0:T(2,128)} %refs_5_.7) | copy-start | bytes 3076
  25.5 0.7 copy-start.5
  26.2 3.2 %copy-start.1 = (f32[1400,128]{1,0:T(8,128)S(1)}, f32[1400,128]{1,0:T(8,128)}, u32[]{:S(2)}) copy-start(f32[1400,128]{1,0:T(8,128)} %rest.1.refs_0_) | copy-start | bytes 2150404
  27.9 8.3 %copy-start.4 = (f32[100,2,128]{2,1,0:T(2,128)S(1)}, f32[100,2,128]{2,1,0:T(2,128)}, u32[]{:S(2)}) copy-start(f32[100,2,128]{2,1,0:T(2,128)} %param.13) | copy-start | bytes 307204
  27.9 7.0 %collective-permute-start.2 = (f32[304,128]{1,0:T(8,128)S(1)}, f32[304,128]{1,0:T(8,128)S(1)}, u32[]{:S(2)}, u32[]{:S(2)}) collective-permute-start(f32[304,128]{1,0:T(8,128)S(1)} %window1_from0.1.refs_0_.refs_11_), channel_id=1, source_target_pairs={{32,0},{64,32},{96,64},{128,96},{160,128},{192,160},{224,192},{256... | collective-permute-start | bytes 466952 | tf_op jit(solution)/shard_map/ppermute | solution.py:405
  33.1 3.2 %copy-start.7 = (s32[2,128]{1,0:T(2,128)S(1)}, s32[2,128]{1,0:T(2,128)}, u32[]{:S(2)}) copy-start(s32[2,128]{1,0:T(2,128)} %refs_13_.1) | copy-start | bytes 3076
  35.0 44.3 %collective-permute-start.4 = (f32[1400,128]{1,0:T(8,128)S(1)}, f32[1400,128]{1,0:T(8,128)S(1)}, u32[]{:S(2)}, u32[]{:S(2)}) collective-permute-start(f32[1400,128]{1,0:T(8,128)S(1)} %window1_from1.1.refs_0_), channel_id=1, source_target_pairs={{32,0},{64,32},{96,64},{128,96},{160,128},{192,160},{224,192},{256... | collective-permute-start | bytes 2150408 | tf_op jit(solution)/shard_map/ppermute | solution.py:405
  64.3 23.6 %all-to-all-start.1 = ((f32[32,1,128]{2,1,0:T(1,128)}), f32[32,1,128]{2,1,0:T(1,128)S(1)}, u32[]{:S(2)}, u32[]{:S(2)}) async-start(f32[32,1,128]{2,1,0:T(1,128)} %bitcast.7), calls=%async_computation.1 | async-start | bytes 32768 | tf_op jit(solution)/shard_map/all_to_all | solution.py:478

commit v6 on v5

--- a/solution.py
+++ b/solution.py
@@ -40,7 +40,7 @@
     return -(-rows // 16) * 8
 
 
-def pack_kernel(adj, clon, clat, stiff, state_h, first, state_s, sem, *, rows):
+def pack_kernel(adj, clon, clat, stiff, state_h, first, west, state_s, sem, *, rows):
     levels, _, width = adj.shape
     half = width // 2
     get = pltpu.make_async_copy(state_h.at[state_h.shape[0] - 1], state_s, sem)
@@ -60,11 +60,12 @@
         acc = place(acc, state_s[lev].astype(F32), half // 2 + WIDE * lev)
     folded = folded_rows(rows)
     upper = jnp.concatenate([acc[folded:], jnp.zeros((2 * folded - rows, width), F32)], axis=0)
-    first[rows : rows + folded] = acc[0:folded] + pltpu.roll(upper, half, 1)
-    at = rows + folded
-    first[at : at + 2] = clon[...]
-    first[at + 2 : at + 4] = clat[...]
-    first[at + 4 : at + 8] = grades[0:4]
+    west[0:folded] = acc[0:folded] + pltpu.roll(upper, half, 1)
+    for out, at in ((first, rows), (west, folded)):
+        out[at : at + 2] = clon[...]
+        out[at + 2 : at + 4] = clat[...]
+        out[at + 4 : at + 8] = grades[0:4]
+    first[rows + EXTRA :] = jnp.zeros((folded + EXTRA, width), F32)
 
 
 def rest_kernel(adj, first, rest, *, rows):
@@ -121,7 +122,7 @@
     def edge(row):
         return pltpu.roll(tall(row), width - 1, 1)[0:1]
 
-    at = rows + folded_rows(rows)
+    at = rows
     lon = [clon[0:1], clon[1:2], north_c[at : at + 1]]
     lat = [clat[0:1], clat[1:2], north_c[at + 2 : at + 3]]
     lon += [edge(west_c[rows : rows + 1]), edge(west_c[rows + 1 : rows + 2])]
@@ -129,16 +130,15 @@
     return with_keep(lon, lat)
 
 
-def strip_kernel(packed, mats, out, both, *, rows):
+def strip_kernel(west_p, north, mats, out, both, *, rows):
     folded = folded_rows(rows)
-    for i in range(2):
-        src, dst = i * (folded + EXTRA), i * (rows + EXTRA)
+    for packed, src, dst in ((west_p, 0, 0), (north, rows + EXTRA, rows + EXTRA)):
         block = packed[src : src + folded]
         both[dst : dst + folded] = block
         both[dst + folded : dst + rows] = pltpu.roll(block, block.shape[1] // 2, 1)[0 : rows - folded]
         both[dst + rows : dst + rows + EXTRA] = packed[src + folded : src + folded + EXTRA]
     west, diag = both.at[0 : rows + EXTRA], both.at[rows + EXTRA : 2 * (rows + EXTRA)]
-    spec, width = rows // 2, both.shape[1]
+    spec, width = rows // 2, out.shape[1]
     half = width // 2
     levels = mats.shape[1]
     at = lanes((spec, width))
@@ -420,15 +420,21 @@
     flat_state = state.reshape(windows, levels, rows, width)
     flat_em = emission.reshape(rows, width)
     mats = jnp.swapaxes(inverses, 2, 3)
-    low1 = pl.pallas_call(
+    folded = folded_rows(rows)
+    low1, west1 = pl.pallas_call(
         functools.partial(pack_kernel, rows=rows),
-        out_shape=jax.ShapeDtypeStruct((rows + folded_rows(rows) + EXTRA, width), F32),
+        out_shape=[
+            jax.ShapeDtypeStruct((rows + folded + 2 * EXTRA, width), F32),
+            jax.ShapeDtypeStruct((folded + EXTRA, width), F32),
+        ],
         in_specs=[VMEM] * 4 + [HBM],
-        out_specs=VMEM,
+        out_specs=[VMEM] * 2,
         scratch_shapes=[pltpu.VMEM((levels, rows, width), BF16), pltpu.SemaphoreType.DMA],
         name="pack",
         compiler_params=vmem(56),
     )(adj, courant_lon, courant_lat, stiffness, flat_state)
+    west1_w = to_west(west1)
+    low1 = lax.dynamic_update_slice(low1, west1_w, (rows + EXTRA, 0))
     low1_n = to_north(low1)
     rest1 = pl.pallas_call(
         functools.partial(rest_kernel, rows=rows),
@@ -437,22 +443,21 @@
         out_specs=VMEM,
         name="rest",
         compiler_params=vmem(56),
-    )(adj, low1)
+    )(adj, west1)
     rest1, low1_n = lax.optimization_barrier((rest1, low1_n))
     rest1_n = to_north(rest1)
-    west1_w = to_west(jnp.concatenate([low1[rows:], low1_n[rows:]], axis=0))
     strip, both = pl.pallas_call(
         functools.partial(strip_kernel, rows=rows),
         out_shape=[
             jax.ShapeDtypeStruct((rows, width), F32),
             jax.ShapeDtypeStruct((2 * (rows + EXTRA), width), F32),
         ],
-        in_specs=[VMEM] * 2,
+        in_specs=[VMEM] * 3,
         out_specs=[VMEM] * 2,
         name="strip",
         cost_estimate=pl.CostEstimate(flops=0, transcendentals=0, bytes_accessed=40_000_000),
         compiler_params=vmem(8),
-    )(west1_w, mats)
+    )(west1_w, low1_n, mats)
     shared = (courant_lon, courant_lat, low1_n, both, stiffness, flat_state, mats)
     low0 = run_window(
         low1, low1_n, both, both, shared, 1, 0, 1, False, edge=strip

time: 88.8 us -> 94.9 us (1.069)
  waiting for transfers between devices: 9.98 us -> 13.1 us
  blocking collectives: 24.7 us -> 27.3 us
  local copies, waits for them, and re-layouts: 1.22 us -> 2.49 us
    ppermute x4, waiting for transfers between devices: 5.43 us -> 8.56 us  [to_north(): return lax.ppermute(block, 'lat', [(i + 1, i) for i in range(bands - 1)])]
    all_to_all x1, blocking collectives: 24.7 us -> 27.3 us  [per_device(): lax.all_to_all(partial, 'lon', 0, 0, axis_index_groups=line, tiled=True)]
    ppermute x1, starting transfers between devices: 9.94 us -> 8.79 us  [to_west(): lax.ppermute(block, 'lon', [((j + 1) % blocks, j) for j in range(blocks)])]
  transfers between devices with their start and end apart: 6 -> 6, of which waited for: 4 -> 4; matrix products, arithmetic and copies ran while one was open for 1% -> 1% of each run, Pallas kernels for 20% -> 19%
where the time goes in v6:
time: 94.9 us; the launch traced here: 94.4 us
  starting transfers between devices  29.4 us (31%)
  blocking collectives  27.3 us (29%)
  Pallas kernels  21.2 us (22%)
  waiting for transfers between devices  13.1 us (14%)
  local copies, waits for them, and re-layouts  2.49 us (3%)
    all_to_all x1, blocking collectives, per_device(): lax.all_to_all(partial, 'lon', 0, 0, axis_index_groups=line, tiled=True)  27.3 us
    all_to_all x1, starting transfers between devices, per_device(): lax.all_to_all(mine, ('lat', 'lon'), 0, 0, axis_index_groups=plane, tiled...  15.3 us
    pallas_call x4, Pallas kernels, run_window(): pl.pallas_call(body, out_shape=out_shape, in_specs=specs, out_specs=out_s...  12.5 us
    ppermute x1, starting transfers between devices, to_west(): lax.ppermute(block, 'lon', [((j + 1) % blocks, j) for j in range(blocks)])  8.79 us
    ppermute x4, waiting for transfers between devices, to_north(): return lax.ppermute(block, 'lat', [(i + 1, i) for i in range(bands - 1)])  8.56 us
    ppermute x4, starting transfers between devices, to_north(): return lax.ppermute(block, 'lat', [(i + 1, i) for i in range(bands - 1)])  5.41 us
    all_to_all x1, waiting for transfers between devices, per_device(): lax.all_to_all(mine, ('lat', 'lon'), 0, 0, axis_index_groups=plane, tiled...  3.48 us
    pallas_call x1, Pallas kernels, per_device(): pl.pallas_call(functools.partial(pack_kernel, rows=rows), out_shape=[jax....  2.91 us
  transfers between devices with their start and end apart: 6, of which 4 were waited for; matrix products, arithmetic and copies ran while one was open for 1% of the time, Pallas kernels for 19%

profile of v6, /device:TPU:1, one launch (start us, length us, event | category | flops | bytes accessed | tf_op | source)
XLA Modules:
  0.0 94.4 jit_solution(2301601913507449282)
XLA Ops:
  0.6 2.9 %pack.1 = (f32[320,128]{1,0:T(8,128)}, f32[112,128]{1,0:T(8,128)}) custom-call(bf16[8,200,128]{2,1,0:T(8,128)(2,1)} %bitcast.26, f32[2,128]{1,0:T(2,128)} %refs_4_.7, f32[2,128]{1,0:T(2,128)} %refs_5_.7, s32[8,2,128]{2,1,0:T(2,128)} %refs_8_.7, bf16[2,8,200,128]{3,2,1,0:T(8,128)(2,1)} %bitcast.17), custom_call_target="tpu_custom_call" | custom-call | tf_op jit(solution)/shard_map/pack/pallas_call | solution.py:424
  3.5 8.8 %collective-permute-start = (f32[112,128]{1,0:T(8,128)}, f32[112,128]{1,0:T(8,128)S(1)}, u32[]{:S(2)}, u32[]{:S(2)}) collective-permute-start(f32[112,128]{1,0:T(8,128)} %get-tuple-element.17.first), channel_id=1, source_target_pairs={{1,0},{2,1},{3,2},{4,3},{5,4},{6,5},{7,6},{8,7},{9,8},{10,9},{11,1... | collective-permute-start | bytes 172040 | tf_op jit(solution)/shard_map/ppermute | solution.py:410
  12.3 1.1 %collective-permute-done.west_p = f32[112,128]{1,0:T(8,128)S(1)} collective-permute-done((f32[112,128]{1,0:T(8,128)}, f32[112,128]{1,0:T(8,128)S(1)}, u32[]{:S(2)}, u32[]{:S(2)}) %collective-permute-start) | collective-permute-done | bytes 57376 | tf_op jit(solution)/shard_map/ppermute | solution.py:410
  13.4 0.6 constant_dynamic-update-slice_fusion.refs_0_
  14.1 1.4 %collective-permute-start.1 = (f32[320,128]{1,0:T(8,128)}, f32[320,128]{1,0:T(8,128)S(1)}, u32[]{:S(2)}, u32[]{:S(2)}) collective-permute-start(f32[320,128]{1,0:T(8,128)} %constant_dynamic-update-slice_fusion.refs_0_), channel_id=1, source_target_pairs={{32,0},{64,32},{96,64},{128,96},{160,128},{192,160},{224,192},{256... | collective-permute-start | bytes 491528 | tf_op jit(solution)/shard_map/ppermute | solution.py:405
  15.5 1.9 %rest.1.refs_0_ = f32[1400,128]{1,0:T(8,128)} custom-call(bf16[8,200,128]{2,1,0:T(8,128)(2,1)} %bitcast.27, f32[112,128]{1,0:T(8,128)} %get-tuple-element.17.first), custom_call_target="tpu_custom_call" | custom-call | tf_op jit(solution)/shard_map/rest/pallas_call | solution.py:439
  17.4 3.0 %collective-permute-done.1.north.refs_1_.refs_6_ = f32[320,128]{1,0:T(8,128)S(1)} collective-permute-done((f32[320,128]{1,0:T(8,128)}, f32[320,128]{1,0:T(8,128)S(1)}, u32[]{:S(2)}, u32[]{:S(2)}) %collective-permute-start.1) | collective-permute-done | bytes 163872 | tf_op jit(solution)/shard_map/ppermute | solution.py:405
  20.4 1.3 %collective-permute-start.3 = (f32[1400,128]{1,0:T(8,128)}, f32[1400,128]{1,0:T(8,128)S(1)}, u32[]{:S(2)}, u32[]{:S(2)}) collective-permute-start(f32[1400,128]{1,0:T(8,128)} %rest.1.refs_0_), channel_id=1, source_target_pairs={{32,0},{64,32},{96,64},{128,96},{160,128},{192,160},{224,192},{256... | collective-permute-start | bytes 2150408 | tf_op jit(solution)/shard_map/ppermute | solution.py:405
  21.7 0.5 copy.12
  22.3 0.0 copy-start.3
  22.3 0.0 copy-start.6
  22.3 2.7 %strip.1 = (f32[200,128]{1,0:T(8,128)S(1)}, f32[416,128]{1,0:T(8,128)S(1)}) custom-call(f32[112,128]{1,0:T(8,128)S(1)} %collective-permute-done.west_p, f32[320,128]{1,0:T(8,128)S(1)} %collective-permute-done.1.north.refs_1_.refs_6_, bf16[3,8,100,100]{3,2,1,0:T(8,128)(2,1)S(1)} %bitcast.12), custom_call_target="tpu_custom_call" | custom-call | bytes 40000000 | tf_op jit(solution)/shard_map/strip/pallas_call | solution.py:449
  25.0 0.0 copy-start.5
  25.1 0.6 copy-done.5
  25.7 1.7 %window1_from0.1.refs_0_.refs_11_ = f32[304,128]{1,0:T(8,128)S(1)} custom-call(f32[320,128]{1,0:T(8,128)S(1)} %copy-done.3, f32[320,128]{1,0:T(8,128)S(1)} %collective-permute-done.1.north.refs_1_.refs_6_, f32[416,128]{1,0:T(8,128)S(1)} %get-tuple-element.19.refs_2_.refs_3_.refs_7_, f32[416,128]{1,0:T(8,128)S(1)} %get-tuple-element.19.refs_2_.refs_3_.refs_7_, ...), custom_call_target="tpu_custom_call" | custom-call | bytes 40000000 | tf_op jit(solution)/shard_map/window1_from0/pallas_call | solution.py:390
  27.4 0.0 copy-start.4
  27.4 1.4 %collective-permute-start.2 = (f32[304,128]{1,0:T(8,128)S(1)}, f32[304,128]{1,0:T(8,128)S(1)}, u32[]{:S(2)}, u32[]{:S(2)}) collective-permute-start(f32[304,128]{1,0:T(8,128)S(1)} %window1_from0.1.refs_0_.refs_11_), channel_id=1, source_target_pairs={{32,0},{64,32},{96,64},{128,96},{160,128},{192,160},{224,192},{256... | collective-permute-start | bytes 466952 | tf_op jit(solution)/shard_map/ppermute | solution.py:405
  28.9 5.5 %collective-permute-done.3.refs_1_ = f32[1400,128]{1,0:T(8,128)S(1)} collective-permute-done((f32[1400,128]{1,0:T(8,128)}, f32[1400,128]{1,0:T(8,128)S(1)}, u32[]{:S(2)}, u32[]{:S(2)}) %collective-permute-start.3) | collective-permute-done | bytes 716832 | tf_op jit(solution)/shard_map/ppermute | solution.py:405
  34.4 3.7 %window1_from1.1.refs_0_ = f32[1400,128]{1,0:T(8,128)S(1)} custom-call(f32[1400,128]{1,0:T(8,128)S(1)} %copy-done.1, f32[1400,128]{1,0:T(8,128)S(1)} %collective-permute-done.3.refs_1_, f32[416,128]{1,0:T(8,128)S(1)} %get-tuple-element.19.refs_2_.refs_3_.refs_7_, f32[416,128]{1,0:T(8,128)S(1)} %get-tuple-element.19.refs_2_.refs_3_.refs_7_, ...), custom_call_target="tpu_custom_call" | custom-call | bytes 10000000 | tf_op jit(solution)/shard_map/window1_from1/pallas_call | solution.py:390
  38.1 0.0 copy-start.8
  38.1 0.0 collective-permute-done.2.refs_1_.refs_3_
  38.1 1.3 %collective-permute-start.4 = (f32[1400,128]{1,0:T(8,128)S(1)}, f32[1400,128]{1,0:T(8,128)S(1)}, u32[]{:S(2)}, u32[]{:S(2)}) collective-permute-start(f32[1400,128]{1,0:T(8,128)S(1)} %window1_from1.1.refs_0_), channel_id=1, source_target_pairs={{32,0},{64,32},{96,64},{128,96},{160,128},{192,160},{224,192},{256... | collective-permute-start | bytes 2150408 | tf_op jit(solution)/shard_map/ppermute | solution.py:405
  39.4 2.7 %window0_from0.1 = (bf16[8,200,128]{2,1,0:T(8,128)(2,1)}, f32[512,128]{1,0:T(8,128)S(1)}) custom-call(f32[304,128]{1,0:T(8,128)S(1)} %window1_from0.1.refs_0_.refs_11_, f32[304,128]{1,0:T(8,128)S(1)} %collective-permute-done.2.refs_1_.refs_3_, f32[200,128]{1,0:T(8,128)S(1)} %get-tuple-element.20.refs_11_.refs_2_, ...), custom_call_target="tpu_custom_call" | custom-call | bytes 10000000 | tf_op jit(solution)/shard_map/window0_from0/pallas_call | solution.py:390
  42.1 27.3 %all_to_all.23 = f32[16,32,128]{2,1,0:T(8,128)S(1)} all-to-all(f32[16,32,128]{2,1,0:T(8,128)S(1)} %bitcast.23), channel_id=1, replica_groups={{0,1,2,3,4,5,6,7,8,9,10,11,12,13,14,15},{16,17,18,19,20,21,22,23,24,25,..., dimensions={0} | all-to-all | bytes 524288 | tf_op jit(solution)/shard_map/all_to_all | solution.py:480
  69.4 0.6 add_16_parts.1
  70.0 15.3 %all-to-all-start.1 = ((f32[32,1,128]{2,1,0:T(1,128)}), f32[32,1,128]{2,1,0:T(1,128)S(1)}, u32[]{:S(2)}, u32[]{:S(2)}) async-start(f32[32,1,128]{2,1,0:T(1,128)} %bitcast.7), calls=%async_computation.1 | async-start | bytes 32768 | tf_op jit(solution)/shard_map/all_to_all | solution.py:483
  85.3 0.0 copy-start.7
  85.3 0.0 collective-permute-done.4.refs_1_
  85.3 0.7 copy-done.7
  85.9 4.5 %window0_from1.1 = bf16[8,200,128]{2,1,0:T(8,128)(2,1)} custom-call(f32[1400,128]{1,0:T(8,128)S(1)} %window1_from1.1.refs_0_, f32[1400,128]{1,0:T(8,128)S(1)} %collective-permute-done.4.refs_1_, f32[200,128]{1,0:T(8,128)S(1)} %get-tuple-element.20.refs_11_.refs_2_, ...), custom_call_target="tpu_custom_call", output_to_operand_aliasing={{}: (11, {})} | custom-call | bytes 10000000 | tf_op jit(solution)/shard_map/window0_from1/pallas_call | solution.py:390
  90.4 3.5 %all-to-all-done.1 = f32[32,1,128]{2,1,0:T(1,128)S(1)} async-done(((f32[32,1,128]{2,1,0:T(1,128)}), f32[32,1,128]{2,1,0:T(1,128)S(1)}, u32[]{:S(2)}, u32[]{:S(2)}) %all-to-all-start.1) | async-done | bytes 16416 | tf_op jit(solution)/shard_map/all_to_all | solution.py:483
  93.9 0.5 add_32_parts.1
  (12 shorter events, 0.0 us)
Async XLA Ops:
  3.5 9.9 %collective-permute-start = (f32[112,128]{1,0:T(8,128)}, f32[112,128]{1,0:T(8,128)S(1)}, u32[]{:S(2)}, u32[]{:S(2)}) collective-permute-start(f32[112,128]{1,0:T(8,128)} %get-tuple-element.17.first), channel_id=1, source_target_pairs={{1,0},{2,1},{3,2},{4,3},{5,4},{6,5},{7,6},{8,7},{9,8},{10,9},{11,1... | collective-permute-start | bytes 172040 | tf_op jit(solution)/shard_map/ppermute | solution.py:410
  14.0 7.7 %copy-start.9 = (bf16[3,8,100,100]{3,1,2,0:T(8,128)(2,1)S(1)}, bf16[3,8,100,100]{3,1,2,0:T(8,128)(2,1)}, u32[]{:S(2)}) copy-start(bf16[3,8,100,100]{3,1,2,0:T(8,128)(2,1)} %param.10) | copy-start | bytes 1440004
  14.1 6.4 %collective-permute-start.1 = (f32[320,128]{1,0:T(8,128)}, f32[320,128]{1,0:T(8,128)S(1)}, u32[]{:S(2)}, u32[]{:S(2)}) collective-permute-start(f32[320,128]{1,0:T(8,128)} %constant_dynamic-update-slice_fusion.refs_0_), channel_id=1, source_target_pairs={{32,0},{64,32},{96,64},{128,96},{160,128},{192,160},{224,192},{256... | collective-permute-start | bytes 491528 | tf_op jit(solution)/shard_map/ppermute | solution.py:405
  17.4 7.6 %copy-start = (bf16[2,8,100,2,128]{4,3,2,1,0:T(2,128)(2,1)S(1)}, bf16[2,8,100,2,128]{4,3,2,1,0:T(2,128)(2,1)}, u32[]{:S(2)}) copy-start(bf16[2,8,100,2,128]{4,3,2,1,0:T(2,128)(2,1)} %param.9) | copy-start | bytes 2457604
  20.4 13.9 %collective-permute-start.3 = (f32[1400,128]{1,0:T(8,128)}, f32[1400,128]{1,0:T(8,128)S(1)}, u32[]{:S(2)}, u32[]{:S(2)}) collective-permute-start(f32[1400,128]{1,0:T(8,128)} %rest.1.refs_0_), channel_id=1, source_target_pairs={{32,0},{64,32},{96,64},{128,96},{160,128},{192,160},{224,192},{256... | collective-permute-start | bytes 2150408 | tf_op jit(solution)/shard_map/ppermute | solution.py:405
  22.3 2.8 %copy-start.2 = (s32[8,2,128]{2,1,0:T(2,128)S(1)}, s32[8,2,128]{2,1,0:T(2,128)}, u32[]{:S(2)}) copy-start(s32[8,2,128]{2,1,0:T(2,128)} %refs_8_.7) | copy-start | bytes 24580
  22.3 2.8 %copy-start.3 = (f32[320,128]{1,0:T(8,128)S(1)}, f32[320,128]{1,0:T(8,128)}, u32[]{:S(2)}) copy-start(f32[320,128]{1,0:T(8,128)} %constant_dynamic-update-slice_fusion.refs_0_) | copy-start | bytes 491524
  22.3 2.8 %copy-start.6 = (f32[2,128]{1,0:T(2,128)S(1)}, f32[2,128]{1,0:T(2,128)}, u32[]{:S(2)}) copy-start(f32[2,128]{1,0:T(2,128)} %refs_5_.7) | copy-start | bytes 3076
  25.0 0.7 copy-start.5
  25.7 8.7 %copy-start.1 = (f32[1400,128]{1,0:T(8,128)S(1)}, f32[1400,128]{1,0:T(8,128)}, u32[]{:S(2)}) copy-start(f32[1400,128]{1,0:T(8,128)} %rest.1.refs_0_) | copy-start | bytes 2150404
  27.4 12.0 %copy-start.4 = (f32[100,2,128]{2,1,0:T(2,128)S(1)}, f32[100,2,128]{2,1,0:T(2,128)}, u32[]{:S(2)}) copy-start(f32[100,2,128]{2,1,0:T(2,128)} %param.13) | copy-start | bytes 307204
  27.4 10.7 %collective-permute-start.2 = (f32[304,128]{1,0:T(8,128)S(1)}, f32[304,128]{1,0:T(8,128)S(1)}, u32[]{:S(2)}, u32[]{:S(2)}) collective-permute-start(f32[304,128]{1,0:T(8,128)S(1)} %window1_from0.1.refs_0_.refs_11_), channel_id=1, source_target_pairs={{32,0},{64,32},{96,64},{128,96},{160,128},{192,160},{224,192},{256... | collective-permute-start | bytes 466952 | tf_op jit(solution)/shard_map/ppermute | solution.py:405
  38.1 1.3 %copy-start.8 = (s32[2,128]{1,0:T(2,128)S(1)}, s32[2,128]{1,0:T(2,128)}, u32[]{:S(2)}) copy-start(s32[2,128]{1,0:T(2,128)} %refs_13_.1) | copy-start | bytes 3076
  38.1 47.2 %collective-permute-start.4 = (f32[1400,128]{1,0:T(8,128)S(1)}, f32[1400,128]{1,0:T(8,128)S(1)}, u32[]{:S(2)}, u32[]{:S(2)}) collective-permute-start(f32[1400,128]{1,0:T(8,128)S(1)} %window1_from1.1.refs_0_), channel_id=1, source_target_pairs={{32,0},{64,32},{96,64},{128,96},{160,128},{192,160},{224,192},{256... | collective-permute-start | bytes 2150408 | tf_op jit(solution)/shard_map/ppermute | solution.py:405
  70.0 23.9 %all-to-all-start.1 = ((f32[32,1,128]{2,1,0:T(1,128)}), f32[32,1,128]{2,1,0:T(1,128)S(1)}, u32[]{:S(2)}, u32[]{:S(2)}) async-start(f32[32,1,128]{2,1,0:T(1,128)} %bitcast.7), calls=%async_computation.1 | async-start | bytes 32768 | tf_op jit(solution)/shard_map/all_to_all | solution.py:483
  85.3 0.7 copy-start.7

commit v7 on v5

--- a/solution.py
+++ b/solution.py
@@ -49,8 +49,6 @@
     grades = jnp.zeros((8, width), F32)
     for lev in range(levels):
         block = adj[lev].astype(F32)
-        if lev == 0:
-            first[0:rows] = block
         acc = place(acc, block, WIDE * lev)
         both = stiff[lev].astype(F32)
         grades = place(grades, tall(both[0:1]), WIDE * lev)
@@ -60,16 +58,15 @@
         acc = place(acc, state_s[lev].astype(F32), half // 2 + WIDE * lev)
     folded = folded_rows(rows)
     upper = jnp.concatenate([acc[folded:], jnp.zeros((2 * folded - rows, width), F32)], axis=0)
-    first[rows : rows + folded] = acc[0:folded] + pltpu.roll(upper, half, 1)
-    at = rows + folded
-    first[at : at + 2] = clon[...]
-    first[at + 2 : at + 4] = clat[...]
-    first[at + 4 : at + 8] = grades[0:4]
+    first[0:folded] = acc[0:folded] + pltpu.roll(upper, half, 1)
+    first[folded : folded + 2] = clon[...]
+    first[folded + 2 : folded + 4] = clat[...]
+    first[folded + 4 : folded + 8] = grades[0:4]
 
 
 def rest_kernel(adj, first, rest, *, rows):
-    for lev in range(1, adj.shape[0]):
-        rest[(lev - 1) * rows : lev * rows] = adj[lev].astype(F32)
+    for lev in range(adj.shape[0]):
+        rest[lev * rows : (lev + 1) * rows] = adj[lev].astype(F32)
 
 
 def pull(block, lane_from, lane_to, width):
@@ -85,12 +82,11 @@
     return {"lon": lon, "lat": lat, "keep": [1.0 - a - b for a, b in zip(lon, lat)]}
 
 
-def advected(own, north, west, corner, lev, start, cour):
+def advected(own, north, west, corner, base, start, cour):
     width = own.shape[1]
     spec = west.shape[0] // 2
     end = width - 1
     last = lanes((spec, width)) == end
-    base = lev * 2 * spec
 
     def pick(ref, first, parity):
         return ref[pl.ds(first + parity, spec, stride=2), :]
@@ -115,15 +111,15 @@
     return b0, b1
 
 
-def courant(clon, clat, north_c, west_c, rows):
-    width = clon.shape[1]
+def courant(own_c, north_c, west_c, rows):
+    width = own_c.shape[1]
+    at = folded_rows(rows)
 
     def edge(row):
         return pltpu.roll(tall(row), width - 1, 1)[0:1]
 
-    at = rows + folded_rows(rows)
-    lon = [clon[0:1], clon[1:2], north_c[at : at + 1]]
-    lat = [clat[0:1], clat[1:2], north_c[at + 2 : at + 3]]
+    lon = [own_c[at : at + 1], own_c[at + 1 : at + 2], north_c[at : at + 1]]
+    lat = [own_c[at + 2 : at + 3], own_c[at + 3 : at + 4], north_c[at + 2 : at + 3]]
     lon += [edge(west_c[rows : rows + 1]), edge(west_c[rows + 1 : rows + 2])]
     lat += [edge(west_c[rows + 2 : rows + 3]), edge(west_c[rows + 3 : rows + 4])]
     return with_keep(lon, lat)
@@ -226,11 +222,11 @@
 
 
 def window_kernel(
-    *refs, window, first_level, count, rows, last, grad, regions, near
+    *refs, window, first_level, count, rows, offset, last, grad, regions, near
 ):
     refs = list(refs)
-    own, north, west, corner_r, clon, clat, north_c, west_c, stiff, state_h, mats_h = refs[:11]
-    refs = refs[11:]
+    own, north, west, corner_r, own_c, north_c, west_c, stiff, state_h, mats_h = refs[:10]
+    refs = refs[10:]
     if grad:
         before, emission, region = refs[:3]
         refs = refs[3:]
@@ -246,24 +242,36 @@
         lam_out = refs.pop(0)
     x_s, y_s, flat_s, state_s, mats_s, sems = refs[:6]
     refs = refs[6:]
-    spec, width = rows // 2, clon.shape[1]
+    spec, width = rows // 2, own_c.shape[1]
     get_state = pltpu.make_async_copy(
         state_h.at[window, pl.ds(first_level, count)], state_s, sems.at[0]
     )
     get_mats = pltpu.make_async_copy(
         mats_h.at[:, pl.ds(first_level, count)], mats_s, sems.at[1]
     )
+    if not last and first_level == 0:
+        near_s = refs.pop(0)
+        gets = [
+            pltpu.make_async_copy(src.at[0:rows], near_s.at[i], sems.at[3 + i])
+            for i, src in enumerate((own, north))
+        ]
+        for get in gets:
+            get.start()
+        own, north = near_s.at[0], near_s.at[1]
     get_state.start()
     get_mats.start()
-    cour = courant(clon, clat, north_c, west_c, rows)
+    cour = courant(own_c, north_c, west_c, rows)
     if last:
         corner = corner_r[rows : rows + spec]
     else:
         corner = corner_r[pl.ds(rows + EXTRA, spec, stride=2), :]
     west_v = west.at[0:rows]
+    if not last and first_level == 0:
+        for get in gets:
+            get.wait()
     for lev in range(count):
         start = WIDE * (first_level + lev)
-        b0, b1 = advected(own, north, west_v, corner, lev, start, cour)
+        b0, b1 = advected(own, north, west_v, corner, offset + lev * rows, start, cour)
         x_s[lev, :, 0:width] = b0
         x_s[lev, :, width : 2 * width] = b1
     get_state.wait()
@@ -335,13 +343,15 @@
 def run_window(
     own, north, west, corner, shared, window, first_level, count, last, extra=None, prior=None, edge=None
 ):
-    clon, clat, north_c, west_c, stiff, state, mats = shared
+    own_c, north_c, west_c, stiff, state, mats = shared
     rows, width = state.shape[2], state.shape[3]
     spec = rows // 2
     grad = extra is not None
     regions, near = 0, 0
-    args = [own, north, west, corner, clon, clat, north_c, west_c, stiff, state, mats]
-    specs = [VMEM] * 9 + [ANY] * 2
+    args = [own, north, west, corner, own_c, north_c, west_c, stiff, state, mats]
+    offset = 0 if last else first_level * rows
+    sliced = not last and first_level == 0
+    specs = [ANY if sliced else VMEM] * 2 + [VMEM] * 6 + [ANY] * 2
     aliases = {}
     if grad:
         before, emission, region, regions, near = extra
@@ -372,16 +382,19 @@
         pltpu.VMEM((count, rows, width), F32),
         pltpu.VMEM((count, rows, width), BF16),
         pltpu.VMEM((STEPS, count, spec, spec), BF16),
-        pltpu.SemaphoreType.DMA((3,)),
+        pltpu.SemaphoreType.DMA((5,)),
     ]
     if last:
         scratch.append(pltpu.VMEM((count, rows, width), BF16))
+    if sliced:
+        scratch.append(pltpu.VMEM((2, rows, width), F32))
     body = functools.partial(
         window_kernel,
         window=window,
         first_level=first_level,
         count=count,
         rows=rows,
+        offset=offset,
         last=last,
         grad=grad,
         regions=regions,
@@ -420,27 +433,27 @@
     flat_state = state.reshape(windows, levels, rows, width)
     flat_em = emission.reshape(rows, width)
     mats = jnp.swapaxes(inverses, 2, 3)
-    low1 = pl.pallas_call(
+    first = pl.pallas_call(
         functools.partial(pack_kernel, rows=rows),
-        out_shape=jax.ShapeDtypeStruct((rows + folded_rows(rows) + EXTRA, width), F32),
+        out_shape=jax.ShapeDtypeStruct((folded_rows(rows) + EXTRA, width), F32),
         in_specs=[VMEM] * 4 + [HBM],
         out_specs=VMEM,
         scratch_shapes=[pltpu.VMEM((levels, rows, width), BF16), pltpu.SemaphoreType.DMA],
         name="pack",
         compiler_params=vmem(56),
     )(adj, courant_lon, courant_lat, stiffness, flat_state)
-    low1_n = to_north(low1)
-    rest1 = pl.pallas_call(
+    first_n = to_north(first)
+    full1 = pl.pallas_call(
         functools.partial(rest_kernel, rows=rows),
-        out_shape=jax.ShapeDtypeStruct(((levels - 1) * rows, width), F32),
+        out_shape=jax.ShapeDtypeStruct((levels * rows, width), F32),
         in_specs=[VMEM, ANY],
         out_specs=VMEM,
         name="rest",
         compiler_params=vmem(56),
-    )(adj, low1)
-    rest1, low1_n = lax.optimization_barrier((rest1, low1_n))
-    rest1_n = to_north(rest1)
-    west1_w = to_west(jnp.concatenate([low1[rows:], low1_n[rows:]], axis=0))
+    )(adj, first)
+    full1, first_n = lax.optimization_barrier((full1, first_n))
+    full1_n = to_north(full1)
+    west1_w = to_west(jnp.concatenate([first, first_n], axis=0))
     strip, both = pl.pallas_call(
         functools.partial(strip_kernel, rows=rows),
         out_shape=[
@@ -453,14 +466,14 @@
         cost_estimate=pl.CostEstimate(flops=0, transcendentals=0, bytes_accessed=40_000_000),
         compiler_params=vmem(8),
     )(west1_w, mats)
-    shared = (courant_lon, courant_lat, low1_n, both, stiffness, flat_state, mats)
+    shared = (first, first_n, both, stiffness, flat_state, mats)
     low0 = run_window(
-        low1, low1_n, both, both, shared, 1, 0, 1, False, edge=strip
+        full1, full1_n, both, both, shared, 1, 0, 1, False, edge=strip
     )[0]
     low0_n = to_north(low0)
-    rest1_n, low0 = lax.optimization_barrier((rest1_n, low0))
+    full1_n, low0 = lax.optimization_barrier((full1_n, low0))
     rest0 = run_window(
-        rest1, rest1_n, both, both, shared, 1, 1, levels - 1, False
+        full1, full1_n, both, both, shared, 1, 1, levels - 1, False
     )[0]
     low0_n, rest0 = lax.optimization_barrier((low0_n, rest0))
     rest0_n = to_north(rest0)

time: 88.8 us -> 96.9 us (1.091)
  blocking collectives: 24.7 us -> 29.9 us
  waiting for transfers between devices: 9.98 us -> 6.87 us
  Pallas kernels: 21.3 us -> 23.6 us
  local copies, waits for them, and re-layouts: 1.22 us -> 3.12 us
  starting transfers between devices: 30.3 us -> 31.9 us
    all_to_all x1, blocking collectives: 24.7 us -> 29.9 us  [per_device(): lax.all_to_all(partial, 'lon', 0, 0, axis_index_groups=line, tiled=True)]
    pallas_call x4, Pallas kernels: 12.5 us -> 14.9 us  [run_window(): pl.pallas_call(body, out_shape=out_shape, in_specs=specs, out_specs=out_s...]
    unnamed x19 -> x21, local copies, waits for them, and re-layouts: 1.21 us -> 3.12 us
    ppermute x4, waiting for transfers between devices: 5.43 us -> 3.9 us  [to_north(): return lax.ppermute(block, 'lat', [(i + 1, i) for i in range(bands - 1)])]
    all_to_all x1, starting transfers between devices: 14.9 us -> 16.4 us  [per_device(): lax.all_to_all(mine, ('lat', 'lon'), 0, 0, axis_index_groups=plane, tiled...]
    all_to_all x1, waiting for transfers between devices: 4.14 us -> 2.97 us  [per_device(): lax.all_to_all(mine, ('lat', 'lon'), 0, 0, axis_index_groups=plane, tiled...]
  transfers between devices with their start and end apart: 6 -> 6, of which waited for: 4 -> 3; matrix products, arithmetic and copies ran while one was open for 1% -> 2% of each run, Pallas kernels for 20% -> 19%
where the time goes in v7:
time: 96.9 us; the launch traced here: 96.3 us
  starting transfers between devices  31.9 us (33%)
  blocking collectives  29.9 us (31%)
  Pallas kernels  23.6 us (24%)
  waiting for transfers between devices  6.87 us (7%)
  local copies, waits for them, and re-layouts  3.12 us (3%)
    all_to_all x1, blocking collectives, per_device(): lax.all_to_all(partial, 'lon', 0, 0, axis_index_groups=line, tiled=True)  29.9 us
    all_to_all x1, starting transfers between devices, per_device(): lax.all_to_all(mine, ('lat', 'lon'), 0, 0, axis_index_groups=plane, tiled...  16.4 us
    pallas_call x4, Pallas kernels, run_window(): pl.pallas_call(body, out_shape=out_shape, in_specs=specs, out_specs=out_s...  14.9 us
    ppermute x1, starting transfers between devices, to_west(): lax.ppermute(block, 'lon', [((j + 1) % blocks, j) for j in range(blocks)])  10.1 us
    ppermute x4, starting transfers between devices, to_north(): return lax.ppermute(block, 'lat', [(i + 1, i) for i in range(bands - 1)])  5.41 us
    ppermute x4, waiting for transfers between devices, to_north(): return lax.ppermute(block, 'lat', [(i + 1, i) for i in range(bands - 1)])  3.9 us
    unnamed x21, local copies, waits for them, and re-layouts  3.12 us
    all_to_all x1, waiting for transfers between devices, per_device(): lax.all_to_all(mine, ('lat', 'lon'), 0, 0, axis_index_groups=plane, tiled...  2.97 us
  transfers between devices with their start and end apart: 6, of which 3 were waited for; matrix products, arithmetic and copies ran while one was open for 2% of the time, Pallas kernels for 19%

profile of v7, /device:TPU:1, one launch (start us, length us, event | category | flops | bytes accessed | tf_op | source)
XLA Modules:
  0.0 96.3 jit_solution(5223886111480281023)
XLA Ops:
  0.6 2.9 %pack.1.first.refs_4_ = f32[112,128]{1,0:T(8,128)} custom-call(bf16[8,200,128]{2,1,0:T(8,128)(2,1)} %bitcast.26, f32[2,128]{1,0:T(2,128)} %clon.1, f32[2,128]{1,0:T(2,128)} %clat.1, s32[8,2,128]{2,1,0:T(2,128)} %refs_7_.7, bf16[2,8,200,128]{3,2,1,0:T(8,128)(2,1)} %bitcast.17), custom_call_target="tpu_custom_call" | custom-call | tf_op jit(solution)/shard_map/pack/pallas_call | solution.py:436
  3.5 0.0 copy-start.2
  3.6 1.4 %collective-permute-start = (f32[112,128]{1,0:T(8,128)}, f32[112,128]{1,0:T(8,128)S(1)}, u32[]{:S(2)}, u32[]{:S(2)}) collective-permute-start(f32[112,128]{1,0:T(8,128)} %pack.1.first.refs_4_), channel_id=1, source_target_pairs={{32,0},{64,32},{96,64},{128,96},{160,128},{192,160},{224,192},{256... | collective-permute-start | bytes 172040 | tf_op jit(solution)/shard_map/ppermute | solution.py:418
  5.0 1.9 %rest.1.refs_0_ = f32[1600,128]{1,0:T(8,128)} custom-call(bf16[8,200,128]{2,1,0:T(8,128)(2,1)} %bitcast.27, f32[112,128]{1,0:T(8,128)} %pack.1.first.refs_4_), custom_call_target="tpu_custom_call" | custom-call | tf_op jit(solution)/shard_map/rest/pallas_call | solution.py:446
  6.9 2.5 %collective-permute-done.refs_5_ = f32[112,128]{1,0:T(8,128)S(1)} collective-permute-done((f32[112,128]{1,0:T(8,128)}, f32[112,128]{1,0:T(8,128)S(1)}, u32[]{:S(2)}, u32[]{:S(2)}) %collective-permute-start) | collective-permute-done | bytes 57376 | tf_op jit(solution)/shard_map/ppermute | solution.py:418
  9.4 1.3 %collective-permute-start.1 = (f32[1600,128]{1,0:T(8,128)}, f32[1600,128]{1,0:T(8,128)S(1)}, u32[]{:S(2)}, u32[]{:S(2)}) collective-permute-start(f32[1600,128]{1,0:T(8,128)} %rest.1.refs_0_), channel_id=1, source_target_pairs={{32,0},{64,32},{96,64},{128,96},{160,128},{192,160},{224,192},{256... | collective-permute-start | bytes 2457608 | tf_op jit(solution)/shard_map/ppermute | solution.py:418
  10.7 0.0 copy-done.2
  10.7 0.0 copy-start
  10.7 10.1 %collective-permute-start.2 = (f32[224,128]{1,0:T(8,128)S(1)}, f32[224,128]{1,0:T(8,128)S(1)}, u32[]{:S(2)}, u32[]{:S(2)}) collective-permute-start(f32[224,128]{1,0:T(8,128)S(1)} %pad_maximum_fusion), channel_id=1, source_target_pairs={{1,0},{2,1},{3,2},{4,3},{5,4},{6,5},{7,6},{8,7},{9,8},{10,9},{11,1... | collective-permute-start | bytes 344072 | tf_op jit(solution)/shard_map/ppermute | solution.py:423
  20.8 1.5 %copy.12 = bf16[3,8,100,100]{2,3,1,0:T(8,128)(2,1)S(1)} copy(bf16[3,8,100,100]{3,1,2,0:T(8,128)(2,1)} %param.10) | data formatting | bytes 960000 | tf_op args[2]
  22.3 0.0 collective-permute-done.2.packed
  22.3 0.0 copy-start.6
  22.4 0.6 copy-done.6
  23.0 0.9 copy-done.7
  23.9 2.7 %strip.1 = (f32[200,128]{1,0:T(8,128)S(1)}, f32[416,128]{1,0:T(8,128)S(1)}) custom-call(f32[224,128]{1,0:T(8,128)S(1)} %copy-done.7, bf16[3,8,100,100]{3,2,1,0:T(8,128)(2,1)S(1)} %bitcast.12), custom_call_target="tpu_custom_call" | custom-call | bytes 40000000 | tf_op jit(solution)/shard_map/strip/pallas_call | solution.py:457
  26.6 0.0 collective-permute-done.1.refs_1_
  26.7 2.1 %window1_from0.1.refs_0_.refs_10_ = f32[304,128]{1,0:T(8,128)S(1)} custom-call(f32[1600,128]{1,0:T(8,128)S(1)} %copy-done.1, f32[1600,128]{1,0:T(8,128)S(1)} %collective-permute-done.1.refs_1_, f32[416,128]{1,0:T(8,128)S(1)} %get-tuple-element.16.refs_2_.refs_3_.refs_6_, f32[416,128]{1,0:T(8,128)S(1)} %get-tuple-element.16.refs_2_.refs_3_.refs_6_, ...), custom_call_target="tpu_custom_call" | custom-call | bytes 40000000 | tf_op jit(solution)/shard_map/window1_from0/pallas_call | solution.py:403
  28.8 0.0 copy-start.8
  28.8 1.4 %collective-permute-start.3 = (f32[304,128]{1,0:T(8,128)S(1)}, f32[304,128]{1,0:T(8,128)S(1)}, u32[]{:S(2)}, u32[]{:S(2)}) collective-permute-start(f32[304,128]{1,0:T(8,128)S(1)} %window1_from0.1.refs_0_.refs_10_), channel_id=1, source_target_pairs={{32,0},{64,32},{96,64},{128,96},{160,128},{192,160},{224,192},{256... | collective-permute-start | bytes 466952 | tf_op jit(solution)/shard_map/ppermute | solution.py:418
  30.2 4.6 %window1_from1.1.refs_0_ = f32[1400,128]{1,0:T(8,128)} custom-call(f32[1600,128]{1,0:T(8,128)S(1)} %copy-done.1, f32[1600,128]{1,0:T(8,128)S(1)} %collective-permute-done.1.refs_1_, f32[416,128]{1,0:T(8,128)S(1)} %get-tuple-element.16.refs_2_.refs_3_.refs_6_, f32[416,128]{1,0:T(8,128)S(1)} %get-tuple-element.16.refs_2_.refs_3_.refs_6_, ...), custom_call_target="tpu_custom_call" | custom-call | bytes 10000000 | tf_op jit(solution)/shard_map/window1_from1/pallas_call | solution.py:403
  34.8 0.0 copy-start.9
  34.8 1.4 %collective-permute-done.3.refs_1_.refs_3_ = f32[304,128]{1,0:T(8,128)S(1)} collective-permute-done((f32[304,128]{1,0:T(8,128)S(1)}, f32[304,128]{1,0:T(8,128)S(1)}, u32[]{:S(2)}, u32[]{:S(2)}) %collective-permute-start.3) | collective-permute-done | bytes 155680 | tf_op jit(solution)/shard_map/ppermute | solution.py:418
  36.2 1.3 %collective-permute-start.4 = (f32[1400,128]{1,0:T(8,128)}, f32[1400,128]{1,0:T(8,128)S(1)}, u32[]{:S(2)}, u32[]{:S(2)}) collective-permute-start(f32[1400,128]{1,0:T(8,128)} %window1_from1.1.refs_0_), channel_id=1, source_target_pairs={{32,0},{64,32},{96,64},{128,96},{160,128},{192,160},{224,192},{256... | collective-permute-start | bytes 2150408 | tf_op jit(solution)/shard_map/ppermute | solution.py:418
  37.5 2.7 %window0_from0.1 = (bf16[8,200,128]{2,1,0:T(8,128)(2,1)}, f32[512,128]{1,0:T(8,128)S(1)}) custom-call(f32[304,128]{1,0:T(8,128)S(1)} %window1_from0.1.refs_0_.refs_10_, f32[304,128]{1,0:T(8,128)S(1)} %collective-permute-done.3.refs_1_.refs_3_, f32[200,128]{1,0:T(8,128)S(1)} %get-tuple-element.17.refs_10_.refs_2_, ...), custom_call_target="tpu_custom_call" | custom-call | bytes 10000000 | tf_op jit(solution)/shard_map/window0_from0/pallas_call | solution.py:403
  40.2 0.0 copy-done.3
  40.2 29.9 %all_to_all.23 = f32[16,32,128]{2,1,0:T(8,128)S(1)} all-to-all(f32[16,32,128]{2,1,0:T(8,128)S(1)} %bitcast.23), channel_id=1, replica_groups={{0,1,2,3,4,5,6,7,8,9,10,11,12,13,14,15},{16,17,18,19,20,21,22,23,24,25,..., dimensions={0} | all-to-all | bytes 524288 | tf_op jit(solution)/shard_map/all_to_all | solution.py:488
  70.1 0.6 add_16_parts.1
  70.7 16.4 %all-to-all-start.1 = ((f32[32,1,128]{2,1,0:T(1,128)}), f32[32,1,128]{2,1,0:T(1,128)S(1)}, u32[]{:S(2)}, u32[]{:S(2)}) async-start(f32[32,1,128]{2,1,0:T(1,128)} %bitcast.7), calls=%async_computation.1 | async-start | bytes 32768 | tf_op jit(solution)/shard_map/all_to_all | solution.py:491
  87.2 0.0 collective-permute-done.4.refs_1_
  87.2 5.6 %window0_from1.1 = bf16[8,200,128]{2,1,0:T(8,128)(2,1)} custom-call(f32[1400,128]{1,0:T(8,128)} %window1_from1.1.refs_0_, f32[1400,128]{1,0:T(8,128)S(1)} %collective-permute-done.4.refs_1_, f32[200,128]{1,0:T(8,128)S(1)} %get-tuple-element.17.refs_10_.refs_2_, f32[304,128]{1,0:T(8,128)S(1)} %copy-done.4, ...), custom_call_target="tpu_custom_call", output_to_operand_aliasing={{}: (10, {})} | custom-call | bytes 10000000 | tf_op jit(solution)/shard_map/window0_from1/pallas_call | solution.py:403
  92.8 3.0 %all-to-all-done.1 = f32[32,1,128]{2,1,0:T(1,128)S(1)} async-done(((f32[32,1,128]{2,1,0:T(1,128)}), f32[32,1,128]{2,1,0:T(1,128)S(1)}, u32[]{:S(2)}, u32[]{:S(2)}) %all-to-all-start.1) | async-done | bytes 16416 | tf_op jit(solution)/shard_map/all_to_all | solution.py:491
  95.8 0.5 add_32_parts.1
  (12 shorter events, 0.0 us)
Async XLA Ops:
  3.5 7.2 %copy-start.2 = (f32[112,128]{1,0:T(8,128)S(1)}, f32[112,128]{1,0:T(8,128)}, u32[]{:S(2)}) copy-start(f32[112,128]{1,0:T(8,128)} %pack.1.first.refs_4_) | copy-start | bytes 172036
  3.6 5.9 %collective-permute-start = (f32[112,128]{1,0:T(8,128)}, f32[112,128]{1,0:T(8,128)S(1)}, u32[]{:S(2)}, u32[]{:S(2)}) collective-permute-start(f32[112,128]{1,0:T(8,128)} %pack.1.first.refs_4_), channel_id=1, source_target_pairs={{32,0},{64,32},{96,64},{128,96},{160,128},{192,160},{224,192},{256... | collective-permute-start | bytes 172040 | tf_op jit(solution)/shard_map/ppermute | solution.py:418
  9.4 17.2 %collective-permute-start.1 = (f32[1600,128]{1,0:T(8,128)}, f32[1600,128]{1,0:T(8,128)S(1)}, u32[]{:S(2)}, u32[]{:S(2)}) collective-permute-start(f32[1600,128]{1,0:T(8,128)} %rest.1.refs_0_), channel_id=1, source_target_pairs={{32,0},{64,32},{96,64},{128,96},{160,128},{192,160},{224,192},{256... | collective-permute-start | bytes 2457608 | tf_op jit(solution)/shard_map/ppermute | solution.py:418
  10.7 15.9 %copy-start = (bf16[2,8,100,2,128]{4,3,2,1,0:T(2,128)(2,1)S(1)}, bf16[2,8,100,2,128]{4,3,2,1,0:T(2,128)(2,1)}, u32[]{:S(2)}) copy-start(bf16[2,8,100,2,128]{4,3,2,1,0:T(2,128)(2,1)} %param.9) | copy-start | bytes 2457604
  10.7 15.9 %copy-start.1 = (f32[1600,128]{1,0:T(8,128)S(1)}, f32[1600,128]{1,0:T(8,128)}, u32[]{:S(2)}) copy-start(f32[1600,128]{1,0:T(8,128)} %rest.1.refs_0_) | copy-start | bytes 2457604
  10.7 11.6 %collective-permute-start.2 = (f32[224,128]{1,0:T(8,128)S(1)}, f32[224,128]{1,0:T(8,128)S(1)}, u32[]{:S(2)}, u32[]{:S(2)}) collective-permute-start(f32[224,128]{1,0:T(8,128)S(1)} %pad_maximum_fusion), channel_id=1, source_target_pairs={{1,0},{2,1},{3,2},{4,3},{5,4},{6,5},{7,6},{8,7},{9,8},{10,9},{11,1... | collective-permute-start | bytes 344072 | tf_op jit(solution)/shard_map/ppermute | solution.py:423
  22.3 0.7 copy-start.6
  23.0 0.9 copy-start.7
  23.9 2.8 %copy-start.5 = (s32[8,2,128]{2,1,0:T(2,128)S(1)}, s32[8,2,128]{2,1,0:T(2,128)}, u32[]{:S(2)}) copy-start(s32[8,2,128]{2,1,0:T(2,128)} %refs_7_.7) | copy-start | bytes 24580
  28.8 8.8 %copy-start.8 = (f32[100,2,128]{2,1,0:T(2,128)S(1)}, f32[100,2,128]{2,1,0:T(2,128)}, u32[]{:S(2)}) copy-start(f32[100,2,128]{2,1,0:T(2,128)} %param.13) | copy-start | bytes 307204
  28.8 7.4 %collective-permute-start.3 = (f32[304,128]{1,0:T(8,128)S(1)}, f32[304,128]{1,0:T(8,128)S(1)}, u32[]{:S(2)}, u32[]{:S(2)}) collective-permute-start(f32[304,128]{1,0:T(8,128)S(1)} %window1_from0.1.refs_0_.refs_10_), channel_id=1, source_target_pairs={{32,0},{64,32},{96,64},{128,96},{160,128},{192,160},{224,192},{256... | collective-permute-start | bytes 466952 | tf_op jit(solution)/shard_map/ppermute | solution.py:418
  34.8 2.7 %copy-start.9 = (s32[2,128]{1,0:T(2,128)S(1)}, s32[2,128]{1,0:T(2,128)}, u32[]{:S(2)}) copy-start(s32[2,128]{1,0:T(2,128)} %refs_12_.1) | copy-start | bytes 3076
  36.2 4.0 %copy-start.3 = (f32[304,128]{1,0:T(8,128)}, f32[304,128]{1,0:T(8,128)S(1)}, u32[]{:S(2)}) copy-start(f32[304,128]{1,0:T(8,128)S(1)} %collective-permute-done.3.refs_1_.refs_3_) | copy-start | bytes 466948
  36.2 50.9 %collective-permute-start.4 = (f32[1400,128]{1,0:T(8,128)}, f32[1400,128]{1,0:T(8,128)S(1)}, u32[]{:S(2)}, u32[]{:S(2)}) collective-permute-start(f32[1400,128]{1,0:T(8,128)} %window1_from1.1.refs_0_), channel_id=1, source_target_pairs={{32,0},{64,32},{96,64},{128,96},{160,128},{192,160},{224,192},{256... | collective-permute-start | bytes 2150408 | tf_op jit(solution)/shard_map/ppermute | solution.py:418
  70.1 17.1 %copy-start.4 = (f32[304,128]{1,0:T(8,128)S(1)}, f32[304,128]{1,0:T(8,128)}, u32[]{:S(2)}) copy-start(f32[304,128]{1,0:T(8,128)} %copy-done.3) | copy-start | bytes 466948
  70.7 25.0 %all-to-all-start.1 = ((f32[32,1,128]{2,1,0:T(1,128)}), f32[32,1,128]{2,1,0:T(1,128)S(1)}, u32[]{:S(2)}, u32[]{:S(2)}) async-start(f32[32,1,128]{2,1,0:T(1,128)} %bitcast.7), calls=%async_computation.1 | async-start | bytes 32768 | tf_op jit(solution)/shard_map/all_to_all | solution.py:491

commit v8 on v5

--- a/solution.py
+++ b/solution.py
@@ -115,15 +115,15 @@
     return b0, b1
 
 
-def courant(clon, clat, north_c, west_c, rows):
-    width = clon.shape[1]
+def courant(own_c, north_c, west_c, rows):
+    width = own_c.shape[1]
+    at = rows + folded_rows(rows)
 
     def edge(row):
         return pltpu.roll(tall(row), width - 1, 1)[0:1]
 
-    at = rows + folded_rows(rows)
-    lon = [clon[0:1], clon[1:2], north_c[at : at + 1]]
-    lat = [clat[0:1], clat[1:2], north_c[at + 2 : at + 3]]
+    lon = [own_c[at : at + 1], own_c[at + 1 : at + 2], north_c[at : at + 1]]
+    lat = [own_c[at + 2 : at + 3], own_c[at + 3 : at + 4], north_c[at + 2 : at + 3]]
     lon += [edge(west_c[rows : rows + 1]), edge(west_c[rows + 1 : rows + 2])]
     lat += [edge(west_c[rows + 2 : rows + 3]), edge(west_c[rows + 3 : rows + 4])]
     return with_keep(lon, lat)
@@ -226,11 +226,11 @@
 
 
 def window_kernel(
-    *refs, window, first_level, count, rows, last, grad, regions, near
+    *refs, window, first_level, count, rows, last, grad, regions
 ):
     refs = list(refs)
-    own, north, west, corner_r, clon, clat, north_c, west_c, stiff, state_h, mats_h = refs[:11]
-    refs = refs[11:]
+    own, north, west, corner_r, own_c, north_c, west_c, stiff, state_h, mats_h = refs[:10]
+    refs = refs[10:]
     if grad:
         before, emission, region = refs[:3]
         refs = refs[3:]
@@ -246,7 +246,7 @@
         lam_out = refs.pop(0)
     x_s, y_s, flat_s, state_s, mats_s, sems = refs[:6]
     refs = refs[6:]
-    spec, width = rows // 2, clon.shape[1]
+    spec, width = rows // 2, own_c.shape[1]
     get_state = pltpu.make_async_copy(
         state_h.at[window, pl.ds(first_level, count)], state_s, sems.at[0]
     )
@@ -255,7 +255,7 @@
     )
     get_state.start()
     get_mats.start()
-    cour = courant(clon, clat, north_c, west_c, rows)
+    cour = courant(own_c, north_c, west_c, rows)
     if last:
         corner = corner_r[rows : rows + spec]
     else:
@@ -313,7 +313,6 @@
     put.start()
     if grad:
         ids = jnp.concatenate([region[0:1], region[1:2]], axis=1)
-        ids = (ids & (near - 1)) * (regions // near) + lax.shift_right_logical(ids, near.bit_length() - 1)
         labels = lax.broadcasted_iota(jnp.int32, (regions, 2 * width), 0)
         onehot = jnp.where(labels == ids, 1.0, 0.0).astype(BF16)
         total = []
@@ -335,16 +334,16 @@
 def run_window(
     own, north, west, corner, shared, window, first_level, count, last, extra=None, prior=None, edge=None
 ):
-    clon, clat, north_c, west_c, stiff, state, mats = shared
+    own_c, north_c, west_c, stiff, state, mats = shared
     rows, width = state.shape[2], state.shape[3]
     spec = rows // 2
     grad = extra is not None
-    regions, near = 0, 0
-    args = [own, north, west, corner, clon, clat, north_c, west_c, stiff, state, mats]
-    specs = [VMEM] * 9 + [ANY] * 2
+    regions = 0
+    args = [own, north, west, corner, own_c, north_c, west_c, stiff, state, mats]
+    specs = [VMEM] * 8 + [ANY] * 2
     aliases = {}
     if grad:
-        before, emission, region, regions, near = extra
+        before, emission, region, regions = extra
         args += [before, emission, region]
         specs += [VMEM] * 3
     if edge is not None:
@@ -385,7 +384,6 @@
         last=last,
         grad=grad,
         regions=regions,
-        near=near,
     )
     return pl.pallas_call(
         body,
@@ -396,7 +394,7 @@
         input_output_aliases=aliases,
         name=f"window{window}_from{first_level}",
         cost_estimate=pl.CostEstimate(flops=0, transcendentals=0, bytes_accessed=COST[window][first_level]),
-        compiler_params=vmem(40 if count > 1 else 8),
+        compiler_params=vmem((16 if not last else 56) if count > 1 else 8),
     )(*args)
 
 
@@ -453,7 +451,7 @@
         cost_estimate=pl.CostEstimate(flops=0, transcendentals=0, bytes_accessed=40_000_000),
         compiler_params=vmem(8),
     )(west1_w, mats)
-    shared = (courant_lon, courant_lat, low1_n, both, stiffness, flat_state, mats)
+    shared = (low1, low1_n, both, stiffness, flat_state, mats)
     low0 = run_window(
         low1, low1_n, both, both, shared, 1, 0, 1, False, edge=strip
     )[0]
@@ -464,25 +462,16 @@
     )[0]
     low0_n, rest0 = lax.optimization_barrier((low0_n, rest0))
     rest0_n = to_north(rest0)
-    bands, blocks = lax.axis_size("lat"), lax.axis_size("lon")
-    near = blocks // 2
-    far = regions // near
-    low_extra = (low0, flat_em, region_id, regions, near)
+    low_extra = (low0, flat_em, region_id, regions)
     out, partial = run_window(
         low0, low0_n, strip, low0_n, shared, 0, 0, 1, True, extra=low_extra
     )
-    line = [list(range(k * near, (k + 1) * near)) for k in range(2)]
-    lines = lax.all_to_all(partial, "lon", 0, 0, axis_index_groups=line, tiled=True)
-    mine = add_parts(lines, near)
-    plane = [list(range(k, regions, near)) for k in range(near)]
-    spread = lax.all_to_all(
-        mine, ("lat", "lon"), 0, 0, axis_index_groups=plane, tiled=True
-    )
+    spread = lax.all_to_all(partial, ("lat", "lon"), 0, 0, tiled=True)
     out = run_window(
         rest0, rest0_n, strip, low0_n, shared, 0, 1, levels - 1, True, prior=out
     )[0]
     out, spread = lax.optimization_barrier((out, spread))
-    grad = add_parts(spread, far)[:, :spec]
+    grad = add_parts(spread, regions)[:, :spec]
     return out.reshape(levels, spec, lat_rows, width), grad
 
 

time: 88.8 us -> 86.9 us (0.979)
  blocking collectives: 24.7 us -> 0 us
  starting transfers between devices: 30.3 us -> 44.8 us
  waiting for transfers between devices: 9.98 us -> 16.6 us
  Pallas kernels: 21.3 us -> 22.7 us
    all_to_all x1 -> x0, blocking collectives: 24.7 us -> none  [per_device(): lax.all_to_all(partial, 'lon', 0, 0, axis_index_groups=line, tiled=True)]
    all_to_all x1, starting transfers between devices: 14.9 us -> 29.4 us  [per_device(): spread = lax.all_to_all(partial, ('lat', 'lon'), 0, 0, tiled=True)]
    all_to_all x1, waiting for transfers between devices: 4.14 us -> 10.7 us  [per_device(): spread = lax.all_to_all(partial, ('lat', 'lon'), 0, 0, tiled=True)]
    pallas_call x4, Pallas kernels: 12.5 us -> 14.5 us  [run_window(): pl.pallas_call(body, out_shape=out_shape, in_specs=specs, out_specs=out_s...]
  transfers between devices with their start and end apart: 6 -> 6, of which waited for: 4 -> 4; matrix products, arithmetic and copies ran while one was open for 1% -> 1% of each run, Pallas kernels for 20% -> 22%
where the time goes in v8:
time: 86.9 us; the launch traced here: 86.4 us
  starting transfers between devices  44.8 us (52%)
  Pallas kernels  22.7 us (26%)
  waiting for transfers between devices  16.6 us (19%)
  local copies, waits for them, and re-layouts  1.5 us (2%)
  between operations  0.95 us (1%)
    all_to_all x1, starting transfers between devices, per_device(): spread = lax.all_to_all(partial, ('lat', 'lon'), 0, 0, tiled=True)  29.4 us
    pallas_call x4, Pallas kernels, run_window(): pl.pallas_call(body, out_shape=out_shape, in_specs=specs, out_specs=out_s...  14.5 us
    all_to_all x1, waiting for transfers between devices, per_device(): spread = lax.all_to_all(partial, ('lat', 'lon'), 0, 0, tiled=True)  10.7 us
    ppermute x1, starting transfers between devices, to_west(): lax.ppermute(block, 'lon', [((j + 1) % blocks, j) for j in range(blocks)])  9.94 us
    ppermute x4, waiting for transfers between devices, to_north(): return lax.ppermute(block, 'lat', [(i + 1, i) for i in range(bands - 1)])  5.46 us
    ppermute x4, starting transfers between devices, to_north(): return lax.ppermute(block, 'lat', [(i + 1, i) for i in range(bands - 1)])  5.41 us
    pallas_call x1, Pallas kernels, per_device(): pl.pallas_call(functools.partial(pack_kernel, rows=rows), out_shape=jax.S...  2.95 us
    pallas_call x1, Pallas kernels, per_device(): pl.pallas_call(functools.partial(strip_kernel, rows=rows), out_shape=[jax...  2.73 us
  transfers between devices with their start and end apart: 6, of which 4 were waited for; matrix products, arithmetic and copies ran while one was open for 1% of the time, Pallas kernels for 22%

profile of v8, /device:TPU:1, one launch (start us, length us, event | category | flops | bytes accessed | tf_op | source)
XLA Modules:
  0.0 86.4 jit_solution(12149641730316428154)
XLA Ops:
  0.6 2.9 %pack.1.first.refs_0_.refs_4_ = f32[312,128]{1,0:T(8,128)} custom-call(bf16[8,200,128]{2,1,0:T(8,128)(2,1)} %bitcast.22, f32[2,128]{1,0:T(2,128)} %clon.1, f32[2,128]{1,0:T(2,128)} %clat.1, s32[8,2,128]{2,1,0:T(2,128)} %refs_7_.7, bf16[2,8,200,128]{3,2,1,0:T(8,128)(2,1)} %bitcast.15), custom_call_target="tpu_custom_call" | custom-call | tf_op jit(solution)/shard_map/pack/pallas_call | solution.py:421
  3.6 0.0 copy-start.3
  3.6 0.0 copy-start.13
  3.6 1.4 %collective-permute-start = (f32[312,128]{1,0:T(8,128)}, f32[312,128]{1,0:T(8,128)S(1)}, u32[]{:S(2)}, u32[]{:S(2)}) collective-permute-start(f32[312,128]{1,0:T(8,128)} %pack.1.first.refs_0_.refs_4_), channel_id=1, source_target_pairs={{32,0},{64,32},{96,64},{128,96},{160,128},{192,160},{224,192},{256... | collective-permute-start | bytes 479240 | tf_op jit(solution)/shard_map/ppermute | solution.py:403
  5.0 1.9 %rest.1.refs_0_ = f32[1400,128]{1,0:T(8,128)} custom-call(bf16[8,200,128]{2,1,0:T(8,128)(2,1)} %bitcast.23, f32[312,128]{1,0:T(8,128)} %pack.1.first.refs_0_.refs_4_), custom_call_target="tpu_custom_call" | custom-call | tf_op jit(solution)/shard_map/rest/pallas_call | solution.py:431
  7.0 3.6 %collective-permute-done.refs_1_.refs_5_ = f32[312,128]{1,0:T(8,128)S(1)} collective-permute-done((f32[312,128]{1,0:T(8,128)}, f32[312,128]{1,0:T(8,128)S(1)}, u32[]{:S(2)}, u32[]{:S(2)}) %collective-permute-start) | collective-permute-done | bytes 159776 | tf_op jit(solution)/shard_map/ppermute | solution.py:403
  10.6 1.3 %collective-permute-start.3 = (f32[1400,128]{1,0:T(8,128)}, f32[1400,128]{1,0:T(8,128)S(1)}, u32[]{:S(2)}, u32[]{:S(2)}) collective-permute-start(f32[1400,128]{1,0:T(8,128)} %rest.1.refs_0_), channel_id=1, source_target_pairs={{32,0},{64,32},{96,64},{128,96},{160,128},{192,160},{224,192},{256... | collective-permute-start | bytes 2150408 | tf_op jit(solution)/shard_map/ppermute | solution.py:403
  11.9 0.0 copy-start.1
  11.9 9.9 %collective-permute-start.1 = (f32[224,128]{1,0:T(8,128)S(1)}, f32[224,128]{1,0:T(8,128)S(1)}, u32[]{:S(2)}, u32[]{:S(2)}) collective-permute-start(f32[224,128]{1,0:T(8,128)S(1)} %pad_maximum_fusion), channel_id=1, source_target_pairs={{1,0},{2,1},{3,2},{4,3},{5,4},{6,5},{7,6},{8,7},{9,8},{10,9},{11,1... | collective-permute-start | bytes 344072 | tf_op jit(solution)/shard_map/ppermute | solution.py:408
  21.9 0.5 copy.12
  22.4 0.4 collective-permute-done.1.packed
  22.8 2.7 %strip.1 = (f32[200,128]{1,0:T(8,128)S(1)}, f32[416,128]{1,0:T(8,128)S(1)}) custom-call(f32[224,128]{1,0:T(8,128)S(1)} %collective-permute-done.1.packed, bf16[3,8,100,100]{3,2,1,0:T(8,128)(2,1)S(1)} %bitcast.10), custom_call_target="tpu_custom_call" | custom-call | bytes 40000000 | tf_op jit(solution)/shard_map/strip/pallas_call | solution.py:442
  25.6 1.7 %window1_from0.1.refs_0_.refs_10_ = f32[304,128]{1,0:T(8,128)S(1)} custom-call(f32[312,128]{1,0:T(8,128)S(1)} %copy-done.3, f32[312,128]{1,0:T(8,128)S(1)} %collective-permute-done.refs_1_.refs_5_, f32[416,128]{1,0:T(8,128)S(1)} %get-tuple-element.15.refs_2_.refs_3_.refs_6_, f32[416,128]{1,0:T(8,128)S(1)} %get-tuple-element.15.refs_2_.refs_3_.refs_6_, ...), custom_call_target="tpu_custom_call" | custom-call | bytes 40000000 | tf_op jit(solution)/shard_map/window1_from0/pallas_call | solution.py:388
  27.3 0.0 copy-start.10
  27.3 1.4 %collective-permute-start.2 = (f32[304,128]{1,0:T(8,128)S(1)}, f32[304,128]{1,0:T(8,128)S(1)}, u32[]{:S(2)}, u32[]{:S(2)}) collective-permute-start(f32[304,128]{1,0:T(8,128)S(1)} %window1_from0.1.refs_0_.refs_10_), channel_id=1, source_target_pairs={{32,0},{64,32},{96,64},{128,96},{160,128},{192,160},{224,192},{256... | collective-permute-start | bytes 466952 | tf_op jit(solution)/shard_map/ppermute | solution.py:403
  28.8 0.0 collective-permute-done.3.refs_1_
  28.8 3.7 %window1_from1.1.refs_0_ = f32[1400,128]{1,0:T(8,128)S(1)} custom-call(f32[1400,128]{1,0:T(8,128)S(1)} %copy-done.6, f32[1400,128]{1,0:T(8,128)S(1)} %collective-permute-done.3.refs_1_, f32[416,128]{1,0:T(8,128)S(1)} %get-tuple-element.15.refs_2_.refs_3_.refs_6_, f32[416,128]{1,0:T(8,128)S(1)} %get-tuple-element.15.refs_2_.refs_3_.refs_6_, ...), custom_call_target="tpu_custom_call" | custom-call | bytes 10000000 | tf_op jit(solution)/shard_map/window1_from1/pallas_call | solution.py:388
  32.5 0.0 copy-start.11
  32.5 1.9 %collective-permute-done.2.refs_1_.refs_3_ = f32[304,128]{1,0:T(8,128)S(1)} collective-permute-done((f32[304,128]{1,0:T(8,128)S(1)}, f32[304,128]{1,0:T(8,128)S(1)}, u32[]{:S(2)}, u32[]{:S(2)}) %collective-permute-start.2) | collective-permute-done | bytes 155680 | tf_op jit(solution)/shard_map/ppermute | solution.py:403
  34.4 1.3 %collective-permute-start.4 = (f32[1400,128]{1,0:T(8,128)S(1)}, f32[1400,128]{1,0:T(8,128)S(1)}, u32[]{:S(2)}, u32[]{:S(2)}) collective-permute-start(f32[1400,128]{1,0:T(8,128)S(1)} %window1_from1.1.refs_0_), channel_id=1, source_target_pairs={{32,0},{64,32},{96,64},{128,96},{160,128},{192,160},{224,192},{256... | collective-permute-start | bytes 2150408 | tf_op jit(solution)/shard_map/ppermute | solution.py:403
  35.6 0.0 copy-done.4
  35.7 0.0 copy-done
  35.7 0.0 copy-done.2
  35.7 0.0 copy-done.8
  35.7 0.0 copy-done.10
  35.7 3.4 %window0_from0.1 = (bf16[8,200,128]{2,1,0:T(8,128)(2,1)}, f32[512,128]{1,0:T(8,128)}) custom-call(f32[304,128]{1,0:T(8,128)S(1)} %window1_from0.1.refs_0_.refs_10_, f32[304,128]{1,0:T(8,128)S(1)} %collective-permute-done.2.refs_1_.refs_3_, f32[200,128]{1,0:T(8,128)S(1)} %get-tuple-element.16.refs_10_.refs_2_, ...), custom_call_target="tpu_custom_call" | custom-call | bytes 10000000 | tf_op jit(solution)/shard_map/window0_from0/pallas_call | solution.py:388
  39.1 29.4 %all-to-all-start = ((f32[512,1,128]{2,1,0:T(1,128)}), f32[512,1,128]{2,1,0:T(1,128)S(1)}, u32[]{:S(2)}, u32[]{:S(2)}) async-start(f32[512,1,128]{2,1,0:T(1,128)} %bitcast.5), calls=%async_computation | async-start | bytes 524288 | tf_op jit(solution)/shard_map/all_to_all | solution.py:469
  68.5 0.0 collective-permute-done.4.refs_1_
  68.5 0.9 %copy-done.12 = f32[1400,128]{1,0:T(8,128)} copy-done((f32[1400,128]{1,0:T(8,128)}, f32[1400,128]{1,0:T(8,128)S(1)}, u32[]{:S(2)}) %copy-start.12) | copy-done | bytes 716824
  69.4 5.7 %window0_from1.1 = bf16[8,200,128]{2,1,0:T(8,128)(2,1)} custom-call(f32[1400,128]{1,0:T(8,128)} %copy-done.5, f32[1400,128]{1,0:T(8,128)} %copy-done.12, f32[200,128]{1,0:T(8,128)} %copy-done.8, f32[304,128]{1,0:T(8,128)} %copy-done.7, f32[312,128]{1,0:T(8,128)} %pack.1.first.refs_0_.refs_4_, f32[312,128]{1,0:T(8,128)} %copy-done.4, ...), custom_call_target="tpu_custom_call", output_to_operand_aliasing={{}: (10, {})} | custom-call | bytes 10000000 | tf_op jit(solution)/shard_map/window0_from1/pallas_call | solution.py:388
  75.1 10.7 %all-to-all-done = f32[512,1,128]{2,1,0:T(1,128)S(1)} async-done(((f32[512,1,128]{2,1,0:T(1,128)}), f32[512,1,128]{2,1,0:T(1,128)S(1)}, u32[]{:S(2)}, u32[]{:S(2)}) %all-to-all-start) | async-done | bytes 262176 | tf_op jit(solution)/shard_map/all_to_all | solution.py:469
  85.8 0.6 add_512_parts.1
  (20 shorter events, 0.1 us)
Async XLA Ops:
  3.6 8.3 %copy-start.3 = (f32[312,128]{1,0:T(8,128)S(1)}, f32[312,128]{1,0:T(8,128)}, u32[]{:S(2)}) copy-start(f32[312,128]{1,0:T(8,128)} %pack.1.first.refs_0_.refs_4_) | copy-start | bytes 479236
  3.6 18.3 %copy-start.13 = (bf16[3,8,100,100]{3,1,2,0:T(8,128)(2,1)S(1)}, bf16[3,8,100,100]{3,1,2,0:T(8,128)(2,1)}, u32[]{:S(2)}) copy-start(bf16[3,8,100,100]{3,1,2,0:T(8,128)(2,1)} %param.10) | copy-start | bytes 1440004
  3.6 6.9 %collective-permute-start = (f32[312,128]{1,0:T(8,128)}, f32[312,128]{1,0:T(8,128)S(1)}, u32[]{:S(2)}, u32[]{:S(2)}) collective-permute-start(f32[312,128]{1,0:T(8,128)} %pack.1.first.refs_0_.refs_4_), channel_id=1, source_target_pairs={{32,0},{64,32},{96,64},{128,96},{160,128},{192,160},{224,192},{256... | collective-permute-start | bytes 479240 | tf_op jit(solution)/shard_map/ppermute | solution.py:403
  10.6 25.1 %copy-start.4 = (f32[312,128]{1,0:T(8,128)}, f32[312,128]{1,0:T(8,128)S(1)}, u32[]{:S(2)}) copy-start(f32[312,128]{1,0:T(8,128)S(1)} %collective-permute-done.refs_1_.refs_5_) | copy-start | bytes 479236
  10.6 18.2 %collective-permute-start.3 = (f32[1400,128]{1,0:T(8,128)}, f32[1400,128]{1,0:T(8,128)S(1)}, u32[]{:S(2)}, u32[]{:S(2)}) collective-permute-start(f32[1400,128]{1,0:T(8,128)} %rest.1.refs_0_), channel_id=1, source_target_pairs={{32,0},{64,32},{96,64},{128,96},{160,128},{192,160},{224,192},{256... | collective-permute-start | bytes 2150408 | tf_op jit(solution)/shard_map/ppermute | solution.py:403
  11.9 13.7 %copy-start.1 = (bf16[2,8,100,2,128]{4,3,2,1,0:T(2,128)(2,1)S(1)}, bf16[2,8,100,2,128]{4,3,2,1,0:T(2,128)(2,1)}, u32[]{:S(2)}) copy-start(bf16[2,8,100,2,128]{4,3,2,1,0:T(2,128)(2,1)} %param.9) | copy-start | bytes 2457604
  11.9 10.9 %collective-permute-start.1 = (f32[224,128]{1,0:T(8,128)S(1)}, f32[224,128]{1,0:T(8,128)S(1)}, u32[]{:S(2)}, u32[]{:S(2)}) collective-permute-start(f32[224,128]{1,0:T(8,128)S(1)} %pad_maximum_fusion), channel_id=1, source_target_pairs={{1,0},{2,1},{3,2},{4,3},{5,4},{6,5},{7,6},{8,7},{9,8},{10,9},{11,1... | collective-permute-start | bytes 344072 | tf_op jit(solution)/shard_map/ppermute | solution.py:408
  22.4 13.3 %copy-start = (bf16[3,8,100,100]{2,3,1,0:T(8,128)(2,1)}, bf16[3,8,100,100]{2,3,1,0:T(8,128)(2,1)S(1)}, u32[]{:S(2)}) copy-start(bf16[3,8,100,100]{2,3,1,0:T(8,128)(2,1)S(1)} %copy.12) | copy-start | bytes 1440004
  22.8 2.8 %copy-start.9 = (s32[8,2,128]{2,1,0:T(2,128)S(1)}, s32[8,2,128]{2,1,0:T(2,128)}, u32[]{:S(2)}) copy-start(s32[8,2,128]{2,1,0:T(2,128)} %refs_7_.7) | copy-start | bytes 24580
  25.5 10.1 %copy-start.2 = (f32[416,128]{1,0:T(8,128)}, f32[416,128]{1,0:T(8,128)S(1)}, u32[]{:S(2)}) copy-start(f32[416,128]{1,0:T(8,128)S(1)} %get-tuple-element.15.refs_2_.refs_3_.refs_6_) | copy-start | bytes 638980
  25.5 10.1 %copy-start.8 = (f32[200,128]{1,0:T(8,128)}, f32[200,128]{1,0:T(8,128)S(1)}, u32[]{:S(2)}) copy-start(f32[200,128]{1,0:T(8,128)S(1)} %get-tuple-element.16.refs_10_.refs_2_) | copy-start | bytes 307204
  25.6 3.2 %copy-start.6 = (f32[1400,128]{1,0:T(8,128)S(1)}, f32[1400,128]{1,0:T(8,128)}, u32[]{:S(2)}) copy-start(f32[1400,128]{1,0:T(8,128)} %rest.1.refs_0_) | copy-start | bytes 2150404
  27.3 8.4 %copy-start.10 = (f32[100,2,128]{2,1,0:T(2,128)S(1)}, f32[100,2,128]{2,1,0:T(2,128)}, u32[]{:S(2)}) copy-start(f32[100,2,128]{2,1,0:T(2,128)} %param.13) | copy-start | bytes 307204
  27.3 7.0 %collective-permute-start.2 = (f32[304,128]{1,0:T(8,128)S(1)}, f32[304,128]{1,0:T(8,128)S(1)}, u32[]{:S(2)}, u32[]{:S(2)}) collective-permute-start(f32[304,128]{1,0:T(8,128)S(1)} %window1_from0.1.refs_0_.refs_10_), channel_id=1, source_target_pairs={{32,0},{64,32},{96,64},{128,96},{160,128},{192,160},{224,192},{256... | collective-permute-start | bytes 466952 | tf_op jit(solution)/shard_map/ppermute | solution.py:403
  32.5 6.6 %copy-start.5 = (f32[1400,128]{1,0:T(8,128)}, f32[1400,128]{1,0:T(8,128)S(1)}, u32[]{:S(2)}) copy-start(f32[1400,128]{1,0:T(8,128)S(1)} %window1_from1.1.refs_0_) | copy-start | bytes 2150404
  32.5 3.2 %copy-start.11 = (s32[2,128]{1,0:T(2,128)S(1)}, s32[2,128]{1,0:T(2,128)}, u32[]{:S(2)}) copy-start(s32[2,128]{1,0:T(2,128)} %refs_12_.1) | copy-start | bytes 3076
  34.4 4.7 %copy-start.7 = (f32[304,128]{1,0:T(8,128)}, f32[304,128]{1,0:T(8,128)S(1)}, u32[]{:S(2)}) copy-start(f32[304,128]{1,0:T(8,128)S(1)} %collective-permute-done.2.refs_1_.refs_3_) | copy-start | bytes 466948
  34.4 34.1 %collective-permute-start.4 = (f32[1400,128]{1,0:T(8,128)S(1)}, f32[1400,128]{1,0:T(8,128)S(1)}, u32[]{:S(2)}, u32[]{:S(2)}) collective-permute-start(f32[1400,128]{1,0:T(8,128)S(1)} %window1_from1.1.refs_0_), channel_id=1, source_target_pairs={{32,0},{64,32},{96,64},{128,96},{160,128},{192,160},{224,192},{256... | collective-permute-start | bytes 2150408 | tf_op jit(solution)/shard_map/ppermute | solution.py:403
  39.1 46.7 %all-to-all-start = ((f32[512,1,128]{2,1,0:T(1,128)}), f32[512,1,128]{2,1,0:T(1,128)S(1)}, u32[]{:S(2)}, u32[]{:S(2)}) async-start(f32[512,1,128]{2,1,0:T(1,128)} %bitcast.5), calls=%async_computation | async-start | bytes 524288 | tf_op jit(solution)/shard_map/all_to_all | solution.py:469
  68.5 0.9 %copy-start.12 = (f32[1400,128]{1,0:T(8,128)}, f32[1400,128]{1,0:T(8,128)S(1)}, u32[]{:S(2)}) copy-start(f32[1400,128]{1,0:T(8,128)S(1)} %collective-permute-done.4.refs_1_) | copy-start | bytes 2150404

commit v9 on v8

--- a/solution.py
+++ b/solution.py
@@ -129,18 +129,9 @@
     return with_keep(lon, lat)
 
 
-def strip_kernel(packed, mats, out, both, *, rows):
-    folded = folded_rows(rows)
-    for i in range(2):
-        src, dst = i * (folded + EXTRA), i * (rows + EXTRA)
-        block = packed[src : src + folded]
-        both[dst : dst + folded] = block
-        both[dst + folded : dst + rows] = pltpu.roll(block, block.shape[1] // 2, 1)[0 : rows - folded]
-        both[dst + rows : dst + rows + EXTRA] = packed[src + folded : src + folded + EXTRA]
-    west, diag = both.at[0 : rows + EXTRA], both.at[rows + EXTRA : 2 * (rows + EXTRA)]
-    spec, width = rows // 2, both.shape[1]
-    half = width // 2
-    levels = mats.shape[1]
+def strip_start(west, diag, levels, rows):
+    spec, width = rows // 2, west.shape[1]
+    half, quarter = width // 2, width // 4
     at = lanes((spec, width))
 
     def pick(ref, parity):
@@ -168,30 +159,63 @@
     b0 = mixed(cour, 0, a0, a1, right(a0))
     b1 = mixed(cour, 1, a1, a2, right(a1))
     value = jnp.where(at < half, b0, pltpu.roll(b1, half, 1))
-    quarter = half // 2
     factor = jnp.where(at < half, pltpu.roll(w0, width - quarter, 1), pltpu.roll(w1, quarter, 1))
-    live = west[rows + 4 : rows + 5]
-    group = (at & (half - 1)) // WIDE
-
-    def times(s, right_side):
-        low = right_side.astype(BF16)
-        acc = jnp.dot(mats[s, 0], low, preferred_element_type=F32)
-        for lev in range(1, levels):
-            prod = jnp.dot(mats[s, lev], low, preferred_element_type=F32)
-            acc = jnp.where(group == lev, prod, acc)
-        return acc
+    return value, factor, west[rows + 4 : rows + 5], (at & (half - 1)) // WIDE
+
+
+def first_kernel(
+    own, north, packed, stiff, state_h, mats_h, lam_out, strip_out, both,
+    x_s, y_s, flat_s, state_s, mats_s, sems, *, rows
+):
+    spec, width = rows // 2, own.shape[1]
+    levels, folded = mats_s.shape[1], folded_rows(rows)
+    get_state = pltpu.make_async_copy(state_h.at[state_h.shape[0] - 1, 0], state_s, sems.at[0])
+    get_mats = pltpu.make_async_copy(mats_h, mats_s, sems.at[1])
+    get_state.start()
+    get_mats.start()
+    for i in range(2):
+        src, dst = i * (folded + EXTRA), i * (rows + EXTRA)
+        block = packed[src : src + folded]
+        both[dst : dst + folded] = block
+        both[dst + folded : dst + rows] = pltpu.roll(block, width // 2, 1)[0 : rows - folded]
+        both[dst + rows : dst + rows + EXTRA] = packed[src + folded : src + folded + EXTRA]
+    west, diag = both.at[0 : rows + EXTRA], both.at[rows + EXTRA : 2 * (rows + EXTRA)]
+    value, factor, grade, group = strip_start(west, diag, levels, rows)
+    cour = courant(own, north, west, rows)
+    corner = diag[pl.ds(0, spec, stride=2), :]
+    b0, b1 = advected(own, north, both.at[0:rows], corner, 0, 0, cour)
+    x_s[:, 0:width] = b0
+    x_s[:, width : 2 * width] = b1
+    get_state.wait()
+    flat_s[...] = state_s[...].astype(F32)
+    y_s[:, 0:width] = flat_s[pl.ds(0, spec, stride=2), :]
+    y_s[:, width : 2 * width] = flat_s[pl.ds(1, spec, stride=2), :]
+    get_mats.wait()
+    live = jnp.concatenate([stiff[0][0:1], stiff[0][1:2]], axis=1)
 
     def stage(i, value):
         s = STEPS - 1 - i
-        one = times(s, value)
-        two = times(s, one * factor)
-        three = times(s, two * factor)
-        cand = 0.4 * value + 0.3 * one + 0.2 * two + 0.1 * three
-        return jnp.where(live > s.astype(F32), cand, value)
+        main, side = x_s[...].astype(BF16), value.astype(BF16)
+        cand, edge = 0.4 * x_s[...], 0.4 * value
+        for k, share in enumerate((0.3, 0.2, 0.1)):
+            prod = jnp.dot(mats_s[s, 0], main, preferred_element_type=F32)
+            part = jnp.dot(mats_s[s, 0], side, preferred_element_type=F32)
+            for lev in range(1, levels):
+                one = jnp.dot(mats_s[s, lev], side, preferred_element_type=F32)
+                part = jnp.where(group == lev, one, part)
+            cand, edge = cand + share * prod, edge + share * part
+            if k < 2:
+                main, side = (prod * y_s[...]).astype(BF16), (part * factor).astype(BF16)
+        x_s[...] = jnp.where(live > s, cand, x_s[...])
+        return jnp.where(grade > s.astype(F32), edge, value)
 
     value = lax.fori_loop(0, STEPS, stage, value)
-    out[pl.ds(0, spec, stride=2), :] = value
-    out[pl.ds(1, spec, stride=2), :] = pltpu.roll(value, half, 1)
+    for r in range(2):
+        lam_out[pl.ds(r, spec, stride=2), :] = x_s[:, r * width : (r + 1) * width]
+    lam_out[rows : rows + spec] = value
+    lam_out[rows + spec :] = jnp.zeros((TAIL - spec, width), F32)
+    strip_out[pl.ds(0, spec, stride=2), :] = value
+    strip_out[pl.ds(1, spec, stride=2), :] = pltpu.roll(value, width // 2, 1)
 
 
 def sum_kernel(parts, out, *, count):
@@ -236,8 +260,6 @@
         refs = refs[3:]
     if last and not grad:
         refs = refs[1:]
-    if not last and first_level == 0:
-        edge_r = refs.pop(0)
     if last:
         out_h = refs.pop(0)
         if grad:
@@ -253,6 +275,20 @@
     get_mats = pltpu.make_async_copy(
         mats_h.at[:, pl.ds(first_level, count)], mats_s, sems.at[1]
     )
+    gets = []
+    if not last:
+        own_s, north_s, level_sems = refs[:3]
+        for lev in range(count):
+            part = pl.ds(lev * rows, rows)
+            gets.append(
+                [
+                    pltpu.make_async_copy(src.at[part], dst.at[part], level_sems.at[i, lev])
+                    for i, (src, dst) in enumerate(((own, own_s), (north, north_s)))
+                ]
+            )
+            for get in gets[lev]:
+                get.start()
+        own, north = own_s, north_s
     get_state.start()
     get_mats.start()
     cour = courant(own_c, north_c, west_c, rows)
@@ -263,6 +299,8 @@
     west_v = west.at[0:rows]
     for lev in range(count):
         start = WIDE * (first_level + lev)
+        for get in gets[lev] if gets else ():
+            get.wait()
         b0, b1 = advected(own, north, west_v, corner, lev, start, cour)
         x_s[lev, :, 0:width] = b0
         x_s[lev, :, width : 2 * width] = b1
@@ -302,9 +340,6 @@
             else:
                 lam_out[pl.ds(lev * rows + r, spec, stride=2), :] = half
     if not last:
-        if first_level == 0:
-            lam_out[rows : rows + spec] = edge_r[pl.ds(0, spec, stride=2), :]
-            lam_out[rows + spec :] = jnp.zeros((TAIL - spec, width), F32)
         return
     out_s = refs.pop(0)
     for lev in range(count):
@@ -332,7 +367,7 @@
 
 
 def run_window(
-    own, north, west, corner, shared, window, first_level, count, last, extra=None, prior=None, edge=None
+    own, north, west, corner, shared, window, first_level, count, last, extra=None, prior=None
 ):
     own_c, north_c, west_c, stiff, state, mats = shared
     rows, width = state.shape[2], state.shape[3]
@@ -340,15 +375,12 @@
     grad = extra is not None
     regions = 0
     args = [own, north, west, corner, own_c, north_c, west_c, stiff, state, mats]
-    specs = [VMEM] * 8 + [ANY] * 2
+    specs = [VMEM if last else ANY] * 2 + [VMEM] * 6 + [ANY] * 2
     aliases = {}
     if grad:
         before, emission, region, regions = extra
         args += [before, emission, region]
         specs += [VMEM] * 3
-    if edge is not None:
-        args.append(edge)
-        specs.append(VMEM)
     if last:
         levels = state.shape[1]
         if not grad:
@@ -362,7 +394,7 @@
             out_specs.append(VMEM)
     else:
         out_shape = [
-            jax.ShapeDtypeStruct((count * rows + (0 if edge is None else TAIL), width), F32),
+            jax.ShapeDtypeStruct((count * rows, width), F32),
         ]
         out_specs = [VMEM]
     scratch = [
@@ -375,6 +407,9 @@
     ]
     if last:
         scratch.append(pltpu.VMEM((count, rows, width), BF16))
+    else:
+        scratch += [pltpu.VMEM((count * rows, width), F32)] * 2
+        scratch.append(pltpu.SemaphoreType.DMA((2, count)))
     body = functools.partial(
         window_kernel,
         window=window,
@@ -394,7 +429,7 @@
         input_output_aliases=aliases,
         name=f"window{window}_from{first_level}",
         cost_estimate=pl.CostEstimate(flops=0, transcendentals=0, bytes_accessed=COST[window][first_level]),
-        compiler_params=vmem((16 if not last else 56) if count > 1 else 8),
+        compiler_params=vmem((16 if last else 52) if count > 1 else 8),
     )(*args)
 
 
@@ -439,22 +474,28 @@
     rest1, low1_n = lax.optimization_barrier((rest1, low1_n))
     rest1_n = to_north(rest1)
     west1_w = to_west(jnp.concatenate([low1[rows:], low1_n[rows:]], axis=0))
-    strip, both = pl.pallas_call(
-        functools.partial(strip_kernel, rows=rows),
+    low0, strip, both = pl.pallas_call(
+        functools.partial(first_kernel, rows=rows),
         out_shape=[
+            jax.ShapeDtypeStruct((rows + TAIL, width), F32),
             jax.ShapeDtypeStruct((rows, width), F32),
             jax.ShapeDtypeStruct((2 * (rows + EXTRA), width), F32),
         ],
-        in_specs=[VMEM] * 2,
-        out_specs=[VMEM] * 2,
-        name="strip",
-        cost_estimate=pl.CostEstimate(flops=0, transcendentals=0, bytes_accessed=40_000_000),
+        in_specs=[VMEM] * 4 + [ANY] * 2,
+        out_specs=[VMEM] * 3,
+        scratch_shapes=[
+            pltpu.VMEM((spec, 2 * width), F32),
+            pltpu.VMEM((spec, 2 * width), F32),
+            pltpu.VMEM((rows, width), F32),
+            pltpu.VMEM((rows, width), BF16),
+            pltpu.VMEM((STEPS, levels, spec, spec), BF16),
+            pltpu.SemaphoreType.DMA((2,)),
+        ],
+        cost_estimate=pl.CostEstimate(flops=0, transcendentals=0, bytes_accessed=60_000_000),
+        name="first",
         compiler_params=vmem(8),
-    )(west1_w, mats)
+    )(low1, low1_n, west1_w, stiffness, flat_state, mats)
     shared = (low1, low1_n, both, stiffness, flat_state, mats)
-    low0 = run_window(
-        low1, low1_n, both, both, shared, 1, 0, 1, False, edge=strip
-    )[0]
     low0_n = to_north(low0)
     rest1_n, low0 = lax.optimization_barrier((rest1_n, low0))
     rest0 = run_window(

time: 86.9 us -> 89.2 us (1.026)
  starting transfers between devices: 44.8 us -> 46.4 us
  waiting for transfers between devices: 16.6 us -> 17.8 us
    all_to_all x1, starting transfers between devices: 29.4 us -> 31.2 us  [per_device(): spread = lax.all_to_all(partial, ('lat', 'lon'), 0, 0, tiled=True)]
    all_to_all x1, waiting for transfers between devices: 10.7 us -> 11.8 us  [per_device(): spread = lax.all_to_all(partial, ('lat', 'lon'), 0, 0, tiled=True)]
    pallas_call x4 -> x3, Pallas kernels: 14.5 us -> 13.8 us  [run_window(): pl.pallas_call(body, out_shape=out_shape, in_specs=specs, out_specs=out_s...]
  transfers between devices with their start and end apart: 6 -> 6, of which waited for: 4 -> 4; matrix products, arithmetic and copies ran while one was open for 1% -> 1% of each run, Pallas kernels for 22% -> 21%
where the time goes in v9:
time: 89.2 us; the launch traced here: 88.8 us
  starting transfers between devices  46.4 us (52%)
  Pallas kernels  22.5 us (25%)
  waiting for transfers between devices  17.8 us (20%)
  local copies, waits for them, and re-layouts  1.23 us (1%)
    all_to_all x1, starting transfers between devices, per_device(): spread = lax.all_to_all(partial, ('lat', 'lon'), 0, 0, tiled=True)  31.2 us
    pallas_call x3, Pallas kernels, run_window(): pl.pallas_call(body, out_shape=out_shape, in_specs=specs, out_specs=out_s...  13.8 us
    all_to_all x1, waiting for transfers between devices, per_device(): spread = lax.all_to_all(partial, ('lat', 'lon'), 0, 0, tiled=True)  11.8 us
    ppermute x1, starting transfers between devices, to_west(): lax.ppermute(block, 'lon', [((j + 1) % blocks, j) for j in range(blocks)])  9.94 us
    ppermute x4, waiting for transfers between devices, to_north(): return lax.ppermute(block, 'lat', [(i + 1, i) for i in range(bands - 1)])  5.66 us
    ppermute x4, starting transfers between devices, to_north(): return lax.ppermute(block, 'lat', [(i + 1, i) for i in range(bands - 1)])  5.28 us
    pallas_call x1, Pallas kernels, per_device(): pl.pallas_call(functools.partial(first_kernel, rows=rows), out_shape=[jax...  3.22 us
    pallas_call x1, Pallas kernels, per_device(): pl.pallas_call(functools.partial(pack_kernel, rows=rows), out_shape=jax.S...  2.94 us
  transfers between devices with their start and end apart: 6, of which 4 were waited for; matrix products, arithmetic and copies ran while one was open for 1% of the time, Pallas kernels for 21%

profile of v9, /device:TPU:1, one launch (start us, length us, event | category | flops | bytes accessed | tf_op | source)
XLA Modules:
  0.0 88.8 jit_solution(13812267059495428388)
XLA Ops:
  0.6 2.9 %pack.1.first.own.refs_4_ = f32[312,128]{1,0:T(8,128)} custom-call(bf16[8,200,128]{2,1,0:T(8,128)(2,1)} %bitcast.21, f32[2,128]{1,0:T(2,128)} %clon.1, f32[2,128]{1,0:T(2,128)} %clat.1, s32[8,2,128]{2,1,0:T(2,128)} %refs_7_.5, bf16[2,8,200,128]{3,2,1,0:T(8,128)(2,1)} %bitcast.10), custom_call_target="tpu_custom_call" | custom-call | tf_op jit(solution)/shard_map/pack/pallas_call | solution.py:456
  3.6 0.0 copy-start.2
  3.6 0.0 copy-start.6
  3.6 1.4 %collective-permute-start = (f32[312,128]{1,0:T(8,128)}, f32[312,128]{1,0:T(8,128)S(1)}, u32[]{:S(2)}, u32[]{:S(2)}) collective-permute-start(f32[312,128]{1,0:T(8,128)} %pack.1.first.own.refs_4_), channel_id=1, source_target_pairs={{32,0},{64,32},{96,64},{128,96},{160,128},{192,160},{224,192},{256... | collective-permute-start | bytes 479240 | tf_op jit(solution)/shard_map/ppermute | solution.py:438
  5.0 1.9 %rest.1.refs_0_ = f32[1400,128]{1,0:T(8,128)} custom-call(bf16[8,200,128]{2,1,0:T(8,128)(2,1)} %bitcast.22, f32[312,128]{1,0:T(8,128)} %pack.1.first.own.refs_4_), custom_call_target="tpu_custom_call" | custom-call | tf_op jit(solution)/shard_map/rest/pallas_call | solution.py:466
  7.0 3.6 %collective-permute-done.north.refs_5_ = f32[312,128]{1,0:T(8,128)S(1)} collective-permute-done((f32[312,128]{1,0:T(8,128)}, f32[312,128]{1,0:T(8,128)S(1)}, u32[]{:S(2)}, u32[]{:S(2)}) %collective-permute-start) | collective-permute-done | bytes 159776 | tf_op jit(solution)/shard_map/ppermute | solution.py:438
  10.6 1.3 %collective-permute-start.3 = (f32[1400,128]{1,0:T(8,128)}, f32[1400,128]{1,0:T(8,128)}, u32[]{:S(2)}, u32[]{:S(2)}) collective-permute-start(f32[1400,128]{1,0:T(8,128)} %rest.1.refs_0_), channel_id=1, source_target_pairs={{32,0},{64,32},{96,64},{128,96},{160,128},{192,160},{224,192},{256... | collective-permute-start | bytes 2150408 | tf_op jit(solution)/shard_map/ppermute | solution.py:438
  11.9 0.0 copy-start
  11.9 0.0 copy-start.3
  11.9 9.9 %collective-permute-start.1 = (f32[224,128]{1,0:T(8,128)S(1)}, f32[224,128]{1,0:T(8,128)S(1)}, u32[]{:S(2)}, u32[]{:S(2)}) collective-permute-start(f32[224,128]{1,0:T(8,128)S(1)} %pad_maximum_fusion), channel_id=1, source_target_pairs={{1,0},{2,1},{3,2},{4,3},{5,4},{6,5},{7,6},{8,7},{9,8},{10,9},{11,1... | collective-permute-start | bytes 344072 | tf_op jit(solution)/shard_map/ppermute | solution.py:443
  21.9 0.0 copy-done.6
  21.9 0.5 copy.12
  22.4 0.4 collective-permute-done.1.packed
  22.8 0.0 copy-done.3
  22.8 3.2 %first.1 = (f32[304,128]{1,0:T(8,128)S(1)}, f32[200,128]{1,0:T(8,128)S(1)}, f32[416,128]{1,0:T(8,128)S(1)}) custom-call(f32[312,128]{1,0:T(8,128)S(1)} %copy-done.2, f32[312,128]{1,0:T(8,128)S(1)} %collective-permute-done.north.refs_5_, f32[224,128]{1,0:T(8,128)S(1)} %collective-permute-done.1.packed, s32[8,2,128]{2,1,0:T(2,128)S(1)} %copy-done.3, ...), custom_call_target="tpu_custom_call" | custom-call | bytes 60000000 | tf_op jit(solution)/shard_map/first/pallas_call | solution.py:477
  26.1 1.3 %collective-permute-start.2 = (f32[304,128]{1,0:T(8,128)S(1)}, f32[304,128]{1,0:T(8,128)S(1)}, u32[]{:S(2)}, u32[]{:S(2)}) collective-permute-start(f32[304,128]{1,0:T(8,128)S(1)} %get-tuple-element.23.refs_0_.refs_10_), channel_id=1, source_target_pairs={{32,0},{64,32},{96,64},{128,96},{160,128},{192,160},{224,192},{256... | collective-permute-start | bytes 466952 | tf_op jit(solution)/shard_map/ppermute | solution.py:438
  27.4 0.0 collective-permute-done.3.refs_1_
  27.4 0.0 copy-start.1
  27.4 0.0 copy-start.4
  27.4 4.9 %window1_from1.1.refs_0_ = f32[1400,128]{1,0:T(8,128)S(1)} custom-call(f32[1400,128]{1,0:T(8,128)} %rest.1.refs_0_, f32[1400,128]{1,0:T(8,128)} %collective-permute-done.3.refs_1_, f32[416,128]{1,0:T(8,128)S(1)} %get-tuple-element.19.refs_2_.refs_3_.refs_6_, f32[416,128]{1,0:T(8,128)S(1)} %get-tuple-element.19.refs_2_.refs_3_.refs_6_, ...), custom_call_target="tpu_custom_call" | custom-call | bytes 10000000 | tf_op jit(solution)/shard_map/window1_from1/pallas_call | solution.py:423
  32.3 2.1 %collective-permute-done.2.refs_1_.refs_3_ = f32[304,128]{1,0:T(8,128)S(1)} collective-permute-done((f32[304,128]{1,0:T(8,128)S(1)}, f32[304,128]{1,0:T(8,128)S(1)}, u32[]{:S(2)}, u32[]{:S(2)}) %collective-permute-start.2) | collective-permute-done | bytes 155680 | tf_op jit(solution)/shard_map/ppermute | solution.py:438
  34.4 1.3 %collective-permute-start.4 = (f32[1400,128]{1,0:T(8,128)S(1)}, f32[1400,128]{1,0:T(8,128)}, u32[]{:S(2)}, u32[]{:S(2)}) collective-permute-start(f32[1400,128]{1,0:T(8,128)S(1)} %window1_from1.1.refs_0_), channel_id=1, source_target_pairs={{32,0},{64,32},{96,64},{128,96},{160,128},{192,160},{224,192},{256... | collective-permute-start | bytes 2150408 | tf_op jit(solution)/shard_map/ppermute | solution.py:438
  35.7 0.0 copy-start.5
  35.7 0.0 copy-done.1
  35.7 0.0 copy-done.4
  35.7 0.7 copy-done.5
  36.4 3.3 %window0_from0.1 = (bf16[8,200,128]{2,1,0:T(8,128)(2,1)}, f32[512,128]{1,0:T(8,128)}) custom-call(f32[304,128]{1,0:T(8,128)S(1)} %get-tuple-element.23.refs_0_.refs_10_, f32[304,128]{1,0:T(8,128)S(1)} %collective-permute-done.2.refs_1_.refs_3_, f32[200,128]{1,0:T(8,128)S(1)} %get-tuple-element.21.refs_2_, ...), custom_call_target="tpu_custom_call" | custom-call | bytes 10000000 | tf_op jit(solution)/shard_map/window0_from0/pallas_call | solution.py:423
  39.7 31.2 %all-to-all-start = ((f32[512,1,128]{2,1,0:T(1,128)}), f32[512,1,128]{2,1,0:T(1,128)S(1)}, u32[]{:S(2)}, u32[]{:S(2)}) async-start(f32[512,1,128]{2,1,0:T(1,128)} %bitcast.5), calls=%async_computation | async-start | bytes 524288 | tf_op jit(solution)/shard_map/all_to_all | solution.py:510
  70.9 0.0 collective-permute-done.4.refs_1_
  70.9 5.6 %window0_from1.1 = bf16[8,200,128]{2,1,0:T(8,128)(2,1)} custom-call(f32[1400,128]{1,0:T(8,128)S(1)} %window1_from1.1.refs_0_, f32[1400,128]{1,0:T(8,128)} %collective-permute-done.4.refs_1_, f32[200,128]{1,0:T(8,128)S(1)} %get-tuple-element.21.refs_2_, f32[304,128]{1,0:T(8,128)S(1)} %collective-permute-done.2.refs_1_.refs_3_, ...), custom_call_target="tpu_custom_call", output_to_operand_aliasing={{}: (10, {})} | custom-call | bytes 10000000 | tf_op jit(solution)/shard_map/window0_from1/pallas_call | solution.py:423
  76.5 11.8 %all-to-all-done = f32[512,1,128]{2,1,0:T(1,128)S(1)} async-done(((f32[512,1,128]{2,1,0:T(1,128)}), f32[512,1,128]{2,1,0:T(1,128)S(1)}, u32[]{:S(2)}, u32[]{:S(2)}) %all-to-all-start) | async-done | bytes 262176 | tf_op jit(solution)/shard_map/all_to_all | solution.py:510
  88.2 0.6 add_512_parts.1
  (5 shorter events, 0.0 us)
Async XLA Ops:
  3.6 8.3 %copy-start.2 = (f32[312,128]{1,0:T(8,128)S(1)}, f32[312,128]{1,0:T(8,128)}, u32[]{:S(2)}) copy-start(f32[312,128]{1,0:T(8,128)} %pack.1.first.own.refs_4_) | copy-start | bytes 479236
  3.6 18.3 %copy-start.6 = (bf16[3,8,100,100]{3,1,2,0:T(8,128)(2,1)S(1)}, bf16[3,8,100,100]{3,1,2,0:T(8,128)(2,1)}, u32[]{:S(2)}) copy-start(bf16[3,8,100,100]{3,1,2,0:T(8,128)(2,1)} %param.10) | copy-start | bytes 1440004
  3.6 6.9 %collective-permute-start = (f32[312,128]{1,0:T(8,128)}, f32[312,128]{1,0:T(8,128)S(1)}, u32[]{:S(2)}, u32[]{:S(2)}) collective-permute-start(f32[312,128]{1,0:T(8,128)} %pack.1.first.own.refs_4_), channel_id=1, source_target_pairs={{32,0},{64,32},{96,64},{128,96},{160,128},{192,160},{224,192},{256... | collective-permute-start | bytes 479240 | tf_op jit(solution)/shard_map/ppermute | solution.py:438
  10.6 16.8 %collective-permute-start.3 = (f32[1400,128]{1,0:T(8,128)}, f32[1400,128]{1,0:T(8,128)}, u32[]{:S(2)}, u32[]{:S(2)}) collective-permute-start(f32[1400,128]{1,0:T(8,128)} %rest.1.refs_0_), channel_id=1, source_target_pairs={{32,0},{64,32},{96,64},{128,96},{160,128},{192,160},{224,192},{256... | collective-permute-start | bytes 2150408 | tf_op jit(solution)/shard_map/ppermute | solution.py:438
  11.9 11.0 %copy-start = (bf16[2,8,100,2,128]{4,3,2,1,0:T(2,128)(2,1)S(1)}, bf16[2,8,100,2,128]{4,3,2,1,0:T(2,128)(2,1)}, u32[]{:S(2)}) copy-start(bf16[2,8,100,2,128]{4,3,2,1,0:T(2,128)(2,1)} %param.9) | copy-start | bytes 2457604
  11.9 10.9 %copy-start.3 = (s32[8,2,128]{2,1,0:T(2,128)S(1)}, s32[8,2,128]{2,1,0:T(2,128)}, u32[]{:S(2)}) copy-start(s32[8,2,128]{2,1,0:T(2,128)} %refs_7_.5) | copy-start | bytes 24580
  11.9 10.9 %collective-permute-start.1 = (f32[224,128]{1,0:T(8,128)S(1)}, f32[224,128]{1,0:T(8,128)S(1)}, u32[]{:S(2)}, u32[]{:S(2)}) collective-permute-start(f32[224,128]{1,0:T(8,128)S(1)} %pad_maximum_fusion), channel_id=1, source_target_pairs={{1,0},{2,1},{3,2},{4,3},{5,4},{6,5},{7,6},{8,7},{9,8},{10,9},{11,1... | collective-permute-start | bytes 344072 | tf_op jit(solution)/shard_map/ppermute | solution.py:443
  26.1 8.3 %collective-permute-start.2 = (f32[304,128]{1,0:T(8,128)S(1)}, f32[304,128]{1,0:T(8,128)S(1)}, u32[]{:S(2)}, u32[]{:S(2)}) collective-permute-start(f32[304,128]{1,0:T(8,128)S(1)} %get-tuple-element.23.refs_0_.refs_10_), channel_id=1, source_target_pairs={{32,0},{64,32},{96,64},{128,96},{160,128},{192,160},{224,192},{256... | collective-permute-start | bytes 466952 | tf_op jit(solution)/shard_map/ppermute | solution.py:438
  27.4 8.3 %copy-start.1 = (bf16[2,8,100,2,128]{4,3,2,1,0:T(2,128)(2,1)S(1)}, bf16[2,8,100,2,128]{4,3,2,1,0:T(2,128)(2,1)}, u32[]{:S(2)}) copy-start(bf16[2,8,100,2,128]{4,3,2,1,0:T(2,128)(2,1)} %param.9) | copy-start | bytes 2457604
  27.4 8.3 %copy-start.4 = (f32[100,2,128]{2,1,0:T(2,128)S(1)}, f32[100,2,128]{2,1,0:T(2,128)}, u32[]{:S(2)}) copy-start(f32[100,2,128]{2,1,0:T(2,128)} %param.13) | copy-start | bytes 307204
  34.4 36.5 %collective-permute-start.4 = (f32[1400,128]{1,0:T(8,128)S(1)}, f32[1400,128]{1,0:T(8,128)}, u32[]{:S(2)}, u32[]{:S(2)}) collective-permute-start(f32[1400,128]{1,0:T(8,128)S(1)} %window1_from1.1.refs_0_), channel_id=1, source_target_pairs={{32,0},{64,32},{96,64},{128,96},{160,128},{192,160},{224,192},{256... | collective-permute-start | bytes 2150408 | tf_op jit(solution)/shard_map/ppermute | solution.py:438
  35.7 0.7 copy-start.5
  39.7 48.5 %all-to-all-start = ((f32[512,1,128]{2,1,0:T(1,128)}), f32[512,1,128]{2,1,0:T(1,128)S(1)}, u32[]{:S(2)}, u32[]{:S(2)}) async-start(f32[512,1,128]{2,1,0:T(1,128)} %bitcast.5), calls=%async_computation | async-start | bytes 524288 | tf_op jit(solution)/shard_map/all_to_all | solution.py:510

commit v10 on v8

--- a/solution.py
+++ b/solution.py
@@ -40,11 +40,14 @@
     return -(-rows // 16) * 8
 
 
-def pack_kernel(adj, clon, clat, stiff, state_h, first, state_s, sem, *, rows):
+def fold(acc, rows):
+    width, folded = acc.shape[1], folded_rows(rows)
+    upper = jnp.concatenate([acc[folded:], jnp.zeros((2 * folded - rows, width), F32)], axis=0)
+    return acc[0:folded] + pltpu.roll(upper, width // 2, 1)
+
+
+def pack_kernel(adj, clon, clat, stiff, first, *, rows):
     levels, _, width = adj.shape
-    half = width // 2
-    get = pltpu.make_async_copy(state_h.at[state_h.shape[0] - 1], state_s, sem)
-    get.start()
     acc = jnp.zeros((rows, width), F32)
     grades = jnp.zeros((8, width), F32)
     for lev in range(levels):
@@ -54,22 +57,27 @@
         acc = place(acc, block, WIDE * lev)
         both = stiff[lev].astype(F32)
         grades = place(grades, tall(both[0:1]), WIDE * lev)
-        grades = place(grades, tall(both[1:2]), half + WIDE * lev)
-    get.wait()
-    for lev in range(levels):
-        acc = place(acc, state_s[lev].astype(F32), half // 2 + WIDE * lev)
-    folded = folded_rows(rows)
-    upper = jnp.concatenate([acc[folded:], jnp.zeros((2 * folded - rows, width), F32)], axis=0)
-    first[rows : rows + folded] = acc[0:folded] + pltpu.roll(upper, half, 1)
-    at = rows + folded
+        grades = place(grades, tall(both[1:2]), width // 2 + WIDE * lev)
+    at = rows + folded_rows(rows)
+    first[rows:at] = fold(acc, rows)
     first[at : at + 2] = clon[...]
     first[at + 2 : at + 4] = clat[...]
     first[at + 4 : at + 8] = grades[0:4]
 
 
-def rest_kernel(adj, first, rest, *, rows):
-    for lev in range(1, adj.shape[0]):
+def rest_kernel(adj, first, state_h, rest, west, state_s, sem, *, rows):
+    levels, _, width = adj.shape
+    get = pltpu.make_async_copy(state_h.at[state_h.shape[0] - 1], state_s, sem)
+    get.start()
+    for lev in range(1, levels):
         rest[(lev - 1) * rows : lev * rows] = adj[lev].astype(F32)
+    get.wait()
+    acc = jnp.zeros((rows, width), F32)
+    for lev in range(levels):
+        acc = place(acc, state_s[lev].astype(F32), width // 4 + WIDE * lev)
+    at = folded_rows(rows)
+    west[0:at] = first[rows : rows + at] + fold(acc, rows)
+    west[at:] = first[rows + at :]
 
 
 def pull(block, lane_from, lane_to, width):
@@ -421,24 +429,27 @@
     low1 = pl.pallas_call(
         functools.partial(pack_kernel, rows=rows),
         out_shape=jax.ShapeDtypeStruct((rows + folded_rows(rows) + EXTRA, width), F32),
-        in_specs=[VMEM] * 4 + [HBM],
+        in_specs=[VMEM] * 4,
         out_specs=VMEM,
-        scratch_shapes=[pltpu.VMEM((levels, rows, width), BF16), pltpu.SemaphoreType.DMA],
         name="pack",
         compiler_params=vmem(56),
-    )(adj, courant_lon, courant_lat, stiffness, flat_state)
+    )(adj, courant_lon, courant_lat, stiffness)
     low1_n = to_north(low1)
-    rest1 = pl.pallas_call(
+    rest1, west1 = pl.pallas_call(
         functools.partial(rest_kernel, rows=rows),
-        out_shape=jax.ShapeDtypeStruct(((levels - 1) * rows, width), F32),
-        in_specs=[VMEM, ANY],
-        out_specs=VMEM,
+        out_shape=[
+            jax.ShapeDtypeStruct(((levels - 1) * rows, width), F32),
+            jax.ShapeDtypeStruct((folded_rows(rows) + EXTRA, width), F32),
+        ],
+        in_specs=[VMEM] * 2 + [HBM],
+        out_specs=[VMEM] * 2,
+        scratch_shapes=[pltpu.VMEM((levels, rows, width), BF16), pltpu.SemaphoreType.DMA],
         name="rest",
         compiler_params=vmem(56),
-    )(adj, low1)
+    )(adj, low1, flat_state)
     rest1, low1_n = lax.optimization_barrier((rest1, low1_n))
     rest1_n = to_north(rest1)
-    west1_w = to_west(jnp.concatenate([low1[rows:], low1_n[rows:]], axis=0))
+    west1_w = to_west(jnp.concatenate([west1, low1_n[rows:]], axis=0))
     strip, both = pl.pallas_call(
         functools.partial(strip_kernel, rows=rows),
         out_shape=[

time: 86.9 us -> 85.8 us (0.987)
  waiting for transfers between devices: 16.6 us -> 15.5 us
    ppermute x4, waiting for transfers between devices: 5.46 us -> 4.38 us  [to_north(): return lax.ppermute(block, 'lat', [(i + 1, i) for i in range(bands - 1)])]
    pallas_call x1, Pallas kernels: 1.92 us -> 2.98 us  [per_device(): pl.pallas_call(functools.partial(rest_kernel, rows=rows), out_shape=[jax....]
    pallas_call x1, Pallas kernels: 2.95 us -> 1.93 us  [per_device(): pl.pallas_call(functools.partial(pack_kernel, rows=rows), out_shape=jax.S...]
  transfers between devices with their start and end apart: 6 -> 6, of which waited for: 4 -> 4; matrix products, arithmetic and copies ran while one was open for 1% -> 1% of each run, Pallas kernels for 22% -> 24%
where the time goes in v10:
time: 85.8 us; the launch traced here: 85.4 us
  starting transfers between devices  44.7 us (52%)
  Pallas kernels  22.7 us (26%)
  waiting for transfers between devices  15.5 us (18%)
  local copies, waits for them, and re-layouts  1.48 us (2%)
  between operations  0.94 us (1%)
    all_to_all x1, starting transfers between devices, per_device(): spread = lax.all_to_all(partial, ('lat', 'lon'), 0, 0, tiled=True)  29.5 us
    pallas_call x4, Pallas kernels, run_window(): pl.pallas_call(body, out_shape=out_shape, in_specs=specs, out_specs=out_s...  14.5 us
    all_to_all x1, waiting for transfers between devices, per_device(): spread = lax.all_to_all(partial, ('lat', 'lon'), 0, 0, tiled=True)  10.7 us
    ppermute x1, starting transfers between devices, to_west(): lax.ppermute(block, 'lon', [((j + 1) % blocks, j) for j in range(blocks)])  9.78 us
    ppermute x4, starting transfers between devices, to_north(): return lax.ppermute(block, 'lat', [(i + 1, i) for i in range(bands - 1)])  5.4 us
    ppermute x4, waiting for transfers between devices, to_north(): return lax.ppermute(block, 'lat', [(i + 1, i) for i in range(bands - 1)])  4.38 us
    pallas_call x1, Pallas kernels, per_device(): pl.pallas_call(functools.partial(rest_kernel, rows=rows), out_shape=[jax....  2.98 us
    pallas_call x1, Pallas kernels, per_device(): pl.pallas_call(functools.partial(strip_kernel, rows=rows), out_shape=[jax...  2.73 us
  transfers between devices with their start and end apart: 6, of which 4 were waited for; matrix products, arithmetic and copies ran while one was open for 1% of the time, Pallas kernels for 24%

profile of v10, /device:TPU:1, one launch (start us, length us, event | category | flops | bytes accessed | tf_op | source)
XLA Modules:
  0.0 85.4 jit_solution(13880178807098390139)
XLA Ops:
  0.6 1.9 %pack.1.first.refs_0_.refs_4_ = f32[312,128]{1,0:T(8,128)} custom-call(bf16[8,200,128]{2,1,0:T(8,128)(2,1)} %bitcast.22, f32[2,128]{1,0:T(2,128)} %clon.1, f32[2,128]{1,0:T(2,128)} %clat.1, s32[8,2,128]{2,1,0:T(2,128)} %refs_7_.7), custom_call_target="tpu_custom_call" | custom-call | tf_op jit(solution)/shard_map/pack/pallas_call | solution.py:429
  2.6 1.3 %collective-permute-start = (f32[312,128]{1,0:T(8,128)}, f32[312,128]{1,0:T(8,128)S(1)}, u32[]{:S(2)}, u32[]{:S(2)}) collective-permute-start(f32[312,128]{1,0:T(8,128)} %pack.1.first.refs_0_.refs_4_), channel_id=1, source_target_pairs={{32,0},{64,32},{96,64},{128,96},{160,128},{192,160},{224,192},{256... | collective-permute-start | bytes 479240 | tf_op jit(solution)/shard_map/ppermute | solution.py:411
  3.8 0.0 copy-start.13
  3.9 3.0 %rest.1 = (f32[1400,128]{1,0:T(8,128)}, f32[112,128]{1,0:T(8,128)}) custom-call(bf16[8,200,128]{2,1,0:T(8,128)(2,1)} %bitcast.23, f32[312,128]{1,0:T(8,128)} %pack.1.first.refs_0_.refs_4_, bf16[2,8,200,128]{3,2,1,0:T(8,128)(2,1)} %bitcast.15), custom_call_target="tpu_custom_call" | custom-call | tf_op jit(solution)/shard_map/rest/pallas_call | solution.py:438
  6.8 2.5 %collective-permute-done.refs_1_.refs_5_ = f32[312,128]{1,0:T(8,128)S(1)} collective-permute-done((f32[312,128]{1,0:T(8,128)}, f32[312,128]{1,0:T(8,128)S(1)}, u32[]{:S(2)}, u32[]{:S(2)}) %collective-permute-start) | collective-permute-done | bytes 159776 | tf_op jit(solution)/shard_map/ppermute | solution.py:411
  9.4 1.4 %collective-permute-start.3 = (f32[1400,128]{1,0:T(8,128)}, f32[1400,128]{1,0:T(8,128)S(1)}, u32[]{:S(2)}, u32[]{:S(2)}) collective-permute-start(f32[1400,128]{1,0:T(8,128)} %get-tuple-element.21.refs_0_), channel_id=1, source_target_pairs={{32,0},{64,32},{96,64},{128,96},{160,128},{192,160},{224,192},{256... | collective-permute-start | bytes 2150408 | tf_op jit(solution)/shard_map/ppermute | solution.py:411
  10.8 0.0 copy-done.14
  10.8 0.0 copy-start.1
  10.8 9.8 %collective-permute-start.1 = (f32[224,128]{1,0:T(8,128)S(1)}, f32[224,128]{1,0:T(8,128)S(1)}, u32[]{:S(2)}, u32[]{:S(2)}) collective-permute-start(f32[224,128]{1,0:T(8,128)S(1)} %pad_maximum_fusion), channel_id=1, source_target_pairs={{1,0},{2,1},{3,2},{4,3},{5,4},{6,5},{7,6},{8,7},{9,8},{10,9},{11,1... | collective-permute-start | bytes 344072 | tf_op jit(solution)/shard_map/ppermute | solution.py:416
  20.6 0.0 copy-done.13
  20.6 0.5 copy.12
  21.2 0.4 collective-permute-done.1.packed
  21.6 2.7 %strip.1 = (f32[200,128]{1,0:T(8,128)S(1)}, f32[416,128]{1,0:T(8,128)S(1)}) custom-call(f32[224,128]{1,0:T(8,128)S(1)} %collective-permute-done.1.packed, bf16[3,8,100,100]{3,2,1,0:T(8,128)(2,1)S(1)} %bitcast.10), custom_call_target="tpu_custom_call" | custom-call | bytes 40000000 | tf_op jit(solution)/shard_map/strip/pallas_call | solution.py:453
  24.3 0.0 copy-start.7
  24.4 1.7 %window1_from0.1.refs_0_.refs_10_ = f32[304,128]{1,0:T(8,128)S(1)} custom-call(f32[312,128]{1,0:T(8,128)S(1)} %copy-done.3, f32[312,128]{1,0:T(8,128)S(1)} %collective-permute-done.refs_1_.refs_5_, f32[416,128]{1,0:T(8,128)S(1)} %get-tuple-element.19.refs_2_.refs_3_.refs_6_, f32[416,128]{1,0:T(8,128)S(1)} %get-tuple-element.19.refs_2_.refs_3_.refs_6_, ...), custom_call_target="tpu_custom_call" | custom-call | bytes 40000000 | tf_op jit(solution)/shard_map/window1_from0/pallas_call | solution.py:396
  26.1 0.0 copy-start.10
  26.1 1.4 %collective-permute-start.2 = (f32[304,128]{1,0:T(8,128)S(1)}, f32[304,128]{1,0:T(8,128)S(1)}, u32[]{:S(2)}, u32[]{:S(2)}) collective-permute-start(f32[304,128]{1,0:T(8,128)S(1)} %window1_from0.1.refs_0_.refs_10_), channel_id=1, source_target_pairs={{32,0},{64,32},{96,64},{128,96},{160,128},{192,160},{224,192},{256... | collective-permute-start | bytes 466952 | tf_op jit(solution)/shard_map/ppermute | solution.py:411
  27.6 0.0 collective-permute-done.3.refs_1_
  27.6 0.0 copy-done.8
  27.6 3.7 %window1_from1.1.refs_0_ = f32[1400,128]{1,0:T(8,128)S(1)} custom-call(f32[1400,128]{1,0:T(8,128)S(1)} %copy-done.8, f32[1400,128]{1,0:T(8,128)S(1)} %collective-permute-done.3.refs_1_, f32[416,128]{1,0:T(8,128)S(1)} %get-tuple-element.19.refs_2_.refs_3_.refs_6_, f32[416,128]{1,0:T(8,128)S(1)} %get-tuple-element.19.refs_2_.refs_3_.refs_6_, ...), custom_call_target="tpu_custom_call" | custom-call | bytes 10000000 | tf_op jit(solution)/shard_map/window1_from1/pallas_call | solution.py:396
  31.3 0.0 copy-start.11
  31.3 1.9 %collective-permute-done.2.refs_1_.refs_3_ = f32[304,128]{1,0:T(8,128)S(1)} collective-permute-done((f32[304,128]{1,0:T(8,128)S(1)}, f32[304,128]{1,0:T(8,128)S(1)}, u32[]{:S(2)}, u32[]{:S(2)}) %collective-permute-start.2) | collective-permute-done | bytes 155680 | tf_op jit(solution)/shard_map/ppermute | solution.py:411
  33.1 1.3 %collective-permute-start.4 = (f32[1400,128]{1,0:T(8,128)S(1)}, f32[1400,128]{1,0:T(8,128)S(1)}, u32[]{:S(2)}, u32[]{:S(2)}) collective-permute-start(f32[1400,128]{1,0:T(8,128)S(1)} %window1_from1.1.refs_0_), channel_id=1, source_target_pairs={{32,0},{64,32},{96,64},{128,96},{160,128},{192,160},{224,192},{256... | collective-permute-start | bytes 2150408 | tf_op jit(solution)/shard_map/ppermute | solution.py:411
  34.5 3.4 %window0_from0.1 = (bf16[8,200,128]{2,1,0:T(8,128)(2,1)}, f32[512,128]{1,0:T(8,128)}) custom-call(f32[304,128]{1,0:T(8,128)S(1)} %window1_from0.1.refs_0_.refs_10_, f32[304,128]{1,0:T(8,128)S(1)} %collective-permute-done.2.refs_1_.refs_3_, f32[200,128]{1,0:T(8,128)S(1)} %get-tuple-element.20.refs_10_.refs_2_, ...), custom_call_target="tpu_custom_call" | custom-call | bytes 10000000 | tf_op jit(solution)/shard_map/window0_from0/pallas_call | solution.py:396
  37.9 0.0 copy-done.5
  37.9 0.0 copy-done.6
  37.9 29.5 %all-to-all-start = ((f32[512,1,128]{2,1,0:T(1,128)}), f32[512,1,128]{2,1,0:T(1,128)S(1)}, u32[]{:S(2)}, u32[]{:S(2)}) async-start(f32[512,1,128]{2,1,0:T(1,128)} %bitcast.5), calls=%async_computation | async-start | bytes 524288 | tf_op jit(solution)/shard_map/all_to_all | solution.py:480
  67.4 0.0 collective-permute-done.4.refs_1_
  67.5 0.9 %copy-done.12 = f32[1400,128]{1,0:T(8,128)} copy-done((f32[1400,128]{1,0:T(8,128)}, f32[1400,128]{1,0:T(8,128)S(1)}, u32[]{:S(2)}) %copy-start.12) | copy-done | bytes 716824
  68.3 5.7 %window0_from1.1 = bf16[8,200,128]{2,1,0:T(8,128)(2,1)} custom-call(f32[1400,128]{1,0:T(8,128)} %copy-done.5, f32[1400,128]{1,0:T(8,128)} %copy-done.12, f32[200,128]{1,0:T(8,128)} %copy-done.7, f32[304,128]{1,0:T(8,128)} %copy-done.6, f32[312,128]{1,0:T(8,128)} %pack.1.first.refs_0_.refs_4_, f32[312,128]{1,0:T(8,128)} %copy-done.4, ...), custom_call_target="tpu_custom_call", output_to_operand_aliasing={{}: (10, {})} | custom-call | bytes 10000000 | tf_op jit(solution)/shard_map/window0_from1/pallas_call | solution.py:396
  74.1 10.7 %all-to-all-done = f32[512,1,128]{2,1,0:T(1,128)S(1)} async-done(((f32[512,1,128]{2,1,0:T(1,128)}), f32[512,1,128]{2,1,0:T(1,128)S(1)}, u32[]{:S(2)}, u32[]{:S(2)}) %all-to-all-start) | async-done | bytes 262176 | tf_op jit(solution)/shard_map/all_to_all | solution.py:480
  84.8 0.6 add_512_parts.1
  (21 shorter events, 0.1 us)
Async XLA Ops:
  2.6 6.8 %collective-permute-start = (f32[312,128]{1,0:T(8,128)}, f32[312,128]{1,0:T(8,128)S(1)}, u32[]{:S(2)}, u32[]{:S(2)}) collective-permute-start(f32[312,128]{1,0:T(8,128)} %pack.1.first.refs_0_.refs_4_), channel_id=1, source_target_pairs={{32,0},{64,32},{96,64},{128,96},{160,128},{192,160},{224,192},{256... | collective-permute-start | bytes 479240 | tf_op jit(solution)/shard_map/ppermute | solution.py:411
  3.8 16.8 %copy-start.13 = (bf16[3,8,100,100]{3,1,2,0:T(8,128)(2,1)S(1)}, bf16[3,8,100,100]{3,1,2,0:T(8,128)(2,1)}, u32[]{:S(2)}) copy-start(bf16[3,8,100,100]{3,1,2,0:T(8,128)(2,1)} %param.10) | copy-start | bytes 1440004
  9.4 25.1 %copy-start.4 = (f32[312,128]{1,0:T(8,128)}, f32[312,128]{1,0:T(8,128)S(1)}, u32[]{:S(2)}) copy-start(f32[312,128]{1,0:T(8,128)S(1)} %collective-permute-done.refs_1_.refs_5_) | copy-start | bytes 479236
  9.4 1.4 %copy-start.14 = (f32[112,128]{1,0:T(8,128)S(1)}, f32[112,128]{1,0:T(8,128)}, u32[]{:S(2)}) copy-start(f32[112,128]{1,0:T(8,128)} %get-tuple-element.18) | copy-start | bytes 172036
  9.4 18.2 %collective-permute-start.3 = (f32[1400,128]{1,0:T(8,128)}, f32[1400,128]{1,0:T(8,128)S(1)}, u32[]{:S(2)}, u32[]{:S(2)}) collective-permute-start(f32[1400,128]{1,0:T(8,128)} %get-tuple-element.21.refs_0_), channel_id=1, source_target_pairs={{32,0},{64,32},{96,64},{128,96},{160,128},{192,160},{224,192},{256... | collective-permute-start | bytes 2150408 | tf_op jit(solution)/shard_map/ppermute | solution.py:411
  10.8 13.5 %copy-start.1 = (bf16[2,8,100,2,128]{4,3,2,1,0:T(2,128)(2,1)S(1)}, bf16[2,8,100,2,128]{4,3,2,1,0:T(2,128)(2,1)}, u32[]{:S(2)}) copy-start(bf16[2,8,100,2,128]{4,3,2,1,0:T(2,128)(2,1)} %param.9) | copy-start | bytes 2457604
  10.8 10.7 %collective-permute-start.1 = (f32[224,128]{1,0:T(8,128)S(1)}, f32[224,128]{1,0:T(8,128)S(1)}, u32[]{:S(2)}, u32[]{:S(2)}) collective-permute-start(f32[224,128]{1,0:T(8,128)S(1)} %pad_maximum_fusion), channel_id=1, source_target_pairs={{1,0},{2,1},{3,2},{4,3},{5,4},{6,5},{7,6},{8,7},{9,8},{10,9},{11,1... | collective-permute-start | bytes 344072 | tf_op jit(solution)/shard_map/ppermute | solution.py:416
  21.2 13.3 %copy-start = (bf16[3,8,100,100]{2,3,1,0:T(8,128)(2,1)}, bf16[3,8,100,100]{2,3,1,0:T(8,128)(2,1)S(1)}, u32[]{:S(2)}) copy-start(bf16[3,8,100,100]{2,3,1,0:T(8,128)(2,1)S(1)} %copy.12) | copy-start | bytes 1440004
  21.6 2.8 %copy-start.3 = (f32[312,128]{1,0:T(8,128)S(1)}, f32[312,128]{1,0:T(8,128)}, u32[]{:S(2)}) copy-start(f32[312,128]{1,0:T(8,128)} %pack.1.first.refs_0_.refs_4_) | copy-start | bytes 479236
  21.6 2.8 %copy-start.9 = (s32[8,2,128]{2,1,0:T(2,128)S(1)}, s32[8,2,128]{2,1,0:T(2,128)}, u32[]{:S(2)}) copy-start(s32[8,2,128]{2,1,0:T(2,128)} %refs_7_.7) | copy-start | bytes 24580
  24.3 10.1 %copy-start.2 = (f32[416,128]{1,0:T(8,128)}, f32[416,128]{1,0:T(8,128)S(1)}, u32[]{:S(2)}) copy-start(f32[416,128]{1,0:T(8,128)S(1)} %get-tuple-element.19.refs_2_.refs_3_.refs_6_) | copy-start | bytes 638980
  24.3 10.2 %copy-start.7 = (f32[200,128]{1,0:T(8,128)}, f32[200,128]{1,0:T(8,128)S(1)}, u32[]{:S(2)}) copy-start(f32[200,128]{1,0:T(8,128)S(1)} %get-tuple-element.20.refs_10_.refs_2_) | copy-start | bytes 307204
  24.4 3.2 %copy-start.8 = (f32[1400,128]{1,0:T(8,128)S(1)}, f32[1400,128]{1,0:T(8,128)}, u32[]{:S(2)}) copy-start(f32[1400,128]{1,0:T(8,128)} %get-tuple-element.21.refs_0_) | copy-start | bytes 2150404
  26.1 8.4 %copy-start.10 = (f32[100,2,128]{2,1,0:T(2,128)S(1)}, f32[100,2,128]{2,1,0:T(2,128)}, u32[]{:S(2)}) copy-start(f32[100,2,128]{2,1,0:T(2,128)} %param.13) | copy-start | bytes 307204
  26.1 7.0 %collective-permute-start.2 = (f32[304,128]{1,0:T(8,128)S(1)}, f32[304,128]{1,0:T(8,128)S(1)}, u32[]{:S(2)}, u32[]{:S(2)}) collective-permute-start(f32[304,128]{1,0:T(8,128)S(1)} %window1_from0.1.refs_0_.refs_10_), channel_id=1, source_target_pairs={{32,0},{64,32},{96,64},{128,96},{160,128},{192,160},{224,192},{256... | collective-permute-start | bytes 466952 | tf_op jit(solution)/shard_map/ppermute | solution.py:411
  31.3 6.6 %copy-start.5 = (f32[1400,128]{1,0:T(8,128)}, f32[1400,128]{1,0:T(8,128)S(1)}, u32[]{:S(2)}) copy-start(f32[1400,128]{1,0:T(8,128)S(1)} %window1_from1.1.refs_0_) | copy-start | bytes 2150404
  31.3 3.2 %copy-start.11 = (s32[2,128]{1,0:T(2,128)S(1)}, s32[2,128]{1,0:T(2,128)}, u32[]{:S(2)}) copy-start(s32[2,128]{1,0:T(2,128)} %refs_12_.1) | copy-start | bytes 3076
  33.1 4.7 %copy-start.6 = (f32[304,128]{1,0:T(8,128)}, f32[304,128]{1,0:T(8,128)S(1)}, u32[]{:S(2)}) copy-start(f32[304,128]{1,0:T(8,128)S(1)} %collective-permute-done.2.refs_1_.refs_3_) | copy-start | bytes 466948
  33.1 34.3 %collective-permute-start.4 = (f32[1400,128]{1,0:T(8,128)S(1)}, f32[1400,128]{1,0:T(8,128)S(1)}, u32[]{:S(2)}, u32[]{:S(2)}) collective-permute-start(f32[1400,128]{1,0:T(8,128)S(1)} %window1_from1.1.refs_0_), channel_id=1, source_target_pairs={{32,0},{64,32},{96,64},{128,96},{160,128},{192,160},{224,192},{256... | collective-permute-start | bytes 2150408 | tf_op jit(solution)/shard_map/ppermute | solution.py:411
  37.9 46.9 %all-to-all-start = ((f32[512,1,128]{2,1,0:T(1,128)}), f32[512,1,128]{2,1,0:T(1,128)S(1)}, u32[]{:S(2)}, u32[]{:S(2)}) async-start(f32[512,1,128]{2,1,0:T(1,128)} %bitcast.5), calls=%async_computation | async-start | bytes 524288 | tf_op jit(solution)/shard_map/all_to_all | solution.py:480
  67.4 0.9 %copy-start.12 = (f32[1400,128]{1,0:T(8,128)}, f32[1400,128]{1,0:T(8,128)S(1)}, u32[]{:S(2)}) copy-start(f32[1400,128]{1,0:T(8,128)S(1)} %collective-permute-done.4.refs_1_) | copy-start | bytes 2150404

commit v11 on v10

--- a/solution.py
+++ b/solution.py
@@ -46,11 +46,17 @@
     return acc[0:folded] + pltpu.roll(upper, width // 2, 1)
 
 
-def pack_kernel(adj, clon, clat, stiff, first, *, rows):
+def pack_kernel(adj_h, clon, clat, stiff, first, adj, sems, *, rows):
     levels, _, width = adj.shape
+    gets = [
+        pltpu.make_async_copy(adj_h.at[lev], adj.at[lev], sems.at[lev]) for lev in range(levels)
+    ]
+    for get in gets:
+        get.start()
     acc = jnp.zeros((rows, width), F32)
     grades = jnp.zeros((8, width), F32)
     for lev in range(levels):
+        gets[lev].wait()
         block = adj[lev].astype(F32)
         if lev == 0:
             first[0:rows] = block
@@ -274,6 +280,11 @@
         b0, b1 = advected(own, north, west_v, corner, lev, start, cour)
         x_s[lev, :, 0:width] = b0
         x_s[lev, :, width : 2 * width] = b1
+    if grad:
+        onehot = refs[1]
+        ids = jnp.concatenate([region[0:1], region[1:2]], axis=1)
+        labels = lax.broadcasted_iota(jnp.int32, (regions, 2 * width), 0)
+        onehot[...] = jnp.where(labels == ids, 1.0, 0.0).astype(BF16)
     get_state.wait()
     for lev in range(count):
         flat_s[lev] = state_s[lev].astype(F32)
@@ -320,9 +331,6 @@
     put = pltpu.make_async_copy(out_s, out_h.at[pl.ds(first_level, count)], sems.at[2])
     put.start()
     if grad:
-        ids = jnp.concatenate([region[0:1], region[1:2]], axis=1)
-        labels = lax.broadcasted_iota(jnp.int32, (regions, 2 * width), 0)
-        onehot = jnp.where(labels == ids, 1.0, 0.0).astype(BF16)
         total = []
         for r in range(2):
             now = flat_s[0, pl.ds(r, spec, stride=2), :]
@@ -333,7 +341,7 @@
         result = jnp.zeros((regions, width), F32)
         for piece in split3(contrib):
             result = result + lax.dot_general(
-                onehot, piece, (((1,), (1,)), ((), ())), preferred_element_type=F32
+                onehot[...], piece, (((1,), (1,)), ((), ())), preferred_element_type=F32
             )
         partial[...] = result
     put.wait()
@@ -383,6 +391,8 @@
     ]
     if last:
         scratch.append(pltpu.VMEM((count, rows, width), BF16))
+    if grad:
+        scratch.append(pltpu.VMEM((regions, 2 * width), BF16))
     body = functools.partial(
         window_kernel,
         window=window,
@@ -429,8 +439,12 @@
     low1 = pl.pallas_call(
         functools.partial(pack_kernel, rows=rows),
         out_shape=jax.ShapeDtypeStruct((rows + folded_rows(rows) + EXTRA, width), F32),
-        in_specs=[VMEM] * 4,
+        in_specs=[HBM] + [VMEM] * 3,
         out_specs=VMEM,
+        scratch_shapes=[
+            pltpu.VMEM((levels, rows, width), BF16),
+            pltpu.SemaphoreType.DMA((levels,)),
+        ],
         name="pack",
         compiler_params=vmem(56),
     )(adj, courant_lon, courant_lat, stiffness)

time: 85.8 us -> 87 us (1.014)
  Pallas kernels: 22.7 us -> 23.9 us
    pallas_call x1, Pallas kernels: 1.93 us -> 3.02 us  [per_device(): pl.pallas_call(functools.partial(pack_kernel, rows=rows), out_shape=jax.S...]
  transfers between devices with their start and end apart: 6 -> 6, of which waited for: 4 -> 4; matrix products, arithmetic and copies ran while one was open for 1% -> 1% of each run, Pallas kernels for 24% -> 23%
where the time goes in v11:
time: 87 us; the launch traced here: 86.5 us
  starting transfers between devices  44.7 us (51%)
  Pallas kernels  23.9 us (27%)
  waiting for transfers between devices  15.5 us (18%)
  local copies, waits for them, and re-layouts  1.48 us (2%)
  between operations  0.95 us (1%)
    all_to_all x1, starting transfers between devices, per_device(): spread = lax.all_to_all(partial, ('lat', 'lon'), 0, 0, tiled=True)  29.6 us
    pallas_call x4, Pallas kernels, run_window(): pl.pallas_call(body, out_shape=out_shape, in_specs=specs, out_specs=out_s...  14.5 us
    all_to_all x1, waiting for transfers between devices, per_device(): spread = lax.all_to_all(partial, ('lat', 'lon'), 0, 0, tiled=True)  10.7 us
    ppermute x1, starting transfers between devices, to_west(): lax.ppermute(block, 'lon', [((j + 1) % blocks, j) for j in range(blocks)])  9.78 us
    ppermute x4, starting transfers between devices, to_north(): return lax.ppermute(block, 'lat', [(i + 1, i) for i in range(bands - 1)])  5.41 us
    ppermute x4, waiting for transfers between devices, to_north(): return lax.ppermute(block, 'lat', [(i + 1, i) for i in range(bands - 1)])  4.39 us
    pallas_call x1, Pallas kernels, per_device(): pl.pallas_call(functools.partial(pack_kernel, rows=rows), out_shape=jax.S...  3.02 us
    pallas_call x1, Pallas kernels, per_device(): pl.pallas_call(functools.partial(rest_kernel, rows=rows), out_shape=[jax....  2.98 us
  transfers between devices with their start and end apart: 6, of which 4 were waited for; matrix products, arithmetic and copies ran while one was open for 1% of the time, Pallas kernels for 23%

profile of v11, /device:TPU:1, one launch (start us, length us, event | category | flops | bytes accessed | tf_op | source)
XLA Modules:
  0.0 86.5 jit_solution(1012652609930418559)
XLA Ops:
  0.6 3.0 %pack.1.first.refs_0_.refs_4_ = f32[312,128]{1,0:T(8,128)} custom-call(bf16[8,200,128]{2,1,0:T(8,128)(2,1)} %bitcast.22, f32[2,128]{1,0:T(2,128)} %clon.1, f32[2,128]{1,0:T(2,128)} %clat.1, s32[8,2,128]{2,1,0:T(2,128)} %refs_7_.7), custom_call_target="tpu_custom_call" | custom-call | tf_op jit(solution)/shard_map/pack/pallas_call | solution.py:439
  3.7 1.3 %collective-permute-start = (f32[312,128]{1,0:T(8,128)}, f32[312,128]{1,0:T(8,128)S(1)}, u32[]{:S(2)}, u32[]{:S(2)}) collective-permute-start(f32[312,128]{1,0:T(8,128)} %pack.1.first.refs_0_.refs_4_), channel_id=1, source_target_pairs={{32,0},{64,32},{96,64},{128,96},{160,128},{192,160},{224,192},{256... | collective-permute-start | bytes 479240 | tf_op jit(solution)/shard_map/ppermute | solution.py:421
  5.0 0.0 copy-start.13
  5.0 3.0 %rest.1 = (f32[1400,128]{1,0:T(8,128)}, f32[112,128]{1,0:T(8,128)}) custom-call(bf16[8,200,128]{2,1,0:T(8,128)(2,1)} %bitcast.23, f32[312,128]{1,0:T(8,128)} %pack.1.first.refs_0_.refs_4_, bf16[2,8,200,128]{3,2,1,0:T(8,128)(2,1)} %bitcast.15), custom_call_target="tpu_custom_call" | custom-call | tf_op jit(solution)/shard_map/rest/pallas_call | solution.py:452
  8.0 2.5 %collective-permute-done.refs_1_.refs_5_ = f32[312,128]{1,0:T(8,128)S(1)} collective-permute-done((f32[312,128]{1,0:T(8,128)}, f32[312,128]{1,0:T(8,128)S(1)}, u32[]{:S(2)}, u32[]{:S(2)}) %collective-permute-start) | collective-permute-done | bytes 159776 | tf_op jit(solution)/shard_map/ppermute | solution.py:421
  10.5 1.4 %collective-permute-start.3 = (f32[1400,128]{1,0:T(8,128)}, f32[1400,128]{1,0:T(8,128)S(1)}, u32[]{:S(2)}, u32[]{:S(2)}) collective-permute-start(f32[1400,128]{1,0:T(8,128)} %get-tuple-element.21.refs_0_), channel_id=1, source_target_pairs={{32,0},{64,32},{96,64},{128,96},{160,128},{192,160},{224,192},{256... | collective-permute-start | bytes 2150408 | tf_op jit(solution)/shard_map/ppermute | solution.py:421
  11.9 0.0 copy-start.1
  11.9 9.8 %collective-permute-start.1 = (f32[224,128]{1,0:T(8,128)S(1)}, f32[224,128]{1,0:T(8,128)S(1)}, u32[]{:S(2)}, u32[]{:S(2)}) collective-permute-start(f32[224,128]{1,0:T(8,128)S(1)} %pad_maximum_fusion), channel_id=1, source_target_pairs={{1,0},{2,1},{3,2},{4,3},{5,4},{6,5},{7,6},{8,7},{9,8},{10,9},{11,1... | collective-permute-start | bytes 344072 | tf_op jit(solution)/shard_map/ppermute | solution.py:426
  21.7 0.5 copy.12
  22.3 0.4 collective-permute-done.1.packed
  22.7 2.7 %strip.1 = (f32[200,128]{1,0:T(8,128)S(1)}, f32[416,128]{1,0:T(8,128)S(1)}) custom-call(f32[224,128]{1,0:T(8,128)S(1)} %collective-permute-done.1.packed, bf16[3,8,100,100]{3,2,1,0:T(8,128)(2,1)S(1)} %bitcast.10), custom_call_target="tpu_custom_call" | custom-call | bytes 40000000 | tf_op jit(solution)/shard_map/strip/pallas_call | solution.py:467
  25.4 0.0 copy-start.7
  25.4 0.0 copy-done.1
  25.4 0.0 copy-done.3
  25.5 0.0 copy-done.9
  25.5 0.0 copy-start.8
  25.5 1.7 %window1_from0.1.refs_0_.refs_10_ = f32[304,128]{1,0:T(8,128)S(1)} custom-call(f32[312,128]{1,0:T(8,128)S(1)} %copy-done.3, f32[312,128]{1,0:T(8,128)S(1)} %collective-permute-done.refs_1_.refs_5_, f32[416,128]{1,0:T(8,128)S(1)} %get-tuple-element.19.refs_2_.refs_3_.refs_6_, f32[416,128]{1,0:T(8,128)S(1)} %get-tuple-element.19.refs_2_.refs_3_.refs_6_, ...), custom_call_target="tpu_custom_call" | custom-call | bytes 40000000 | tf_op jit(solution)/shard_map/window1_from0/pallas_call | solution.py:406
  27.2 0.0 copy-start.10
  27.2 1.4 %collective-permute-start.2 = (f32[304,128]{1,0:T(8,128)S(1)}, f32[304,128]{1,0:T(8,128)S(1)}, u32[]{:S(2)}, u32[]{:S(2)}) collective-permute-start(f32[304,128]{1,0:T(8,128)S(1)} %window1_from0.1.refs_0_.refs_10_), channel_id=1, source_target_pairs={{32,0},{64,32},{96,64},{128,96},{160,128},{192,160},{224,192},{256... | collective-permute-start | bytes 466952 | tf_op jit(solution)/shard_map/ppermute | solution.py:421
  28.7 0.0 collective-permute-done.3.refs_1_
  28.7 3.7 %window1_from1.1.refs_0_ = f32[1400,128]{1,0:T(8,128)S(1)} custom-call(f32[1400,128]{1,0:T(8,128)S(1)} %copy-done.8, f32[1400,128]{1,0:T(8,128)S(1)} %collective-permute-done.3.refs_1_, f32[416,128]{1,0:T(8,128)S(1)} %get-tuple-element.19.refs_2_.refs_3_.refs_6_, f32[416,128]{1,0:T(8,128)S(1)} %get-tuple-element.19.refs_2_.refs_3_.refs_6_, ...), custom_call_target="tpu_custom_call" | custom-call | bytes 10000000 | tf_op jit(solution)/shard_map/window1_from1/pallas_call | solution.py:406
  32.4 0.0 copy-start.11
  32.4 1.9 %collective-permute-done.2.refs_1_.refs_3_ = f32[304,128]{1,0:T(8,128)S(1)} collective-permute-done((f32[304,128]{1,0:T(8,128)S(1)}, f32[304,128]{1,0:T(8,128)S(1)}, u32[]{:S(2)}, u32[]{:S(2)}) %collective-permute-start.2) | collective-permute-done | bytes 155680 | tf_op jit(solution)/shard_map/ppermute | solution.py:421
  34.3 1.3 %collective-permute-start.4 = (f32[1400,128]{1,0:T(8,128)S(1)}, f32[1400,128]{1,0:T(8,128)S(1)}, u32[]{:S(2)}, u32[]{:S(2)}) collective-permute-start(f32[1400,128]{1,0:T(8,128)S(1)} %window1_from1.1.refs_0_), channel_id=1, source_target_pairs={{32,0},{64,32},{96,64},{128,96},{160,128},{192,160},{224,192},{256... | collective-permute-start | bytes 2150408 | tf_op jit(solution)/shard_map/ppermute | solution.py:421
  35.5 0.0 copy-done.4
  35.6 3.4 %window0_from0.1 = (bf16[8,200,128]{2,1,0:T(8,128)(2,1)}, f32[512,128]{1,0:T(8,128)}) custom-call(f32[304,128]{1,0:T(8,128)S(1)} %window1_from0.1.refs_0_.refs_10_, f32[304,128]{1,0:T(8,128)S(1)} %collective-permute-done.2.refs_1_.refs_3_, f32[200,128]{1,0:T(8,128)S(1)} %get-tuple-element.20.refs_10_.refs_2_, ...), custom_call_target="tpu_custom_call" | custom-call | bytes 10000000 | tf_op jit(solution)/shard_map/window0_from0/pallas_call | solution.py:406
  39.0 29.6 %all-to-all-start = ((f32[512,1,128]{2,1,0:T(1,128)}), f32[512,1,128]{2,1,0:T(1,128)S(1)}, u32[]{:S(2)}, u32[]{:S(2)}) async-start(f32[512,1,128]{2,1,0:T(1,128)} %bitcast.5), calls=%async_computation | async-start | bytes 524288 | tf_op jit(solution)/shard_map/all_to_all | solution.py:494
  68.6 0.0 collective-permute-done.4.refs_1_
  68.6 0.9 %copy-done.12 = f32[1400,128]{1,0:T(8,128)} copy-done((f32[1400,128]{1,0:T(8,128)}, f32[1400,128]{1,0:T(8,128)S(1)}, u32[]{:S(2)}) %copy-start.12) | copy-done | bytes 716824
  69.5 5.7 %window0_from1.1 = bf16[8,200,128]{2,1,0:T(8,128)(2,1)} custom-call(f32[1400,128]{1,0:T(8,128)} %copy-done.5, f32[1400,128]{1,0:T(8,128)} %copy-done.12, f32[200,128]{1,0:T(8,128)} %copy-done.7, f32[304,128]{1,0:T(8,128)} %copy-done.6, f32[312,128]{1,0:T(8,128)} %pack.1.first.refs_0_.refs_4_, f32[312,128]{1,0:T(8,128)} %copy-done.4, ...), custom_call_target="tpu_custom_call", output_to_operand_aliasing={{}: (10, {})} | custom-call | bytes 10000000 | tf_op jit(solution)/shard_map/window0_from1/pallas_call | solution.py:406
  75.2 10.7 %all-to-all-done = f32[512,1,128]{2,1,0:T(1,128)S(1)} async-done(((f32[512,1,128]{2,1,0:T(1,128)}), f32[512,1,128]{2,1,0:T(1,128)S(1)}, u32[]{:S(2)}, u32[]{:S(2)}) %all-to-all-start) | async-done | bytes 262176 | tf_op jit(solution)/shard_map/all_to_all | solution.py:494
  85.9 0.6 add_512_parts.1
  (21 shorter events, 0.1 us)
Async XLA Ops:
  3.7 6.8 %collective-permute-start = (f32[312,128]{1,0:T(8,128)}, f32[312,128]{1,0:T(8,128)S(1)}, u32[]{:S(2)}, u32[]{:S(2)}) collective-permute-start(f32[312,128]{1,0:T(8,128)} %pack.1.first.refs_0_.refs_4_), channel_id=1, source_target_pairs={{32,0},{64,32},{96,64},{128,96},{160,128},{192,160},{224,192},{256... | collective-permute-start | bytes 479240 | tf_op jit(solution)/shard_map/ppermute | solution.py:421
  5.0 16.8 %copy-start.13 = (bf16[3,8,100,100]{3,1,2,0:T(8,128)(2,1)S(1)}, bf16[3,8,100,100]{3,1,2,0:T(8,128)(2,1)}, u32[]{:S(2)}) copy-start(bf16[3,8,100,100]{3,1,2,0:T(8,128)(2,1)} %param.10) | copy-start | bytes 1440004
  10.5 25.1 %copy-start.4 = (f32[312,128]{1,0:T(8,128)}, f32[312,128]{1,0:T(8,128)S(1)}, u32[]{:S(2)}) copy-start(f32[312,128]{1,0:T(8,128)S(1)} %collective-permute-done.refs_1_.refs_5_) | copy-start | bytes 479236
  10.5 1.4 %copy-start.14 = (f32[112,128]{1,0:T(8,128)S(1)}, f32[112,128]{1,0:T(8,128)}, u32[]{:S(2)}) copy-start(f32[112,128]{1,0:T(8,128)} %get-tuple-element.18) | copy-start | bytes 172036
  10.5 18.2 %collective-permute-start.3 = (f32[1400,128]{1,0:T(8,128)}, f32[1400,128]{1,0:T(8,128)S(1)}, u32[]{:S(2)}, u32[]{:S(2)}) collective-permute-start(f32[1400,128]{1,0:T(8,128)} %get-tuple-element.21.refs_0_), channel_id=1, source_target_pairs={{32,0},{64,32},{96,64},{128,96},{160,128},{192,160},{224,192},{256... | collective-permute-start | bytes 2150408 | tf_op jit(solution)/shard_map/ppermute | solution.py:421
  11.9 13.5 %copy-start.1 = (bf16[2,8,100,2,128]{4,3,2,1,0:T(2,128)(2,1)S(1)}, bf16[2,8,100,2,128]{4,3,2,1,0:T(2,128)(2,1)}, u32[]{:S(2)}) copy-start(bf16[2,8,100,2,128]{4,3,2,1,0:T(2,128)(2,1)} %param.9) | copy-start | bytes 2457604
  11.9 10.7 %collective-permute-start.1 = (f32[224,128]{1,0:T(8,128)S(1)}, f32[224,128]{1,0:T(8,128)S(1)}, u32[]{:S(2)}, u32[]{:S(2)}) collective-permute-start(f32[224,128]{1,0:T(8,128)S(1)} %pad_maximum_fusion), channel_id=1, source_target_pairs={{1,0},{2,1},{3,2},{4,3},{5,4},{6,5},{7,6},{8,7},{9,8},{10,9},{11,1... | collective-permute-start | bytes 344072 | tf_op jit(solution)/shard_map/ppermute | solution.py:426
  22.3 13.3 %copy-start = (bf16[3,8,100,100]{2,3,1,0:T(8,128)(2,1)}, bf16[3,8,100,100]{2,3,1,0:T(8,128)(2,1)S(1)}, u32[]{:S(2)}) copy-start(bf16[3,8,100,100]{2,3,1,0:T(8,128)(2,1)S(1)} %copy.12) | copy-start | bytes 1440004
  22.7 2.8 %copy-start.3 = (f32[312,128]{1,0:T(8,128)S(1)}, f32[312,128]{1,0:T(8,128)}, u32[]{:S(2)}) copy-start(f32[312,128]{1,0:T(8,128)} %pack.1.first.refs_0_.refs_4_) | copy-start | bytes 479236
  22.7 2.8 %copy-start.9 = (s32[8,2,128]{2,1,0:T(2,128)S(1)}, s32[8,2,128]{2,1,0:T(2,128)}, u32[]{:S(2)}) copy-start(s32[8,2,128]{2,1,0:T(2,128)} %refs_7_.7) | copy-start | bytes 24580
  25.4 10.1 %copy-start.2 = (f32[416,128]{1,0:T(8,128)}, f32[416,128]{1,0:T(8,128)S(1)}, u32[]{:S(2)}) copy-start(f32[416,128]{1,0:T(8,128)S(1)} %get-tuple-element.19.refs_2_.refs_3_.refs_6_) | copy-start | bytes 638980
  25.4 10.2 %copy-start.7 = (f32[200,128]{1,0:T(8,128)}, f32[200,128]{1,0:T(8,128)S(1)}, u32[]{:S(2)}) copy-start(f32[200,128]{1,0:T(8,128)S(1)} %get-tuple-element.20.refs_10_.refs_2_) | copy-start | bytes 307204
  25.5 3.2 %copy-start.8 = (f32[1400,128]{1,0:T(8,128)S(1)}, f32[1400,128]{1,0:T(8,128)}, u32[]{:S(2)}) copy-start(f32[1400,128]{1,0:T(8,128)} %get-tuple-element.21.refs_0_) | copy-start | bytes 2150404
  27.2 8.4 %copy-start.10 = (f32[100,2,128]{2,1,0:T(2,128)S(1)}, f32[100,2,128]{2,1,0:T(2,128)}, u32[]{:S(2)}) copy-start(f32[100,2,128]{2,1,0:T(2,128)} %param.13) | copy-start | bytes 307204
  27.2 7.0 %collective-permute-start.2 = (f32[304,128]{1,0:T(8,128)S(1)}, f32[304,128]{1,0:T(8,128)S(1)}, u32[]{:S(2)}, u32[]{:S(2)}) collective-permute-start(f32[304,128]{1,0:T(8,128)S(1)} %window1_from0.1.refs_0_.refs_10_), channel_id=1, source_target_pairs={{32,0},{64,32},{96,64},{128,96},{160,128},{192,160},{224,192},{256... | collective-permute-start | bytes 466952 | tf_op jit(solution)/shard_map/ppermute | solution.py:421
  32.4 6.7 %copy-start.5 = (f32[1400,128]{1,0:T(8,128)}, f32[1400,128]{1,0:T(8,128)S(1)}, u32[]{:S(2)}) copy-start(f32[1400,128]{1,0:T(8,128)S(1)} %window1_from1.1.refs_0_) | copy-start | bytes 2150404
  32.4 3.2 %copy-start.11 = (s32[2,128]{1,0:T(2,128)S(1)}, s32[2,128]{1,0:T(2,128)}, u32[]{:S(2)}) copy-start(s32[2,128]{1,0:T(2,128)} %refs_12_.1) | copy-start | bytes 3076
  34.2 4.8 %copy-start.6 = (f32[304,128]{1,0:T(8,128)}, f32[304,128]{1,0:T(8,128)S(1)}, u32[]{:S(2)}) copy-start(f32[304,128]{1,0:T(8,128)S(1)} %collective-permute-done.2.refs_1_.refs_3_) | copy-start | bytes 466948
  34.3 34.4 %collective-permute-start.4 = (f32[1400,128]{1,0:T(8,128)S(1)}, f32[1400,128]{1,0:T(8,128)S(1)}, u32[]{:S(2)}, u32[]{:S(2)}) collective-permute-start(f32[1400,128]{1,0:T(8,128)S(1)} %window1_from1.1.refs_0_), channel_id=1, source_target_pairs={{32,0},{64,32},{96,64},{128,96},{160,128},{192,160},{224,192},{256... | collective-permute-start | bytes 2150408 | tf_op jit(solution)/shard_map/ppermute | solution.py:421
  39.0 46.9 %all-to-all-start = ((f32[512,1,128]{2,1,0:T(1,128)}), f32[512,1,128]{2,1,0:T(1,128)S(1)}, u32[]{:S(2)}, u32[]{:S(2)}) async-start(f32[512,1,128]{2,1,0:T(1,128)} %bitcast.5), calls=%async_computation | async-start | bytes 524288 | tf_op jit(solution)/shard_map/all_to_all | solution.py:494
  68.6 0.9 %copy-start.12 = (f32[1400,128]{1,0:T(8,128)}, f32[1400,128]{1,0:T(8,128)S(1)}, u32[]{:S(2)}) copy-start(f32[1400,128]{1,0:T(8,128)S(1)} %collective-permute-done.4.refs_1_) | copy-start | bytes 2150404
